TPU v7x, 512 devices: a whole 4x4x16 slice. The times are simulated.
512 devices in a mesh: ka: 64 (over z, y_hi, core), ga: 8 (over y_lo, x).
Axes of the slice: x: 4, y: 4 (y_hi: 2, y_lo: 2; y = y_hi * 2 + y_lo), z: 16, core: 2. Of those that a mesh axis runs over, the one named last changes fastest.
Arguments:
- orbitals: bfloat16 [64, 16, 4096], P('ka', None, 'ga'), may hold values from -6 to 6
- interp_vectors: bfloat16 [4096, 4096], P(None, 'ga'), may hold values from -0.09375 to 0.09375
- screening: bfloat16 [9216, 4096], P('ka', 'ga'), may hold values from 0.049804688 to 2
- bare_coulomb: float32 [4096], P('ga'), may hold values from 0.05 to 2
- slab_kpoints: int32 [64], P('ka'), may hold values from 0 to 9215, as said below
Outputs:
- kernel: float32 [64, 7, 1, 4096], P('ka', None, None, 'ga')
Inputs may be any that keep to these rules, and one draw needn't show every extreme that they name: `slab_kpoints`: distinct grid points, each written as ix * 96 + iy with ix and iy its two grid coordinates.
All inputs are finite; a program needn't handle non-finite values.
Results may differ from a plain program's by a relative error of at most 0.0049.
Values may be sent and summed in bfloat16 or wider, within the bound.
No kernel may reach another device: no remote copies, remote signals or barrier semaphores. Data moves between devices by JAX's collectives and lax.ppermute only.
A program may use at most 64 MiB of HBM per device.

v0:
```python
import jax
import jax.numpy as jnp
from jax import lax
from jax.sharding import PartitionSpec as P

NV = 8
NC = 8
NG = 4096
NKX = 96
RSTEPS = 3


def copy_for_each(shard, axis):
    size = lax.axis_size(axis)
    return lax.all_to_all(
        jnp.broadcast_to(shard[None], (size, *shard.shape)), axis, 0, 0, tiled=True
    )


def in_order(tiles, dim):
    tiles = jnp.moveaxis(tiles, 0, dim)
    lengths = tiles.shape
    return tiles.reshape(*lengths[:dim], lengths[dim] * lengths[dim + 1], *lengths[dim + 2 :])


def gather_directly(shard, axis, dim):
    tiles = copy_for_each(shard, axis)
    return in_order(tiles, dim)


def from_behind(block, axis, distance):
    devices = range(lax.axis_size(axis))
    route = [((i - distance) % len(devices), i) for i in devices]
    return lax.ppermute(block, axis, route)


def in_blocks(shard, dim, size):
    lengths = shard.shape
    tiles = shard.reshape(*lengths[:dim], size, lengths[dim] // size, *lengths[dim + 1 :])
    return jnp.moveaxis(tiles, dim, 0)


def sent_and_summed(shard, axis, dim):
    tiles = in_blocks(shard, dim, lax.axis_size(axis))
    arrived = lax.all_to_all(tiles, axis, split_axis=0, concat_axis=0, tiled=True)
    return arrived.sum(axis=0)


def products_across(own_full, partner_full):
    product = (
        own_full.astype(jnp.float32)[:, None, :, None, :]
        * partner_full.astype(jnp.float32)[None, :, None, :, :]
    )
    return product.reshape(
        own_full.shape[0],
        partner_full.shape[0],
        own_full.shape[1] * partner_full.shape[1],
        own_full.shape[2],
    ).astype(jnp.bfloat16)


def project(points, interp_vectors):
    dims_in = points.shape
    flattened = points.reshape(-1, dims_in[-1])
    pair_waves = jnp.dot(flattened, interp_vectors, preferred_element_type=jnp.float32)
    return pair_waves.astype(jnp.bfloat16).reshape(dims_in[:-1] + (interp_vectors.shape[1],))


def exchange_of(block_full, interp_vectors):
    rows_here = block_full.shape[0]
    product = (
        block_full[:, :NV].astype(jnp.float32)[:, :, None, :]
        * block_full[:, NV:].astype(jnp.float32)[:, None, :, :]
    )
    return project(product.reshape(rows_here, NV * NC, -1).astype(jnp.bfloat16), interp_vectors)


def momentum_index(first_point, second_point):
    row_step = (first_point // NKX - second_point // NKX) % NKX
    col_step = (first_point % NKX - second_point % NKX) % NKX
    return row_step * NKX + col_step


def pair_block(own_full, partner_full, weighted_x, partner_ex, screen_rows, interp_vectors):
    rows_here = own_full.shape[0]
    cond_pairs = products_across(own_full[:, NV:], partner_full[:, NV:])
    vale_pairs = products_across(own_full[:, :NV], partner_full[:, :NV])
    pair_waves = project(jnp.concatenate([cond_pairs, vale_pairs], axis=2), interp_vectors)
    weighted = (
        pair_waves[:, :, : NC * NC].astype(jnp.float32) * screen_rows[:, :, None, :]
    ).astype(jnp.bfloat16)
    direct = jnp.einsum(
        "klxg,klyg->klxy", weighted, pair_waves[:, :, NC * NC :], preferred_element_type=jnp.float32
    )
    direct = (
        direct.reshape(rows_here, rows_here, NC, NC, NV, NV)
        .transpose(0, 1, 4, 2, 5, 3)
        .reshape(rows_here, rows_here, -1)
    )
    exch_term = jnp.einsum(
        "kxg,lyg->klxy", weighted_x, partner_ex, preferred_element_type=jnp.float32
    )
    return 2.0 * exch_term.reshape(rows_here, rows_here, -1) - direct


def per_device(orbitals, interp_vectors, screening, bare_coulomb, slab_kpoints):
    cycle_size = lax.axis_size("ka")
    own_full = gather_directly(orbitals, "ga", 2)
    own_exchange = exchange_of(own_full, interp_vectors)
    weighted_x = (own_exchange.astype(jnp.float32) * bare_coulomb).astype(jnp.bfloat16)
    offsets = list(range(-RSTEPS, RSTEPS + 1))
    momenta = []
    for offset in offsets:
        if offset == 0:
            partner = slab_kpoints
        else:
            partner = from_behind(slab_kpoints, "ka", offset)
        momenta.append(momentum_index(slab_kpoints[:, None], partner[None, :]))
    wanted = jnp.stack(momenta).reshape(-1)
    rows_here = slab_kpoints.shape[0]
    table_rows = screening.shape[0]
    owners = wanted // table_rows
    holders = jnp.arange(cycle_size, dtype=jnp.int32)[:, None]
    queries = jnp.where(owners[None, :] == holders, (wanted % table_rows)[None, :], -1)
    received = lax.all_to_all(queries, "ka", split_axis=0, concat_axis=0, tiled=True)
    picker = (
        received.reshape(-1)[:, None] == jnp.arange(table_rows, dtype=jnp.int32)[None, :]
    ).astype(jnp.bfloat16)
    replies = jnp.dot(picker, screening, preferred_element_type=jnp.float32).astype(jnp.bfloat16)
    replies = replies.reshape(cycle_size, wanted.shape[0], -1)
    returned = lax.all_to_all(replies, "ka", split_axis=0, concat_axis=0, tiled=True)
    fetched = jnp.sum(returned.astype(jnp.float32), axis=0)
    screen_rows = fetched.reshape(len(offsets), rows_here, rows_here, -1)
    partials = {
        0: pair_block(
            own_full, own_full, weighted_x, own_exchange, screen_rows[RSTEPS], interp_vectors
        )
    }
    forward_block = (own_full, own_exchange)
    backward_block = (own_full, own_exchange)
    for travel in range(1, RSTEPS + 1):
        forward_block = from_behind((forward_block[0], forward_block[1]), "ka", 1)
        backward_block = from_behind((backward_block[0], backward_block[1]), "ka", -1)
        partials[travel] = pair_block(
            own_full,
            forward_block[0],
            weighted_x,
            forward_block[1],
            screen_rows[RSTEPS + travel],
            interp_vectors,
        )
        partials[-travel] = pair_block(
            own_full,
            backward_block[0],
            weighted_x,
            backward_block[1],
            screen_rows[RSTEPS - travel],
            interp_vectors,
        )
    partial_terms = jnp.stack([partials[offset] for offset in offsets], axis=1)
    summed = sent_and_summed(partial_terms, "ga", 3)
    return summed * NG ** (-0.5)


def solution(mesh):
    in_specs = (P("ka", None, "ga"), P(None, "ga"), P("ka", "ga"), P("ga"), P("ka"))
    out_specs = P("ka", None, None, "ga")
    return jax.shard_map(
        per_device, mesh=mesh, in_specs=in_specs, out_specs=out_specs, check_vma=False
    )
```

profile of v0, /device:TPU:113, one launch (start us, length us, event | category | flops | bytes accessed | tf_op | source)
XLA Modules:
  0.0 183.4 jit_solution(484038648080361033)
XLA Ops:
  0.0 2.6 %collective-permute-start.6 = (s32[1]{0:T(128)}, s32[1]{0:T(128)}, u32[]{:S(2)}, u32[]{:S(2)}) collective-permute-start(s32[1]{0:T(128)} %param.9), channel_id=1, source_target_pairs={{24,0},{32,8},{40,16},{48,24},{56,32},{64,40},{72,48},{80,56},{88,... | collective-permute-start | bytes 20 | tf_op jit(solution)/shard_map/ppermute | solution.py:34
  2.7 4.4 %collective-permute-start.7 = (s32[1]{0:T(128)}, s32[1]{0:T(128)}, u32[]{:S(2)}, u32[]{:S(2)}) collective-permute-start(s32[1]{0:T(128)} %param.9), channel_id=1, source_target_pairs={{16,0},{24,8},{32,16},{40,24},{48,32},{56,40},{64,48},{72,56},{80,... | collective-permute-start | bytes 20 | tf_op jit(solution)/shard_map/ppermute | solution.py:34
  7.0 1.9 %collective-permute-start.8 = (s32[1]{0:T(128)}, s32[1]{0:T(128)}, u32[]{:S(2)}, u32[]{:S(2)}) collective-permute-start(s32[1]{0:T(128)} %param.9), channel_id=1, source_target_pairs={{8,0},{16,8},{24,16},{32,24},{40,32},{48,40},{56,48},{64,56},{72,6... | collective-permute-start | bytes 20 | tf_op jit(solution)/shard_map/ppermute | solution.py:34
  9.0 7.3 %collective-permute-start.9 = (s32[1]{0:T(128)}, s32[1]{0:T(128)}, u32[]{:S(2)}, u32[]{:S(2)}) collective-permute-start(s32[1]{0:T(128)} %param.9), channel_id=1, source_target_pairs={{504,0},{0,8},{8,16},{16,24},{24,32},{32,40},{40,48},{48,56},{56,6... | collective-permute-start | bytes 20 | tf_op jit(solution)/shard_map/ppermute | solution.py:34
  16.2 2.4 %collective-permute-start.10 = (s32[1]{0:T(128)}, s32[1]{0:T(128)}, u32[]{:S(2)}, u32[]{:S(2)}) collective-permute-start(s32[1]{0:T(128)} %param.9), channel_id=1, source_target_pairs={{496,0},{504,8},{0,16},{8,24},{16,32},{24,40},{32,48},{40,56},{48,... | collective-permute-start | bytes 20 | tf_op jit(solution)/shard_map/ppermute | solution.py:34
  19.4 3.3 %collective-permute-start.11 = (s32[1]{0:T(128)}, s32[1]{0:T(128)}, u32[]{:S(2)}, u32[]{:S(2)}) collective-permute-start(s32[1]{0:T(128)} %param.9), channel_id=1, source_target_pairs={{488,0},{496,8},{504,16},{0,24},{8,32},{16,40},{24,48},{32,56},{40... | collective-permute-start | bytes 20 | tf_op jit(solution)/shard_map/ppermute | solution.py:34
  34.9 28.0 %all_to_all.21 = s32[64,1,7]{2,1,0:T(1,128)S(1)} all-to-all(s32[64,1,7]{2,1,0:T(1,128)S(1)} %compare_select_fusion), channel_id=1, replica_groups=mesh['ka'=64,'ga'=8] {'ka'}, dimensions={0} | all-to-all | bytes 3584 | tf_op jit(solution)/shard_map/all_to_all | solution.py:125
  62.9 1.4 broadcast_in_dim.13
  64.3 4.7 %all-to-all-start = ((bf16[8,1,16,512]{3,2,1,0:T(8,128)(2,1)}), bf16[8,1,16,512]{3,2,1,0:T(8,128)(2,1)S(1)}, u32[]{:S(2)}, u32[]{:S(2)}) async-start(bf16[8,1,16,512]{3,2,1,0:T(8,128)(2,1)} %broadcast_in_dim.13), calls=%async_computation | async-start | bytes 262144 | tf_op jit(solution)/shard_map/all_to_all | solution.py:15
  69.5 0.7 reduce.4
  70.8 0.9 reshape.1113
  71.7 2.8 %all-to-all-done = bf16[8,1,16,512]{3,2,1,0:T(8,128)(2,1)S(1)} async-done(((bf16[8,1,16,512]{3,2,1,0:T(8,128)(2,1)}), bf16[8,1,16,512]{3,2,1,0:T(8,128)(2,1)S(1)}, u32[]{:S(2)}, u32[]{:S(2)}) %all-to-all-start) | async-done | bytes 131104 | tf_op jit(solution)/shard_map/all_to_all | solution.py:15
  74.5 10.8 %all-to-all-start.2 = ((bf16[64,7,512]{2,1,0:T(8,128)(2,1)}), bf16[64,7,512]{2,1,0:T(8,128)(2,1)S(1)}, u32[]{:S(2)}, u32[]{:S(2)}) async-start(bf16[64,7,512]{2,1,0:T(8,128)(2,1)} %reshape.1113), calls=%async_computation.2 | async-start | bytes 1048576 | tf_op jit(solution)/shard_map/all_to_all | solution.py:131
  85.4 4.6 %collective-permute-start.13 = (bf16[1,16,4096]{2,1,0:T(8,128)(2,1)S(1)}, bf16[1,16,4096]{2,1,0:T(8,128)(2,1)S(1)}, u32[]{:S(2)}, u32[]{:S(2)}) collective-permute-start(bf16[1,16,4096]{2,1,0:T(8,128)(2,1)S(1)} %bitcast.393), channel_id=1, source_target_pairs={{504,0},{0,8},{8,16},{16,24},{24,32},{32,40},{40,48},{48,56},{56,6... | collective-permute-start | bytes 393224 | tf_op jit(solution)/shard_map/ppermute | solution.py:34
  90.0 1.9 %collective-permute-start.3 = (bf16[1,16,4096]{2,1,0:T(8,128)(2,1)S(1)}, bf16[1,16,4096]{2,1,0:T(8,128)(2,1)S(1)}, u32[]{:S(2)}, u32[]{:S(2)}) collective-permute-start(bf16[1,16,4096]{2,1,0:T(8,128)(2,1)S(1)} %bitcast.394), channel_id=1, source_target_pairs={{8,0},{16,8},{24,16},{32,24},{40,32},{48,40},{56,48},{64,56},{72,6... | collective-permute-start | bytes 393224 | tf_op jit(solution)/shard_map/ppermute | solution.py:34
  92.0 3.0 %convolution_convert_fusion.8 = bf16[64,512]{1,0:T(8,128)(2,1)S(1)} fusion(bf16[4096,512]{1,0:T(8,128)(2,1)} %param.6, f32[8,4096]{1,0:T(8,128)S(1)} %get-tuple-element.32, f32[8,4096]{1,0:T(8,128)S(1)} %get-tuple-element.31), kind=kOutput, calls=%fused_computation.22 | convolution fusion | flops 268992512 | bytes 4521984 | tf_op jit(solution)/shard_map/dot_general | solution.py:65
  95.0 2.9 %collective-permute-start = (bf16[1,64,512]{2,1,0:T(8,128)(2,1)S(1)}, bf16[1,64,512]{2,1,0:T(8,128)(2,1)S(1)}, u32[]{:S(2)}, u32[]{:S(2)}) collective-permute-start(bf16[1,64,512]{2,1,0:T(8,128)(2,1)S(1)} %bitcast.391), channel_id=1, source_target_pairs={{8,0},{16,8},{24,16},{32,24},{40,32},{48,40},{56,48},{64,56},{72,6... | collective-permute-start | bytes 196616 | tf_op jit(solution)/shard_map/ppermute | solution.py:34
  97.9 6.3 %collective-permute-start.12 = (bf16[1,64,512]{2,1,0:T(8,128)(2,1)S(1)}, bf16[1,64,512]{2,1,0:T(8,128)(2,1)S(1)}, u32[]{:S(2)}, u32[]{:S(2)}) collective-permute-start(bf16[1,64,512]{2,1,0:T(8,128)(2,1)S(1)} %bitcast.392), channel_id=1, source_target_pairs={{504,0},{0,8},{8,16},{16,24},{24,32},{32,40},{40,48},{48,56},{56,6... | collective-permute-start | bytes 196616 | tf_op jit(solution)/shard_map/ppermute | solution.py:34
  104.5 8.0 %collective-permute-done = bf16[1,64,512]{2,1,0:T(8,128)(2,1)S(1)} collective-permute-done((bf16[1,64,512]{2,1,0:T(8,128)(2,1)S(1)}, bf16[1,64,512]{2,1,0:T(8,128)(2,1)S(1)}, u32[]{:S(2)}, u32[]{:S(2)}) %collective-permute-start) | collective-permute-done | bytes 65568 | tf_op jit(solution)/shard_map/ppermute | solution.py:34
  112.8 1.9 %collective-permute-start.1 = (bf16[1,64,512]{2,1,0:T(8,128)(2,1)S(1)}, bf16[1,64,512]{2,1,0:T(8,128)(2,1)S(1)}, u32[]{:S(2)}, u32[]{:S(2)}) collective-permute-start(bf16[1,64,512]{2,1,0:T(8,128)(2,1)S(1)} %collective-permute-done), channel_id=1, source_target_pairs={{8,0},{16,8},{24,16},{32,24},{40,32},{48,40},{56,48},{64,56},{72,6... | collective-permute-start | bytes 196616 | tf_op jit(solution)/shard_map/ppermute | solution.py:34
  115.1 7.3 %collective-permute-start.14 = (bf16[1,64,512]{2,1,0:T(8,128)(2,1)S(1)}, bf16[1,64,512]{2,1,0:T(8,128)(2,1)S(1)}, u32[]{:S(2)}, u32[]{:S(2)}) collective-permute-start(bf16[1,64,512]{2,1,0:T(8,128)(2,1)S(1)} %collective-permute-done.12), channel_id=1, source_target_pairs={{504,0},{0,8},{8,16},{16,24},{24,32},{32,40},{40,48},{48,56},{56,6... | collective-permute-start | bytes 196616 | tf_op jit(solution)/shard_map/ppermute | solution.py:34
  122.7 1.0 collective-permute-done.14
  124.0 7.9 %collective-permute-start.15 = (bf16[1,16,4096]{2,1,0:T(8,128)(2,1)S(1)}, bf16[1,16,4096]{2,1,0:T(8,128)(2,1)S(1)}, u32[]{:S(2)}, u32[]{:S(2)}) collective-permute-start(bf16[1,16,4096]{2,1,0:T(8,128)(2,1)S(1)} %collective-permute-done.13), channel_id=1, source_target_pairs={{504,0},{0,8},{8,16},{16,24},{24,32},{32,40},{40,48},{48,56},{56,6... | collective-permute-start | bytes 393224 | tf_op jit(solution)/shard_map/ppermute | solution.py:34
  131.9 1.9 %collective-permute-start.2 = (bf16[1,64,512]{2,1,0:T(8,128)(2,1)S(1)}, bf16[1,64,512]{2,1,0:T(8,128)(2,1)S(1)}, u32[]{:S(2)}, u32[]{:S(2)}) collective-permute-start(bf16[1,64,512]{2,1,0:T(8,128)(2,1)S(1)} %collective-permute-done.1), channel_id=1, source_target_pairs={{8,0},{16,8},{24,16},{32,24},{40,32},{48,40},{56,48},{64,56},{72,6... | collective-permute-start | bytes 196616 | tf_op jit(solution)/shard_map/ppermute | solution.py:34
  133.8 1.9 %collective-permute-start.4 = (bf16[1,16,4096]{2,1,0:T(8,128)(2,1)S(1)}, bf16[1,16,4096]{2,1,0:T(8,128)(2,1)S(1)}, u32[]{:S(2)}, u32[]{:S(2)}) collective-permute-start(bf16[1,16,4096]{2,1,0:T(8,128)(2,1)S(1)} %collective-permute-done.3), channel_id=1, source_target_pairs={{8,0},{16,8},{24,16},{32,24},{40,32},{48,40},{56,48},{64,56},{72,6... | collective-permute-start | bytes 393224 | tf_op jit(solution)/shard_map/ppermute | solution.py:34
  135.8 7.3 %collective-permute-start.16 = (bf16[1,64,512]{2,1,0:T(8,128)(2,1)S(1)}, bf16[1,64,512]{2,1,0:T(8,128)(2,1)S(1)}, u32[]{:S(2)}, u32[]{:S(2)}) collective-permute-start(bf16[1,64,512]{2,1,0:T(8,128)(2,1)S(1)} %collective-permute-done.14), channel_id=1, source_target_pairs={{504,0},{0,8},{8,16},{16,24},{24,32},{32,40},{40,48},{48,56},{56,6... | collective-permute-start | bytes 196616 | tf_op jit(solution)/shard_map/ppermute | solution.py:34
  143.4 1.0 collective-permute-done.16
  144.7 7.9 %collective-permute-start.17 = (bf16[1,16,4096]{2,1,0:T(8,128)(2,1)S(1)}, bf16[1,16,4096]{2,1,0:T(8,128)(2,1)S(1)}, u32[]{:S(2)}, u32[]{:S(2)}) collective-permute-start(bf16[1,16,4096]{2,1,0:T(8,128)(2,1)S(1)} %collective-permute-done.15), channel_id=1, source_target_pairs={{504,0},{0,8},{8,16},{16,24},{24,32},{32,40},{40,48},{48,56},{56,6... | collective-permute-start | bytes 393224 | tf_op jit(solution)/shard_map/ppermute | solution.py:34
  152.6 2.1 %collective-permute-start.5 = (bf16[1,16,4096]{2,1,0:T(8,128)(2,1)S(1)}, bf16[1,16,4096]{2,1,0:T(8,128)(2,1)S(1)}, u32[]{:S(2)}, u32[]{:S(2)}) collective-permute-start(bf16[1,16,4096]{2,1,0:T(8,128)(2,1)S(1)} %collective-permute-done.4), channel_id=1, source_target_pairs={{8,0},{16,8},{24,16},{32,24},{40,32},{48,40},{56,48},{64,56},{72,6... | collective-permute-start | bytes 393224 | tf_op jit(solution)/shard_map/ppermute | solution.py:34
  154.8 7.7 %collective-permute-done.5 = bf16[1,16,4096]{2,1,0:T(8,128)(2,1)S(1)} collective-permute-done((bf16[1,16,4096]{2,1,0:T(8,128)(2,1)S(1)}, bf16[1,16,4096]{2,1,0:T(8,128)(2,1)S(1)}, u32[]{:S(2)}, u32[]{:S(2)}) %collective-permute-start.5) | collective-permute-done | bytes 131104 | tf_op jit(solution)/shard_map/ppermute | solution.py:34
  162.5 1.7 fusion.42
  174.4 8.2 %all_to_all.22 = f32[8,1,7,1,512]{4,3,2,1,0:T(1,128)S(1)} all-to-all(f32[8,1,7,1,512]{4,3,2,1,0:T(1,128)S(1)} %copy.50), channel_id=1, replica_groups=mesh['ka'=64,'ga'=8] {'ga'}, dimensions={0} | all-to-all | bytes 229376 | tf_op jit(solution)/shard_map/all_to_all | solution.py:45
  (97 shorter events, 14.2 us)
Async XLA Ops:
  0.0 70.4 %copy-start = (bf16[144,512]{1,0:T(8,128)(2,1)S(1)}, bf16[144,512]{1,0:T(8,128)(2,1)}, u32[]{:S(2)}) copy-start(bf16[144,512]{1,0:T(8,128)(2,1)} %param.7) | copy-start | bytes 442372
  0.0 19.3 %collective-permute-start.6 = (s32[1]{0:T(128)}, s32[1]{0:T(128)}, u32[]{:S(2)}, u32[]{:S(2)}) collective-permute-start(s32[1]{0:T(128)} %param.9), channel_id=1, source_target_pairs={{24,0},{32,8},{40,16},{48,24},{56,32},{64,40},{72,48},{80,56},{88,... | collective-permute-start | bytes 20 | tf_op jit(solution)/shard_map/ppermute | solution.py:34
  2.7 21.8 %collective-permute-start.7 = (s32[1]{0:T(128)}, s32[1]{0:T(128)}, u32[]{:S(2)}, u32[]{:S(2)}) collective-permute-start(s32[1]{0:T(128)} %param.9), channel_id=1, source_target_pairs={{16,0},{24,8},{32,16},{40,24},{48,32},{56,40},{64,48},{72,56},{80,... | collective-permute-start | bytes 20 | tf_op jit(solution)/shard_map/ppermute | solution.py:34
  7.0 19.5 %collective-permute-start.8 = (s32[1]{0:T(128)}, s32[1]{0:T(128)}, u32[]{:S(2)}, u32[]{:S(2)}) collective-permute-start(s32[1]{0:T(128)} %param.9), channel_id=1, source_target_pairs={{8,0},{16,8},{24,16},{32,24},{40,32},{48,40},{56,48},{64,56},{72,6... | collective-permute-start | bytes 20 | tf_op jit(solution)/shard_map/ppermute | solution.py:34
  9.0 19.7 %collective-permute-start.9 = (s32[1]{0:T(128)}, s32[1]{0:T(128)}, u32[]{:S(2)}, u32[]{:S(2)}) collective-permute-start(s32[1]{0:T(128)} %param.9), channel_id=1, source_target_pairs={{504,0},{0,8},{8,16},{16,24},{24,32},{32,40},{40,48},{48,56},{56,6... | collective-permute-start | bytes 20 | tf_op jit(solution)/shard_map/ppermute | solution.py:34
  16.2 14.4 %collective-permute-start.10 = (s32[1]{0:T(128)}, s32[1]{0:T(128)}, u32[]{:S(2)}, u32[]{:S(2)}) collective-permute-start(s32[1]{0:T(128)} %param.9), channel_id=1, source_target_pairs={{496,0},{504,8},{0,16},{8,24},{16,32},{24,40},{32,48},{40,56},{48,... | collective-permute-start | bytes 20 | tf_op jit(solution)/shard_map/ppermute | solution.py:34
  19.4 13.1 %collective-permute-start.11 = (s32[1]{0:T(128)}, s32[1]{0:T(128)}, u32[]{:S(2)}, u32[]{:S(2)}) collective-permute-start(s32[1]{0:T(128)} %param.9), channel_id=1, source_target_pairs={{488,0},{496,8},{504,16},{0,24},{8,32},{16,40},{24,48},{32,56},{40... | collective-permute-start | bytes 20 | tf_op jit(solution)/shard_map/ppermute | solution.py:34
  34.8 69.3 %copy-start.2 = (f32[512]{0:T(512)S(1)}, f32[512]{0:T(512)}, u32[]{:S(2)}) copy-start(f32[512]{0:T(512)} %param.8) | copy-start | bytes 6148
  64.3 10.3 %all-to-all-start = ((bf16[8,1,16,512]{3,2,1,0:T(8,128)(2,1)}), bf16[8,1,16,512]{3,2,1,0:T(8,128)(2,1)S(1)}, u32[]{:S(2)}, u32[]{:S(2)}) async-start(bf16[8,1,16,512]{3,2,1,0:T(8,128)(2,1)} %broadcast_in_dim.13), calls=%async_computation | async-start | bytes 262144 | tf_op jit(solution)/shard_map/all_to_all | solution.py:15
  74.5 95.3 %all-to-all-start.2 = ((bf16[64,7,512]{2,1,0:T(8,128)(2,1)}), bf16[64,7,512]{2,1,0:T(8,128)(2,1)S(1)}, u32[]{:S(2)}, u32[]{:S(2)}) async-start(bf16[64,7,512]{2,1,0:T(8,128)(2,1)} %reshape.1113), calls=%async_computation.2 | async-start | bytes 1048576 | tf_op jit(solution)/shard_map/all_to_all | solution.py:131
  85.4 38.6 %collective-permute-start.13 = (bf16[1,16,4096]{2,1,0:T(8,128)(2,1)S(1)}, bf16[1,16,4096]{2,1,0:T(8,128)(2,1)S(1)}, u32[]{:S(2)}, u32[]{:S(2)}) collective-permute-start(bf16[1,16,4096]{2,1,0:T(8,128)(2,1)S(1)} %bitcast.393), channel_id=1, source_target_pairs={{504,0},{0,8},{8,16},{16,24},{24,32},{32,40},{40,48},{48,56},{56,6... | collective-permute-start | bytes 393224 | tf_op jit(solution)/shard_map/ppermute | solution.py:34
  90.0 43.8 %collective-permute-start.3 = (bf16[1,16,4096]{2,1,0:T(8,128)(2,1)S(1)}, bf16[1,16,4096]{2,1,0:T(8,128)(2,1)S(1)}, u32[]{:S(2)}, u32[]{:S(2)}) collective-permute-start(bf16[1,16,4096]{2,1,0:T(8,128)(2,1)S(1)} %bitcast.394), channel_id=1, source_target_pairs={{8,0},{16,8},{24,16},{32,24},{40,32},{48,40},{56,48},{64,56},{72,6... | collective-permute-start | bytes 393224 | tf_op jit(solution)/shard_map/ppermute | solution.py:34
  95.0 17.5 %collective-permute-start = (bf16[1,64,512]{2,1,0:T(8,128)(2,1)S(1)}, bf16[1,64,512]{2,1,0:T(8,128)(2,1)S(1)}, u32[]{:S(2)}, u32[]{:S(2)}) collective-permute-start(bf16[1,64,512]{2,1,0:T(8,128)(2,1)S(1)} %bitcast.391), channel_id=1, source_target_pairs={{8,0},{16,8},{24,16},{32,24},{40,32},{48,40},{56,48},{64,56},{72,6... | collective-permute-start | bytes 196616 | tf_op jit(solution)/shard_map/ppermute | solution.py:34
  97.9 16.9 %collective-permute-start.12 = (bf16[1,64,512]{2,1,0:T(8,128)(2,1)S(1)}, bf16[1,64,512]{2,1,0:T(8,128)(2,1)S(1)}, u32[]{:S(2)}, u32[]{:S(2)}) collective-permute-start(bf16[1,64,512]{2,1,0:T(8,128)(2,1)S(1)} %bitcast.392), channel_id=1, source_target_pairs={{504,0},{0,8},{8,16},{16,24},{24,32},{32,40},{40,48},{48,56},{56,6... | collective-permute-start | bytes 196616 | tf_op jit(solution)/shard_map/ppermute | solution.py:34
  112.8 9.5 %collective-permute-start.1 = (bf16[1,64,512]{2,1,0:T(8,128)(2,1)S(1)}, bf16[1,64,512]{2,1,0:T(8,128)(2,1)S(1)}, u32[]{:S(2)}, u32[]{:S(2)}) collective-permute-start(bf16[1,64,512]{2,1,0:T(8,128)(2,1)S(1)} %collective-permute-done), channel_id=1, source_target_pairs={{8,0},{16,8},{24,16},{32,24},{40,32},{48,40},{56,48},{64,56},{72,6... | collective-permute-start | bytes 196616 | tf_op jit(solution)/shard_map/ppermute | solution.py:34
  115.1 8.6 %collective-permute-start.14 = (bf16[1,64,512]{2,1,0:T(8,128)(2,1)S(1)}, bf16[1,64,512]{2,1,0:T(8,128)(2,1)S(1)}, u32[]{:S(2)}, u32[]{:S(2)}) collective-permute-start(bf16[1,64,512]{2,1,0:T(8,128)(2,1)S(1)} %collective-permute-done.12), channel_id=1, source_target_pairs={{504,0},{0,8},{8,16},{16,24},{24,32},{32,40},{40,48},{48,56},{56,6... | collective-permute-start | bytes 196616 | tf_op jit(solution)/shard_map/ppermute | solution.py:34
  124.0 20.7 %collective-permute-start.15 = (bf16[1,16,4096]{2,1,0:T(8,128)(2,1)S(1)}, bf16[1,16,4096]{2,1,0:T(8,128)(2,1)S(1)}, u32[]{:S(2)}, u32[]{:S(2)}) collective-permute-start(bf16[1,16,4096]{2,1,0:T(8,128)(2,1)S(1)} %collective-permute-done.13), channel_id=1, source_target_pairs={{504,0},{0,8},{8,16},{16,24},{24,32},{32,40},{40,48},{48,56},{56,6... | collective-permute-start | bytes 393224 | tf_op jit(solution)/shard_map/ppermute | solution.py:34
  131.9 11.2 %collective-permute-start.2 = (bf16[1,64,512]{2,1,0:T(8,128)(2,1)S(1)}, bf16[1,64,512]{2,1,0:T(8,128)(2,1)S(1)}, u32[]{:S(2)}, u32[]{:S(2)}) collective-permute-start(bf16[1,64,512]{2,1,0:T(8,128)(2,1)S(1)} %collective-permute-done.1), channel_id=1, source_target_pairs={{8,0},{16,8},{24,16},{32,24},{40,32},{48,40},{56,48},{64,56},{72,6... | collective-permute-start | bytes 196616 | tf_op jit(solution)/shard_map/ppermute | solution.py:34
  133.8 18.8 %collective-permute-start.4 = (bf16[1,16,4096]{2,1,0:T(8,128)(2,1)S(1)}, bf16[1,16,4096]{2,1,0:T(8,128)(2,1)S(1)}, u32[]{:S(2)}, u32[]{:S(2)}) collective-permute-start(bf16[1,16,4096]{2,1,0:T(8,128)(2,1)S(1)} %collective-permute-done.3), channel_id=1, source_target_pairs={{8,0},{16,8},{24,16},{32,24},{40,32},{48,40},{56,48},{64,56},{72,6... | collective-permute-start | bytes 393224 | tf_op jit(solution)/shard_map/ppermute | solution.py:34
  135.8 8.6 %collective-permute-start.16 = (bf16[1,64,512]{2,1,0:T(8,128)(2,1)S(1)}, bf16[1,64,512]{2,1,0:T(8,128)(2,1)S(1)}, u32[]{:S(2)}, u32[]{:S(2)}) collective-permute-start(bf16[1,64,512]{2,1,0:T(8,128)(2,1)S(1)} %collective-permute-done.14), channel_id=1, source_target_pairs={{504,0},{0,8},{8,16},{16,24},{24,32},{32,40},{40,48},{48,56},{56,6... | collective-permute-start | bytes 196616 | tf_op jit(solution)/shard_map/ppermute | solution.py:34
  144.7 10.1 %collective-permute-start.17 = (bf16[1,16,4096]{2,1,0:T(8,128)(2,1)S(1)}, bf16[1,16,4096]{2,1,0:T(8,128)(2,1)S(1)}, u32[]{:S(2)}, u32[]{:S(2)}) collective-permute-start(bf16[1,16,4096]{2,1,0:T(8,128)(2,1)S(1)} %collective-permute-done.15), channel_id=1, source_target_pairs={{504,0},{0,8},{8,16},{16,24},{24,32},{32,40},{40,48},{48,56},{56,6... | collective-permute-start | bytes 393224 | tf_op jit(solution)/shard_map/ppermute | solution.py:34
  152.6 9.9 %collective-permute-start.5 = (bf16[1,16,4096]{2,1,0:T(8,128)(2,1)S(1)}, bf16[1,16,4096]{2,1,0:T(8,128)(2,1)S(1)}, u32[]{:S(2)}, u32[]{:S(2)}) collective-permute-start(bf16[1,16,4096]{2,1,0:T(8,128)(2,1)S(1)} %collective-permute-done.4), channel_id=1, source_target_pairs={{8,0},{16,8},{24,16},{32,24},{40,32},{48,40},{56,48},{64,56},{72,6... | collective-permute-start | bytes 393224 | tf_op jit(solution)/shard_map/ppermute | solution.py:34
  162.5 2.2 %copy-start.1 = (bf16[4096,512]{1,0:T(8,128)(2,1)S(1)}, bf16[4096,512]{1,0:T(8,128)(2,1)}, u32[]{:S(2)}) copy-start(bf16[4096,512]{1,0:T(8,128)(2,1)} %param.6) | copy-start | bytes 12582916
where the time goes:
time: 185 us; the launch traced here: 183 us
  starting transfers between devices  91.3 us (49%)
  blocking collectives  36.2 us (20%)
  waiting for transfers between devices  20.6 us (11%)
  between operations  13.3 us (7%)
  matrix products  11.6 us (6%)
  local copies, waits for them, and re-layouts  7.47 us (4%)
  other arithmetic  2.87 us (2%)
    ppermute x18, starting transfers between devices, from_behind(): return lax.ppermute(block, axis, route)  75.8 us
    all_to_all x1, blocking collectives, per_device(): lax.all_to_all(queries, 'ka', split_axis=0, concat_axis=0, tiled=True)  28 us
    ppermute x18, waiting for transfers between devices, from_behind(): return lax.ppermute(block, axis, route)  17.7 us
    all_to_all x1, starting transfers between devices, per_device(): lax.all_to_all(replies, 'ka', split_axis=0, concat_axis=0, tiled=True)  10.8 us
    all_to_all x1, blocking collectives, sent_and_summed(): lax.all_to_all(tiles, axis, split_axis=0, concat_axis=0, tiled=True)  8.2 us
    dot_general x8, matrix products, project(): jnp.dot(flattened, interp_vectors, preferred_element_type=jnp.float32)  8.06 us
    all_to_all x1, starting transfers between devices, copy_for_each(): lax.all_to_all(jnp.broadcast_to(shard[None], (size, *shard.shape)), axis,...  4.74 us
  transfers between devices with their start and end apart: 20, of which 5 were waited for; matrix products, arithmetic and copies ran while one was open for 8% of the time, Pallas kernels for 0%

commit v1 on v0

v1 whole, which is shorter than its diff:
```python
import jax
import jax.numpy as jnp
from jax import lax
from jax.sharding import PartitionSpec as P

NV = 8
NC = 8
NG = 4096
NKX = 96
RSTEPS = 3
NEAR = 8


def near_groups(size, shift):
    return [
        [(start + shift + j) % size for j in range(NEAR)] for start in range(0, size, NEAR)
    ]


def far_groups(size):
    return [[j + start for start in range(0, size, NEAR)] for j in range(NEAR)]


def copy_for_each(shard, axis, size, groups=None):
    return lax.all_to_all(
        jnp.broadcast_to(shard[None], (size, *shard.shape)),
        axis,
        0,
        0,
        tiled=True,
        axis_index_groups=groups,
    )


def momentum_index(first_point, second_point):
    row_step = first_point // NKX - second_point // NKX
    col_step = first_point % NKX - second_point % NKX
    row_step = jnp.where(row_step < 0, row_step + NKX, row_step)
    col_step = jnp.where(col_step < 0, col_step + NKX, col_step)
    return row_step * NKX + col_step


def window(orbitals, size):
    place = lax.axis_index("ka") % NEAR
    block = copy_for_each(orbitals, "ka", NEAR, near_groups(size, 0))
    shifted = copy_for_each(orbitals, "ka", NEAR, near_groups(size, NEAR // 2))
    half = NEAR // 2
    low = jnp.concatenate([shifted[:half], block])
    high = jnp.concatenate([block, shifted[half:]])
    twelve = jnp.where(place < half, low, high)
    start = jnp.where(place < half, place + half - RSTEPS, place - RSTEPS)
    return lax.dynamic_slice_in_dim(twelve, start, 2 * RSTEPS + 1, 0)


def asked_rows(points, screening, size):
    offsets = range(-RSTEPS, RSTEPS + 1)
    partners = jnp.stack([jnp.roll(points, d) for d in offsets], axis=0)
    wanted = momentum_index(points[None, :], partners)
    table_rows = screening.shape[0]
    local = wanted - lax.axis_index("ka") * table_rows
    blocks = size // NEAR
    local = local.reshape(-1, blocks, NEAR).transpose(2, 1, 0)
    picker = (local[..., None] == jnp.arange(table_rows, dtype=jnp.int32)).astype(jnp.bfloat16)
    replies = jnp.dot(
        picker.reshape(-1, table_rows), screening, preferred_element_type=jnp.float32
    ).astype(jnp.bfloat16)
    replies = replies.reshape(NEAR, blocks * local.shape[-1], -1)
    near = lax.all_to_all(
        replies, "ka", 0, 0, tiled=True, axis_index_groups=near_groups(size, 0)
    )
    near = near.astype(jnp.float32).sum(axis=0).astype(jnp.bfloat16)
    near = near.reshape(blocks, local.shape[-1], -1)
    far = lax.all_to_all(near, "ka", 0, 0, tiled=True, axis_index_groups=far_groups(size))
    return far.astype(jnp.float32).sum(axis=0)


def band_products(first, second):
    product = first.astype(jnp.float32)[:, :, None, :] * second.astype(jnp.float32)[:, None, :, :]
    return product.reshape(product.shape[0], -1, product.shape[-1]).astype(jnp.bfloat16)


def per_device(orbitals, interp_vectors, screening, bare_coulomb, slab_kpoints):
    size = lax.axis_size("ka")
    parts = lax.axis_size("ga")
    points = copy_for_each(slab_kpoints, "ka", size).reshape(-1)
    near = window(orbitals[0], size)
    count = near.shape[0]
    full = copy_for_each(near, "ga", parts)
    full = jnp.moveaxis(full, 0, 2).reshape(count, NV + NC, -1)
    own = jnp.broadcast_to(full[RSTEPS][None], full.shape)
    screen_rows = asked_rows(points, screening, size)
    rows = jnp.concatenate(
        [
            band_products(own[:, NV:], full[:, NV:]),
            band_products(own[:, :NV], full[:, :NV]),
            band_products(full[:, :NV], full[:, NV:]),
        ],
        axis=1,
    )
    total = rows.shape[1]
    waves = jnp.dot(
        rows.reshape(count * total, -1), interp_vectors, preferred_element_type=jnp.float32
    ).astype(jnp.bfloat16).reshape(count, total, -1)
    waves = waves[::-1]
    exchange = waves[:, NC * NC + NV * NV :]
    weighted_x = (exchange[RSTEPS].astype(jnp.float32) * bare_coulomb).astype(jnp.bfloat16)
    exch = jnp.einsum("xg,dyg->dxy", weighted_x, exchange, preferred_element_type=jnp.float32)
    weighted = (waves[:, : NC * NC].astype(jnp.float32) * screen_rows[:, None, :]).astype(
        jnp.bfloat16
    )
    direct = jnp.einsum(
        "dxg,dyg->dxy",
        weighted,
        waves[:, NC * NC : NC * NC + NV * NV],
        preferred_element_type=jnp.float32,
    )
    direct = direct.reshape(count, NC, NC, NV, NV).transpose(3, 0, 1, 4, 2)
    exch = exch.reshape(count, NV, NC, NV * NC).transpose(1, 0, 2, 3)
    partial = 2.0 * exch.reshape(NV, count, -1) - direct.reshape(NV, count, -1)
    arrived = lax.all_to_all(partial, "ga", 0, 0, tiled=True)
    return (arrived.sum(axis=0) * NG ** (-0.5))[None, :, None, :]


def solution(mesh):
    in_specs = (P("ka", None, "ga"), P(None, "ga"), P("ka", "ga"), P("ga"), P("ka"))
    out_specs = P("ka", None, None, "ga")
    return jax.shard_map(
        per_device, mesh=mesh, in_specs=in_specs, out_specs=out_specs, check_vma=False
    )
```

time: 185 us -> 141 us (0.76)
  the two profiles are of different devices: /device:TPU:113 before, /device:TPU:16 now
where the time goes in v1:
time: 141 us; the launch traced here: 140 us
  starting transfers between devices  44 us (31%)
  waiting for transfers between devices  41.5 us (29%)
  local copies, waits for them, and re-layouts  18.6 us (13%)
  other arithmetic  17.6 us (12%)
  blocking collectives  9.72 us (7%)
  matrix products  7.71 us (5%)
    all_to_all x4, starting transfers between devices, copy_for_each(): lax.all_to_all(jnp.broadcast_to(shard[None], (size, *shard.shape)), axis,...  35.4 us
    all_to_all x4, waiting for transfers between devices, copy_for_each(): lax.all_to_all(jnp.broadcast_to(shard[None], (size, *shard.shape)), axis,...  27.6 us
    all_to_all x1, waiting for transfers between devices, asked_rows(): lax.all_to_all(near, 'ka', 0, 0, tiled=True, axis_index_groups=far_groups...  13.8 us
    all_to_all x1, blocking collectives, per_device(): arrived = lax.all_to_all(partial, 'ga', 0, 0, tiled=True)  9.72 us
    concatenate x1, other arithmetic, per_device(): jnp.concatenate([band_products(own[:, NV:], full[:, NV:]), band_products(...  8.66 us
    slice x6, local copies, waits for them, and re-layouts, asked_rows(): partners = jnp.stack([jnp.roll(points, d) for d in offsets], axis=0)  7.78 us
    dot_general x1, matrix products, per_device(): jnp.dot(rows.reshape(count * total, -1), interp_vectors, preferred_elemen...  6.07 us
    all_to_all x1, starting transfers between devices, asked_rows(): lax.all_to_all(replies, 'ka', 0, 0, tiled=True, axis_index_groups=near_gr...  5.27 us
  transfers between devices with their start and end apart: 6, of which 4 were waited for; matrix products, arithmetic and copies ran while one was open for 25% of the time, Pallas kernels for 0%

profile of v1, /device:TPU:16, one launch (start us, length us, event | category | flops | bytes accessed | tf_op | source)
XLA Modules:
  0.0 140.2 jit_solution(7301213957178192718)
XLA Ops:
  0.7 0.6 broadcast_in_dim.14
  1.3 18.6 %all-to-all-start.3 = ((s32[64,1,1]{2,1,0:T(1,128)}), s32[64,1,1]{2,1,0:T(1,128)S(1)}, u32[]{:S(2)}, u32[]{:S(2)}) async-start(s32[64,1,1]{2,1,0:T(1,128)} %broadcast_in_dim.14), calls=%async_computation.3 | async-start | bytes 65536 | tf_op jit(solution)/shard_map/all_to_all | solution.py:25
  20.0 12.4 %all-to-all-done.3 = s32[64,1,1]{2,1,0:T(1,128)S(1)} async-done(((s32[64,1,1]{2,1,0:T(1,128)}), s32[64,1,1]{2,1,0:T(1,128)S(1)}, u32[]{:S(2)}, u32[]{:S(2)}) %all-to-all-start.3) | async-done | bytes 288 | tf_op jit(solution)/shard_map/all_to_all | solution.py:25
  32.4 1.4 broadcast_in_dim.11
  33.8 6.9 %all-to-all-start = ((bf16[8,16,512]{2,1,0:T(8,128)(2,1)}), bf16[8,16,512]{2,1,0:T(8,128)(2,1)S(1)}, u32[]{:S(2)}, u32[]{:S(2)}) async-start(bf16[8,16,512]{2,1,0:T(8,128)(2,1)} %broadcast_in_dim.11), calls=%async_computation | async-start | bytes 262144 | tf_op jit(solution)/shard_map/all_to_all | solution.py:25
  40.7 2.3 %slice_reduce_fusion.4 = (s32[61]{0:T(128)S(1)}, s32[61]{0:T(128)S(1)}) fusion(s32[64,1,1]{2,1,0:T(1,128)S(1)} %all-to-all-done.3), kind=kLoop, calls=%fused_computation.45 | loop fusion | bytes 976 | tf_op jit(solution)/shard_map/jit(_roll_static)/slice | solution.py:57
  43.1 2.3 %slice_reduce_fusion.2 = (s32[62]{0:T(128)S(1)}, s32[62]{0:T(128)S(1)}) fusion(s32[64,1,1]{2,1,0:T(1,128)S(1)} %all-to-all-done.3), kind=kLoop, calls=%fused_computation.43 | loop fusion | bytes 992 | tf_op jit(solution)/shard_map/jit(_roll_static)/slice | solution.py:57
  45.7 0.5 fusion.25
  46.2 2.3 %slice_reduce_fusion = (s32[63]{0:T(128)S(1)}, s32[63]{0:T(128)S(1)}) fusion(s32[64,1,1]{2,1,0:T(1,128)S(1)} %all-to-all-done.3), kind=kLoop, calls=%fused_computation.41 | loop fusion | bytes 1008 | tf_op jit(solution)/shard_map/jit(_roll_static)/slice | solution.py:57
  48.5 1.3 pad_add_fusion.2
  49.8 3.5 %divide_reduce_fusion = (s32[64]{0:T(128)S(1)}, s32[64]{0:T(128)S(1)}, s32[64]{0:T(128)S(1)}) fusion(s32[64,1,1]{2,1,0:T(1,128)S(1)} %all-to-all-done.3), kind=kLoop, calls=%fused_computation.40 | loop fusion | flops 128 | bytes 1024 | tf_op jit(solution)/shard_map/jit(floor_divide)/div | solution.py:36
  53.9 4.8 %all-to-all-start.1 = ((bf16[8,16,512]{2,1,0:T(8,128)(2,1)}), bf16[8,16,512]{2,1,0:T(8,128)(2,1)S(1)}, u32[]{:S(2)}, u32[]{:S(2)}) async-start(bf16[8,16,512]{2,1,0:T(8,128)(2,1)} %broadcast_in_dim.11), calls=%async_computation.1 | async-start | bytes 262144 | tf_op jit(solution)/shard_map/all_to_all | solution.py:25
  58.7 1.2 compare_reduce_fusion
  60.0 2.8 %all-to-all-done.1 = bf16[8,16,512]{2,1,0:T(8,128)(2,1)S(1)} async-done(((bf16[8,16,512]{2,1,0:T(8,128)(2,1)}), bf16[8,16,512]{2,1,0:T(8,128)(2,1)S(1)}, u32[]{:S(2)}, u32[]{:S(2)}) %all-to-all-start.1) | async-done | bytes 131104 | tf_op jit(solution)/shard_map/all_to_all | solution.py:25
  62.9 1.0 broadcast_in_dim.12
  63.9 5.0 %all-to-all-start.2 = ((bf16[8,7,16,512]{3,2,1,0:T(8,128)(2,1)}), bf16[8,7,16,512]{3,2,1,0:T(8,128)(2,1)S(1)}, u32[]{:S(2)}, u32[]{:S(2)}) async-start(bf16[8,7,16,512]{3,2,1,0:T(8,128)(2,1)} %broadcast_in_dim.12), calls=%async_computation.2 | async-start | bytes 1835008 | tf_op jit(solution)/shard_map/all_to_all | solution.py:25
  69.6 1.1 convolution_convert_fusion.1
  70.7 12.4 %all-to-all-done.2 = bf16[8,7,16,512]{3,2,1,0:T(8,128)(2,1)S(1)} async-done(((bf16[8,7,16,512]{3,2,1,0:T(8,128)(2,1)}), bf16[8,7,16,512]{3,2,1,0:T(8,128)(2,1)S(1)}, u32[]{:S(2)}, u32[]{:S(2)}) %all-to-all-start.2) | async-done | bytes 917536 | tf_op jit(solution)/shard_map/all_to_all | solution.py:25
  83.2 5.3 %all-to-all-start.4 = ((bf16[8,56,512]{2,1,0:T(8,128)(2,1)}), bf16[8,56,512]{2,1,0:T(8,128)(2,1)S(1)}, u32[]{:S(2)}, u32[]{:S(2)}) async-start(bf16[8,56,512]{2,1,0:T(8,128)(2,1)} %bitcast.20), calls=%async_computation.4 | async-start | bytes 917504 | tf_op jit(solution)/shard_map/all_to_all | solution.py:68
  89.0 2.3 %fusion = (bf16[7,64,4096]{2,1,0:T(8,128)(2,1)S(1)}, bf16[7,64,4096]{2,1,0:T(8,128)(2,1)S(1)}, bf16[7,64,4096]{2,1,0:T(8,128)(2,1)S(1)}) fusion(f32[7,8,4096]{2,1,0:T(8,128)S(1)} %get-tuple-element.25, f32[64,4096]{1,0:T(8,128)S(1)} %get-tuple-element.40, f32[7,8,4096]{2,1,0:T(8,128)S(1)} %get-tuple-element.26, f32[64,4096]{1,0:T(8,128)S(1)} %get-tuple-element.39), kind=kLoop, calls=%fused_computation.3 | loop fusion | flops 11010048 | bytes 14942208 | tf_op jit(solution)/shard_map/convert_element_type | solution.py:79
  91.3 8.7 %pad_maximum_fusion = bf16[7,192,4096]{2,1,0:T(8,128)(2,1)S(1)} fusion(bf16[7,64,4096]{2,1,0:T(8,128)(2,1)S(1)} %get-tuple-element.21, bf16[7,64,4096]{2,1,0:T(8,128)(2,1)S(1)} %get-tuple-element.22, bf16[7,64,4096]{2,1,0:T(8,128)(2,1)S(1)} %get-tuple-element.20), kind=kLoop, calls=%fused_computation | loop fusion | flops 33030144 | bytes 22020096 | tf_op jit(solution)/shard_map/concatenate | solution.py:92
  100.0 6.1 %convolution_convert_fusion = bf16[1344,512]{1,0:T(8,128)(2,1)S(1)} fusion(bf16[1344,4096]{1,0:T(8,128)(2,1)S(1)} %bitcast.61, bf16[4096,512]{1,0:T(8,128)(2,1)S(1)} %copy-done.2), kind=kOutput, calls=%fused_computation.7 | convolution fusion | flops 5637832704 | bytes 16580608 | tf_op jit(solution)/shard_map/dot_general | solution.py:101
  106.3 0.6 reshape.196
  107.0 3.3 %all-to-all-start.5 = ((bf16[8,7,512]{2,1,0:T(8,128)(2,1)}), bf16[8,7,512]{2,1,0:T(8,128)(2,1)S(1)}, u32[]{:S(2)}, u32[]{:S(2)}) async-start(bf16[8,7,512]{2,1,0:T(8,128)(2,1)} %reshape.196), calls=%async_computation.5 | async-start | bytes 131072 | tf_op jit(solution)/shard_map/all_to_all | solution.py:73
  110.3 0.3 fusion.3
  110.8 13.8 %all-to-all-done.5 = bf16[8,7,512]{2,1,0:T(8,128)(2,1)S(1)} async-done(((bf16[8,7,512]{2,1,0:T(8,128)(2,1)}), bf16[8,7,512]{2,1,0:T(8,128)(2,1)S(1)}, u32[]{:S(2)}, u32[]{:S(2)}) %all-to-all-start.5) | async-done | bytes 57376 | tf_op jit(solution)/shard_map/all_to_all | solution.py:73
  124.7 0.3 fusion.4
  125.0 0.5 reshape.197
  125.5 1.7 %copy.17 = f32[7,8,8,8,8]{2,4,1,3,0:T(8,128)} copy(f32[7,8,8,8,8]{4,3,2,1,0:T(8,128)S(1)} %reshape.197) | data formatting | bytes 229376 | tf_op jit(solution)/shard_map/reshape | solution.py:117
  127.2 2.5 %reshape.198 = f32[8,7,512]{2,0,1:T(8,128)S(1)} reshape(f32[8,7,8,8,8]{4,3,2,0,1:T(8,128)} %bitcast.62) | data formatting | bytes 229376 | tf_op jit(solution)/shard_map/reshape | solution.py:119
  129.8 9.7 %all_to_all.36 = f32[8,7,512]{2,1,0:T(8,128)S(1)} all-to-all(f32[8,7,512]{2,1,0:T(8,128)S(1)} %copy.18), channel_id=1, replica_groups=mesh['ka'=64,'ga'=8] {'ga'}, dimensions={0} | all-to-all | bytes 229376 | tf_op jit(solution)/shard_map/all_to_all | solution.py:120
  139.6 0.6 mul.140
  (52 shorter events, 2.8 us)
Async XLA Ops:
  0.0 69.6 %copy-start = (bf16[144,512]{1,0:T(8,128)(2,1)S(1)}, bf16[144,512]{1,0:T(8,128)(2,1)}, u32[]{:S(2)}) copy-start(bf16[144,512]{1,0:T(8,128)(2,1)} %param.7) | copy-start | bytes 442372
  1.3 31.1 %all-to-all-start.3 = ((s32[64,1,1]{2,1,0:T(1,128)}), s32[64,1,1]{2,1,0:T(1,128)S(1)}, u32[]{:S(2)}, u32[]{:S(2)}) async-start(s32[64,1,1]{2,1,0:T(1,128)} %broadcast_in_dim.14), calls=%async_computation.3 | async-start | bytes 65536 | tf_op jit(solution)/shard_map/all_to_all | solution.py:25
  33.8 20.2 %all-to-all-start = ((bf16[8,16,512]{2,1,0:T(8,128)(2,1)}), bf16[8,16,512]{2,1,0:T(8,128)(2,1)S(1)}, u32[]{:S(2)}, u32[]{:S(2)}) async-start(bf16[8,16,512]{2,1,0:T(8,128)(2,1)} %broadcast_in_dim.11), calls=%async_computation | async-start | bytes 262144 | tf_op jit(solution)/shard_map/all_to_all | solution.py:25
  53.9 8.9 %all-to-all-start.1 = ((bf16[8,16,512]{2,1,0:T(8,128)(2,1)}), bf16[8,16,512]{2,1,0:T(8,128)(2,1)S(1)}, u32[]{:S(2)}, u32[]{:S(2)}) async-start(bf16[8,16,512]{2,1,0:T(8,128)(2,1)} %broadcast_in_dim.11), calls=%async_computation.1 | async-start | bytes 262144 | tf_op jit(solution)/shard_map/all_to_all | solution.py:25
  63.9 19.2 %all-to-all-start.2 = ((bf16[8,7,16,512]{3,2,1,0:T(8,128)(2,1)}), bf16[8,7,16,512]{3,2,1,0:T(8,128)(2,1)S(1)}, u32[]{:S(2)}, u32[]{:S(2)}) async-start(bf16[8,7,16,512]{3,2,1,0:T(8,128)(2,1)} %broadcast_in_dim.12), calls=%async_computation.2 | async-start | bytes 1835008 | tf_op jit(solution)/shard_map/all_to_all | solution.py:25
  83.2 23.1 %all-to-all-start.4 = ((bf16[8,56,512]{2,1,0:T(8,128)(2,1)}), bf16[8,56,512]{2,1,0:T(8,128)(2,1)S(1)}, u32[]{:S(2)}, u32[]{:S(2)}) async-start(bf16[8,56,512]{2,1,0:T(8,128)(2,1)} %bitcast.20), calls=%async_computation.4 | async-start | bytes 917504 | tf_op jit(solution)/shard_map/all_to_all | solution.py:68
  91.3 8.7 %copy-start.2 = (bf16[4096,512]{1,0:T(8,128)(2,1)S(1)}, bf16[4096,512]{1,0:T(8,128)(2,1)}, u32[]{:S(2)}) copy-start(bf16[4096,512]{1,0:T(8,128)(2,1)} %param.6) | copy-start | bytes 12582916
  106.1 4.3 %copy-start.1 = (f32[512]{0:T(512)S(1)}, f32[512]{0:T(512)}, u32[]{:S(2)}) copy-start(f32[512]{0:T(512)} %param.8) | copy-start | bytes 6148
  107.0 17.7 %all-to-all-start.5 = ((bf16[8,7,512]{2,1,0:T(8,128)(2,1)}), bf16[8,7,512]{2,1,0:T(8,128)(2,1)S(1)}, u32[]{:S(2)}, u32[]{:S(2)}) async-start(bf16[8,7,512]{2,1,0:T(8,128)(2,1)} %reshape.196), calls=%async_computation.5 | async-start | bytes 131072 | tf_op jit(solution)/shard_map/all_to_all | solution.py:73

commit v2 on v1

v2 whole, which is shorter than its diff:
```python
import jax
import jax.numpy as jnp
from jax import lax
from jax.experimental import pallas as pl
from jax.experimental.pallas import tpu as pltpu
from jax.sharding import PartitionSpec as P


NV = 8
NC = 8
NG = 4096
NKX = 96
RSTEPS = 3
NOFF = 2 * RSTEPS + 1
NEAR = 8
LANES = 128
BANDS = NV + NC
PAIRS = NC * NC


def near_groups(size):
    return [[start + j for j in range(NEAR)] for start in range(0, size, NEAR)]


def far_groups(size):
    return [[j + start for start in range(0, size, NEAR)] for j in range(NEAR)]


def swap(tiles, axis, groups=None):
    return lax.all_to_all(tiles, axis, 0, 0, tiled=True, axis_index_groups=groups)


VMEM = pl.BlockSpec(memory_space=pltpu.VMEM)
SMEM = pl.BlockSpec(memory_space=pltpu.SMEM)


def message_kernel(point_ref, own_ref, out_ref):
    chunk = own_ref.shape[1]
    row = point_ref[0] // NKX
    col = point_ref[0] - row * NKX
    lane = lax.broadcasted_iota(jnp.int32, (NEAR, chunk), 1)
    coords = jnp.where(lane < LANES, row, col).astype(jnp.float32).astype(jnp.bfloat16)
    for j in range(out_ref.shape[0]):
        out_ref[j, :BANDS, :] = own_ref[...]
        out_ref[j, BANDS:, :] = coords


def message_of(points, own):
    return pl.pallas_call(
        message_kernel,
        out_shape=jax.ShapeDtypeStruct((NEAR, BANDS + NEAR, own.shape[1]), own.dtype),
        in_specs=[SMEM, VMEM],
        out_specs=VMEM,
        compiler_params=pltpu.CompilerParams(vmem_limit_bytes=2 << 20),
        name="message",
    )(points, own)


def edges_kernel(place_ref, block_ref, coords_ref, edge_ref):
    rows = [block_ref[j, BANDS : BANDS + 1, : 2 * LANES] for j in range(NEAR)]
    rows = jnp.concatenate([r.astype(jnp.float32) for r in rows], axis=0)
    for b in range(coords_ref.shape[0]):
        coords_ref[b] = rows.astype(jnp.bfloat16)
    inner = lax.rem(place_ref[0], NEAR)
    first = jnp.where(inner < NEAR // 2, 0, NEAR - RSTEPS)
    for n in range(RSTEPS):
        edge_ref[n * BANDS : (n + 1) * BANDS, :] = block_ref[first + n, :BANDS, :]


def edges_of(place, block, blocks):
    return pl.pallas_call(
        edges_kernel,
        out_shape=(
            jax.ShapeDtypeStruct((blocks, NEAR, 2 * LANES), block.dtype),
            jax.ShapeDtypeStruct((RSTEPS * BANDS, block.shape[2]), block.dtype),
        ),
        in_specs=[SMEM, VMEM],
        out_specs=(VMEM, VMEM),
        compiler_params=pltpu.CompilerParams(vmem_limit_bytes=2 << 20),
        name="edges",
    )(place, block)


def edge_route(size):
    route = []
    for k in range(size):
        start, inner = k - k % NEAR, k % NEAR
        if inner < RSTEPS:
            route.append((k, (start - NEAR + NEAR - 1 - inner) % size))
        elif inner >= NEAR - RSTEPS:
            route.append((k, (start + NEAR + NEAR - 1 - inner) % size))
    return route


def window_kernel(place_ref, block_ref, edge_ref, out_ref):
    inner = lax.rem(place_ref[0], NEAR)
    copies = out_ref.shape[0]

    def put(n, value):
        for g in range(copies):
            out_ref[g, n * BANDS : (n + 1) * BANDS, :] = value

    for n in range(NOFF):
        at = inner + (n - RSTEPS)
        inside = jnp.logical_and(at >= 0, at < NEAR)
        over = jnp.where(at < 0, at + RSTEPS, at - NEAR)

        @pl.when(inside)
        def _():
            put(n, block_ref[at, :BANDS, :])

        @pl.when(jnp.logical_not(inside))
        def _():
            rows = pl.ds(pl.multiple_of(over * BANDS, BANDS), BANDS)
            put(n, edge_ref[rows, :])


def window_of(place, block, edge, copies):
    return pl.pallas_call(
        window_kernel,
        out_shape=jax.ShapeDtypeStruct((copies, NOFF * BANDS, block.shape[2]), block.dtype),
        in_specs=[SMEM, VMEM, VMEM],
        out_specs=VMEM,
        compiler_params=pltpu.CompilerParams(vmem_limit_bytes=4 << 20),
        name="window",
    )(place, block, edge)


def near_sum_kernel(rows_ref, out_ref):
    total = rows_ref[0].astype(jnp.float32)
    for b in range(1, rows_ref.shape[0]):
        total = total + rows_ref[b].astype(jnp.float32)
    for b in range(out_ref.shape[0]):
        out_ref[b] = total[b * NOFF : (b + 1) * NOFF].astype(out_ref.dtype)


def near_sum(rows, blocks):
    return pl.pallas_call(
        near_sum_kernel,
        out_shape=jax.ShapeDtypeStruct((blocks, NOFF, rows.shape[2]), rows.dtype),
        in_specs=[VMEM],
        out_specs=VMEM,
        compiler_params=pltpu.CompilerParams(vmem_limit_bytes=4 << 20),
        name="near_sum",
    )(rows)


def result_kernel(terms_ref, out_ref):
    total = terms_ref[0]
    for g in range(1, terms_ref.shape[0]):
        total = total + terms_ref[g]
    out_ref[...] = total * NG ** (-0.5)


def result_of(terms):
    return pl.pallas_call(
        result_kernel,
        out_shape=jax.ShapeDtypeStruct(terms.shape[1:], terms.dtype),
        in_specs=[VMEM],
        out_specs=VMEM,
        compiler_params=pltpu.CompilerParams(vmem_limit_bytes=2 << 20),
        name="result",
    )(terms)


def pick_kernel(place_ref, grid_ref, table_ref, out_ref, local_ref, hot_ref):
    size = grid_ref.shape[0]
    blocks = size // NEAR
    table_rows = table_ref.shape[0]
    row = grid_ref[:, :LANES].astype(jnp.float32)
    col = grid_ref[:, LANES:].astype(jnp.float32)
    base = (place_ref[0] * table_rows).astype(jnp.float32)
    for i in range(NOFF):
        d = i - RSTEPS
        row_step = row - jnp.roll(row, d, axis=0) if d else jnp.zeros_like(row)
        col_step = col - jnp.roll(col, d, axis=0) if d else jnp.zeros_like(col)
        row_step = jnp.where(row_step < 0, row_step + NKX, row_step)
        col_step = jnp.where(col_step < 0, col_step + NKX, col_step)
        local_ref[i * size : (i + 1) * size, :] = row_step * NKX + col_step - base
    lane = lax.broadcasted_iota(jnp.int32, (blocks, LANES), 1).astype(jnp.float32)
    for j in range(NEAR):
        for i in range(NOFF):
            local = local_ref[pl.ds(i * size + j, blocks, stride=NEAR), :]
            rows = pl.ds(j * blocks * NOFF + i, blocks, stride=NOFF)
            for part in range(hot_ref.shape[0]):
                hot_ref[part, rows, :] = jnp.where(local == lane + part * LANES, 1.0, 0.0)
    total = None
    for part in range(hot_ref.shape[0]):
        count = min(LANES, table_rows - part * LANES)
        term = jnp.dot(
            hot_ref[part, :, :count].astype(jnp.bfloat16),
            table_ref[part * LANES : part * LANES + count, :],
            preferred_element_type=jnp.float32,
        )
        total = term if total is None else total + term
    out_ref[...] = total.astype(jnp.bfloat16)


def pick_rows(place, grid, table):
    size = grid.shape[0]
    return pl.pallas_call(
        pick_kernel,
        out_shape=jax.ShapeDtypeStruct((size * NOFF, table.shape[1]), jnp.bfloat16),
        in_specs=[SMEM, VMEM, VMEM],
        out_specs=VMEM,
        scratch_shapes=[
            pltpu.VMEM((NOFF * size, LANES), jnp.float32),
            pltpu.VMEM((pl.cdiv(table.shape[0], LANES), size * NOFF, LANES), jnp.float32),
        ],
        compiler_params=pltpu.CompilerParams(vmem_limit_bytes=6 << 20),
        name="pick_rows",
    )(place, grid, table)


def outer_rows(singles, many):
    rows = []
    for h in range(0, singles.shape[0], 2):
        both = jnp.concatenate(
            [singles[h : h + 1] * many, singles[h + 1 : h + 2] * many], axis=0
        )
        rows.append(both.astype(jnp.bfloat16))
    return rows


def waves_kernel(
    full_ref, vec_ref, bare_ref, cond_ref, vale_ref, exch_ref, perm_ref, pts_ref, acc_ref
):
    parts = full_ref.shape[0]
    chunk = full_ref.shape[2]
    step = 3 * PAIRS

    def put(start, pieces):
        for h, piece in enumerate(pieces):
            pts_ref[start + 2 * NV * h : start + 2 * NV * (h + 1), :] = piece

    def add_chunk(s, carry):
        own = full_ref[s, RSTEPS * BANDS : (RSTEPS + 1) * BANDS, :].astype(jnp.float32)
        own_v, own_c = own[:NV], own[NV:]
        for n in range(NOFF):
            there = full_ref[s, n * BANDS : (n + 1) * BANDS, :].astype(jnp.float32)
            there_v, there_c = there[:NV], there[NV:]
            put(n * step, outer_rows(own_c, there_c))
            put(n * step + PAIRS, outer_rows(there_v, own_v))
            put(n * step + 2 * PAIRS, outer_rows(there_v, there_c))
        put(NOFF * step, outer_rows(own_c, own_v))
        vec = vec_ref[pl.ds(pl.multiple_of(s * chunk, chunk), chunk), :]
        acc_ref[...] += jnp.dot(pts_ref[...], vec, preferred_element_type=jnp.float32)
        return carry

    acc_ref[...] = jnp.zeros_like(acc_ref)
    lax.fori_loop(0, parts, add_chunk, 0)
    own_x = acc_ref[NOFF * step :, :].astype(jnp.bfloat16).astype(jnp.float32)
    weighted = (own_x * bare_ref[...]).astype(jnp.bfloat16)
    for i in range(NOFF):
        start = (NOFF - 1 - i) * step
        cond_ref[i * PAIRS : (i + 1) * PAIRS, :] = acc_ref[start : start + PAIRS, :].astype(
            jnp.bfloat16
        )
        vale_ref[i * PAIRS : (i + 1) * PAIRS, :] = acc_ref[
            start + PAIRS : start + 2 * PAIRS, :
        ].astype(jnp.bfloat16)
        there_x = acc_ref[start + 2 * PAIRS : start + 3 * PAIRS, :].astype(jnp.bfloat16)
        term = lax.dot_general(
            weighted, there_x, (((1,), (1,)), ((), ())), preferred_element_type=jnp.float32
        )
        exch_ref[i * NV : (i + 1) * NV, :] = jnp.concatenate(
            [term[c * NV : (c + 1) * NV] for c in range(NC)], axis=1
        )
    source = lax.broadcasted_iota(jnp.int32, perm_ref.shape, 0)
    target = lax.broadcasted_iota(jnp.int32, perm_ref.shape, 1)
    moved = ((source >> 3) & 7) * (NV * NC) + (source >> 6) * NC + (source & 7)
    perm_ref[...] = jnp.where(moved == target, 1.0, 0.0).astype(jnp.bfloat16)


def waves_of(full, interp_vectors, bare):
    ng = interp_vectors.shape[1]
    total = NOFF * 3 * PAIRS + PAIRS
    flops = 2 * total * interp_vectors.shape[0] * ng
    columns = NC * NV * NC
    return pl.pallas_call(
        waves_kernel,
        out_shape=(
            jax.ShapeDtypeStruct((NOFF * PAIRS, ng), jnp.bfloat16),
            jax.ShapeDtypeStruct((NOFF * PAIRS, ng), jnp.bfloat16),
            jax.ShapeDtypeStruct((NOFF * NV, columns), jnp.float32),
            jax.ShapeDtypeStruct((columns, columns), jnp.bfloat16),
        ),
        in_specs=[VMEM] * 3,
        out_specs=(VMEM,) * 4,
        scratch_shapes=[
            pltpu.VMEM((total, full.shape[2]), jnp.bfloat16),
            pltpu.VMEM((total, ng), jnp.float32),
        ],
        cost_estimate=pl.CostEstimate(
            flops=flops, bytes_accessed=6 * 1024 * 1024, transcendentals=0
        ),
        compiler_params=pltpu.CompilerParams(vmem_limit_bytes=16 << 20),
        name="pair_waves",
    )(full, interp_vectors, bare)


def final_kernel(rows_ref, cond_ref, vale_ref, exch_ref, perm_ref, out_ref, all_ref, parts_ref):
    screen = rows_ref[0].astype(jnp.float32)
    for b in range(1, rows_ref.shape[0]):
        screen = screen + rows_ref[b].astype(jnp.float32)
    for i in range(NOFF):
        weighted = (
            cond_ref[i * PAIRS : (i + 1) * PAIRS, :].astype(jnp.float32) * screen[i : i + 1]
        ).astype(jnp.bfloat16)
        direct = lax.dot_general(
            vale_ref[i * PAIRS : (i + 1) * PAIRS, :],
            weighted,
            (((1,), (1,)), ((), ())),
            preferred_element_type=jnp.float32,
        )
        all_ref[i * NV : (i + 1) * NV, :] = jnp.concatenate(
            [direct[v * NV : (v + 1) * NV] for v in range(NV)], axis=1
        )
    value = all_ref[...]
    high = value.astype(jnp.bfloat16)
    rest = value - high.astype(jnp.float32)
    middle = rest.astype(jnp.bfloat16)
    low = (rest - middle.astype(jnp.float32)).astype(jnp.bfloat16)
    perm = perm_ref[...]
    moved = (
        jnp.dot(high, perm, preferred_element_type=jnp.float32)
        + jnp.dot(middle, perm, preferred_element_type=jnp.float32)
        + jnp.dot(low, perm, preferred_element_type=jnp.float32)
    )
    partial = 2.0 * exch_ref[...] - moved
    for p in range(parts_ref.shape[0]):
        lanes = slice(p * LANES, (p + 1) * LANES)
        parts_ref[p] = partial[:, lanes]
        for v in range(NV):
            out_ref[v, :, lanes] = parts_ref[p, pl.ds(v, NOFF, stride=NV), :]


def final_terms(rows, cond, vale, exch, perm):
    return pl.pallas_call(
        final_kernel,
        out_shape=jax.ShapeDtypeStruct((NV, NOFF, NC * NV * NC), jnp.float32),
        in_specs=[VMEM] * 5,
        out_specs=VMEM,
        scratch_shapes=[
            pltpu.VMEM((NOFF * NV, NC * NV * NC), jnp.float32),
            pltpu.VMEM((NC * NV * NC // LANES, NOFF * NV, LANES), jnp.float32),
        ],
        compiler_params=pltpu.CompilerParams(vmem_limit_bytes=6 << 20),
        name="final_terms",
    )(rows, cond, vale, exch, perm)


def per_device(orbitals, interp_vectors, screening, bare_coulomb, slab_kpoints):
    size = lax.axis_size("ka")
    parts = lax.axis_size("ga")
    blocks = size // NEAR
    place = lax.axis_index("ka").astype(jnp.int32).reshape(1)
    near = near_groups(size)
    far = far_groups(size)
    message = message_of(slab_kpoints, orbitals[0])
    block = swap(message, "ka", near)
    coords, edge = edges_of(place, block, blocks)
    grid = swap(coords, "ka", far)
    edge = lax.ppermute(edge, "ka", edge_route(size))
    window = window_of(place, block, edge, parts)
    full = swap(window, "ga")
    picked = pick_rows(place, grid.reshape(size, 2 * LANES), screening)
    arrived = swap(picked.reshape(NEAR, blocks * NOFF, -1), "ka", near)
    summed = near_sum(arrived, blocks)
    summed, full = lax.optimization_barrier((summed, full))
    rows = swap(summed, "ka", far)
    cond, vale, exch, perm = waves_of(full, interp_vectors, bare_coulomb[None])
    partial = final_terms(rows, cond, vale, exch, perm)
    terms = swap(partial, "ga")
    return result_of(terms)[None, :, None, :]


def solution(mesh):
    in_specs = (P("ka", None, "ga"), P(None, "ga"), P("ka", "ga"), P("ga"), P("ka"))
    out_specs = P("ka", None, None, "ga")
    return jax.shard_map(
        per_device, mesh=mesh, in_specs=in_specs, out_specs=out_specs, check_vma=False
    )
```

time: 141 us -> 104 us (0.74)
  the two profiles are of different devices: /device:TPU:16 before, /device:TPU:2 now
where the time goes in v2:
time: 104 us
  blocking collectives  36.1 us (35%)
  waiting for transfers between devices  27.2 us (26%)
  starting transfers between devices  22.6 us (22%)
  Pallas kernels  12.6 us (12%)
  local copies, waits for them, and re-layouts  4.42 us (4%)
    all_to_all x2, blocking collectives, swap(): lax.all_to_all(tiles, axis, 0, 0, tiled=True, axis_index_groups=groups)  36.1 us
    all_to_all x4, waiting for transfers between devices, swap(): lax.all_to_all(tiles, axis, 0, 0, tiled=True, axis_index_groups=groups)  23 us
    all_to_all x4, starting transfers between devices, swap(): lax.all_to_all(tiles, axis, 0, 0, tiled=True, axis_index_groups=groups)  17.6 us
    pallas_call x1, Pallas kernels, waves_of(): pl.pallas_call(waves_kernel, out_shape=(jax.ShapeDtypeStruct((NOFF * PAIR...  8.14 us
    ppermute x1, starting transfers between devices, per_device(): edge = lax.ppermute(edge, 'ka', edge_route(size))  5.05 us
    ppermute x1, waiting for transfers between devices, per_device(): edge = lax.ppermute(edge, 'ka', edge_route(size))  4.18 us
    unnamed x8, local copies, waits for them, and re-layouts  3.81 us
  transfers between devices with their start and end apart: 5, of which 5 were waited for; matrix products, arithmetic and copies ran while one was open for 0% of the time, Pallas kernels for 10%

profile of v2, /device:TPU:2, one launch (start us, length us, event | category | flops | bytes accessed | tf_op | source)
XLA Modules:
  0.0 103.8 jit_solution(18224598395784355573)
XLA Ops:
  0.0 0.0 copy-start.3
  0.7 0.0 copy-start.1
  0.7 0.7 copy-done.1
  1.4 0.7 message.1
  2.1 5.8 %all-to-all-start = ((bf16[8,24,512]{2,1,0:T(8,128)(2,1)}), bf16[8,24,512]{2,1,0:T(8,128)(2,1)S(1)}, u32[]{:S(2)}, u32[]{:S(2)}) async-start(bf16[8,24,512]{2,1,0:T(8,128)(2,1)} %message.1), calls=%async_computation | async-start | bytes 393216 | tf_op jit(solution)/shard_map/all_to_all | solution.py:30
  7.9 7.2 %all-to-all-done.block_ref = bf16[8,24,512]{2,1,0:T(8,128)(2,1)S(1)} async-done(((bf16[8,24,512]{2,1,0:T(8,128)(2,1)}), bf16[8,24,512]{2,1,0:T(8,128)(2,1)S(1)}, u32[]{:S(2)}, u32[]{:S(2)}) %all-to-all-start) | async-done | bytes 196640 | tf_op jit(solution)/shard_map/all_to_all | solution.py:30
  15.1 26.9 %all_to_all.30 = bf16[8,8,256]{2,1,0:T(8,128)(2,1)S(1)} all-to-all(bf16[8,8,256]{2,1,0:T(8,128)(2,1)S(1)} %get-tuple-element.13), channel_id=1, replica_groups={{0,64,128,192,256,320,384,448},{8,72,136,200,264,328,392,456},{16,80,14..., dimensions={0} | all-to-all | bytes 65536 | tf_op jit(solution)/shard_map/all_to_all | solution.py:30
  42.0 0.0 copy-start
  42.0 0.9 copy-done
  42.9 1.3 %pick_rows.1 = bf16[448,512]{1,0:T(8,128)(2,1)} custom-call(s32[1]{0:T(128)} %bitcast.place_ref, bf16[64,256]{1,0:T(8,128)(2,1)S(1)} %bitcast.6, bf16[144,512]{1,0:T(8,128)(2,1)S(1)} %copy-done), custom_call_target="tpu_custom_call" | custom-call | tf_op jit(solution)/shard_map/pick_rows/pallas_call | solution.py:201
  44.2 3.5 %all-to-all-start.2 = ((bf16[8,56,512]{2,1,0:T(8,128)(2,1)}), bf16[8,56,512]{2,1,0:T(8,128)(2,1)S(1)}, u32[]{:S(2)}, u32[]{:S(2)}) async-start(bf16[8,56,512]{2,1,0:T(8,128)(2,1)} %bitcast.3), calls=%async_computation.2 | async-start | bytes 917504 | tf_op jit(solution)/shard_map/all_to_all | solution.py:30
  47.7 5.0 %collective-permute-start = (bf16[48,512]{1,0:T(8,128)(2,1)S(1)}, bf16[48,512]{1,0:T(8,128)(2,1)S(1)}, u32[]{:S(2)}, u32[]{:S(2)}) collective-permute-start(bf16[48,512]{1,0:T(8,128)(2,1)S(1)} %get-tuple-element.14), channel_id=1, source_target_pairs={{0,504},{8,496},{16,488},{40,80},{48,72},{56,64},{64,56},{72,48},{... | collective-permute-start | bytes 147464 | tf_op jit(solution)/shard_map/ppermute | solution.py:364
  52.7 4.2 %collective-permute-done.edge_ref = bf16[48,512]{1,0:T(8,128)(2,1)S(1)} collective-permute-done((bf16[48,512]{1,0:T(8,128)(2,1)S(1)}, bf16[48,512]{1,0:T(8,128)(2,1)S(1)}, u32[]{:S(2)}, u32[]{:S(2)}) %collective-permute-start) | collective-permute-done | bytes 49184 | tf_op jit(solution)/shard_map/ppermute | solution.py:364
  56.9 1.0 window.1
  58.0 0.3 all-to-all-done.2.rows_ref
  58.3 4.9 %all-to-all-start.3 = ((bf16[8,112,512]{2,1,0:T(8,128)(2,1)}), bf16[8,112,512]{2,1,0:T(8,128)(2,1)S(1)}, u32[]{:S(2)}, u32[]{:S(2)}) async-start(bf16[8,112,512]{2,1,0:T(8,128)(2,1)} %window.1), calls=%async_computation.3 | async-start | bytes 1835008 | tf_op jit(solution)/shard_map/all_to_all | solution.py:30
  63.2 0.7 near_sum.1
  63.9 12.6 %all-to-all-done.3.full_ref = bf16[8,112,512]{2,1,0:T(8,128)(2,1)S(1)} async-done(((bf16[8,112,512]{2,1,0:T(8,128)(2,1)}), bf16[8,112,512]{2,1,0:T(8,128)(2,1)S(1)}, u32[]{:S(2)}, u32[]{:S(2)}) %all-to-all-start.3) | async-done | bytes 917536 | tf_op jit(solution)/shard_map/all_to_all | solution.py:30
  76.6 3.3 %all-to-all-start.4 = ((bf16[8,7,512]{2,1,0:T(8,128)(2,1)}), bf16[8,7,512]{2,1,0:T(8,128)(2,1)S(1)}, u32[]{:S(2)}, u32[]{:S(2)}) async-start(bf16[8,7,512]{2,1,0:T(8,128)(2,1)} %near_sum.1), calls=%async_computation.4 | async-start | bytes 131072 | tf_op jit(solution)/shard_map/all_to_all | solution.py:30
  79.9 0.0 copy-done.3
  79.9 0.0 copy-start.2
  79.9 2.2 %copy-done.2 = bf16[4096,512]{1,0:T(8,128)(2,1)S(1)} copy-done((bf16[4096,512]{1,0:T(8,128)(2,1)S(1)}, bf16[4096,512]{1,0:T(8,128)(2,1)}, u32[]{:S(2)}) %copy-start.2) | copy-done | bytes 4194328
  82.1 8.1 %pair_waves.1 = (bf16[448,512]{1,0:T(8,128)(2,1)S(1)}, bf16[448,512]{1,0:T(8,128)(2,1)S(1)}, f32[56,512]{1,0:T(8,128)S(1)}, bf16[512,512]{1,0:T(8,128)(2,1)S(1)}) custom-call(bf16[8,112,512]{2,1,0:T(8,128)(2,1)S(1)} %all-to-all-done.3.full_ref, bf16[4096,512]{1,0:T(8,128)(2,1)S(1)} %copy-done.2, f32[1,512]{1,0:T(1,128)S(1)} %bitcast.9), custom_call_target="tpu_custom_call" | custom-call | flops 5905580032 | bytes 6291456 | tf_op jit(solution)/shard_map/pair_waves/pallas_call | solution.py:280
  90.3 2.9 %all-to-all-done.4.rows_ref = bf16[8,7,512]{2,1,0:T(8,128)(2,1)S(1)} async-done(((bf16[8,7,512]{2,1,0:T(8,128)(2,1)}), bf16[8,7,512]{2,1,0:T(8,128)(2,1)S(1)}, u32[]{:S(2)}, u32[]{:S(2)}) %all-to-all-start.4) | async-done | bytes 57376 | tf_op jit(solution)/shard_map/all_to_all | solution.py:30
  93.2 0.7 final_terms.1
  93.9 9.2 %all_to_all.31.terms_ref = f32[8,7,512]{2,1,0:T(8,128)S(1)} all-to-all(f32[8,7,512]{2,1,0:T(8,128)S(1)} %final_terms.1), channel_id=1, replica_groups=mesh['ka'=64,'ga'=8] {'ga'}, dimensions={0} | all-to-all | bytes 229376 | tf_op jit(solution)/shard_map/all_to_all | solution.py:30
  103.1 0.6 copy.6
  (2 shorter events, 0.0 us)
Async XLA Ops:
  0.0 79.9 %copy-start.3 = (f32[512]{0:T(512)S(1)}, f32[512]{0:T(512)}, u32[]{:S(2)}) copy-start(f32[512]{0:T(512)} %param.8) | copy-start | bytes 6148
  0.7 0.7 copy-start.1
  2.1 13.0 %all-to-all-start = ((bf16[8,24,512]{2,1,0:T(8,128)(2,1)}), bf16[8,24,512]{2,1,0:T(8,128)(2,1)S(1)}, u32[]{:S(2)}, u32[]{:S(2)}) async-start(bf16[8,24,512]{2,1,0:T(8,128)(2,1)} %message.1), calls=%async_computation | async-start | bytes 393216 | tf_op jit(solution)/shard_map/all_to_all | solution.py:30
  42.0 0.9 copy-start
  44.2 14.1 %all-to-all-start.2 = ((bf16[8,56,512]{2,1,0:T(8,128)(2,1)}), bf16[8,56,512]{2,1,0:T(8,128)(2,1)S(1)}, u32[]{:S(2)}, u32[]{:S(2)}) async-start(bf16[8,56,512]{2,1,0:T(8,128)(2,1)} %bitcast.3), calls=%async_computation.2 | async-start | bytes 917504 | tf_op jit(solution)/shard_map/all_to_all | solution.py:30
  47.7 9.2 %collective-permute-start = (bf16[48,512]{1,0:T(8,128)(2,1)S(1)}, bf16[48,512]{1,0:T(8,128)(2,1)S(1)}, u32[]{:S(2)}, u32[]{:S(2)}) collective-permute-start(bf16[48,512]{1,0:T(8,128)(2,1)S(1)} %get-tuple-element.14), channel_id=1, source_target_pairs={{0,504},{8,496},{16,488},{40,80},{48,72},{56,64},{64,56},{72,48},{... | collective-permute-start | bytes 147464 | tf_op jit(solution)/shard_map/ppermute | solution.py:364
  58.3 18.3 %all-to-all-start.3 = ((bf16[8,112,512]{2,1,0:T(8,128)(2,1)}), bf16[8,112,512]{2,1,0:T(8,128)(2,1)S(1)}, u32[]{:S(2)}, u32[]{:S(2)}) async-start(bf16[8,112,512]{2,1,0:T(8,128)(2,1)} %window.1), calls=%async_computation.3 | async-start | bytes 1835008 | tf_op jit(solution)/shard_map/all_to_all | solution.py:30
  76.6 16.6 %all-to-all-start.4 = ((bf16[8,7,512]{2,1,0:T(8,128)(2,1)}), bf16[8,7,512]{2,1,0:T(8,128)(2,1)S(1)}, u32[]{:S(2)}, u32[]{:S(2)}) async-start(bf16[8,7,512]{2,1,0:T(8,128)(2,1)} %near_sum.1), calls=%async_computation.4 | async-start | bytes 131072 | tf_op jit(solution)/shard_map/all_to_all | solution.py:30
  79.9 2.2 %copy-start.2 = (bf16[4096,512]{1,0:T(8,128)(2,1)S(1)}, bf16[4096,512]{1,0:T(8,128)(2,1)}, u32[]{:S(2)}) copy-start(bf16[4096,512]{1,0:T(8,128)(2,1)} %vec_ref.1) | copy-start | bytes 12582916

commit v3 on v2

--- a/solution.py
+++ b/solution.py
@@ -94,11 +94,9 @@
 
 def window_kernel(place_ref, block_ref, edge_ref, out_ref):
     inner = lax.rem(place_ref[0], NEAR)
-    copies = out_ref.shape[0]
 
     def put(n, value):
-        for g in range(copies):
-            out_ref[g, n * BANDS : (n + 1) * BANDS, :] = value
+        out_ref[n * BANDS : (n + 1) * BANDS, :] = value
 
     for n in range(NOFF):
         at = inner + (n - RSTEPS)
@@ -115,10 +113,10 @@
             put(n, edge_ref[rows, :])
 
 
-def window_of(place, block, edge, copies):
+def window_of(place, block, edge):
     return pl.pallas_call(
         window_kernel,
-        out_shape=jax.ShapeDtypeStruct((copies, NOFF * BANDS, block.shape[2]), block.dtype),
+        out_shape=jax.ShapeDtypeStruct((NOFF * BANDS, block.shape[2]), block.dtype),
         in_specs=[SMEM, VMEM, VMEM],
         out_specs=VMEM,
         compiler_params=pltpu.CompilerParams(vmem_limit_bytes=4 << 20),
@@ -222,33 +220,56 @@
     return rows
 
 
+GATHER_STEPS = (2, 1, 4)
+
+
+def gather_mask(s):
+    first, second, third = GATHER_STEPS
+    return (s & 1) * first + ((s >> 1) & 1) * second + ((s >> 2) & 1) * third
+
+
 def waves_kernel(
-    full_ref, vec_ref, bare_ref, cond_ref, vale_ref, exch_ref, perm_ref, pts_ref, acc_ref
+    part_ref,
+    first_ref,
+    second_ref,
+    vec_ref,
+    bare_ref,
+    cond_ref,
+    vale_ref,
+    exch_ref,
+    perm_ref,
+    pts_ref,
+    acc_ref,
 ):
-    parts = full_ref.shape[0]
-    chunk = full_ref.shape[2]
+    half = first_ref.shape[0]
+    chunk = first_ref.shape[2]
     step = 3 * PAIRS
 
     def put(start, pieces):
         for h, piece in enumerate(pieces):
             pts_ref[start + 2 * NV * h : start + 2 * NV * (h + 1), :] = piece
 
-    def add_chunk(s, carry):
-        own = full_ref[s, RSTEPS * BANDS : (RSTEPS + 1) * BANDS, :].astype(jnp.float32)
-        own_v, own_c = own[:NV], own[NV:]
-        for n in range(NOFF):
-            there = full_ref[s, n * BANDS : (n + 1) * BANDS, :].astype(jnp.float32)
-            there_v, there_c = there[:NV], there[NV:]
-            put(n * step, outer_rows(own_c, there_c))
-            put(n * step + PAIRS, outer_rows(there_v, own_v))
-            put(n * step + 2 * PAIRS, outer_rows(there_v, there_c))
-        put(NOFF * step, outer_rows(own_c, own_v))
-        vec = vec_ref[pl.ds(pl.multiple_of(s * chunk, chunk), chunk), :]
-        acc_ref[...] += jnp.dot(pts_ref[...], vec, preferred_element_type=jnp.float32)
-        return carry
+    def add_chunk(source_ref, offset):
+        def add(s, carry):
+            own = source_ref[s, RSTEPS * BANDS : (RSTEPS + 1) * BANDS, :].astype(jnp.float32)
+            own_v, own_c = own[:NV], own[NV:]
+            for n in range(NOFF):
+                there = source_ref[s, n * BANDS : (n + 1) * BANDS, :].astype(jnp.float32)
+                there_v, there_c = there[:NV], there[NV:]
+                put(n * step, outer_rows(own_c, there_c))
+                put(n * step + PAIRS, outer_rows(there_v, own_v))
+                put(n * step + 2 * PAIRS, outer_rows(there_v, there_c))
+            put(NOFF * step, outer_rows(own_c, own_v))
+            at = jnp.bitwise_xor(part_ref[0], gather_mask(s + offset))
+            vec = vec_ref[pl.ds(pl.multiple_of(at * chunk, chunk), chunk), :]
+            acc_ref[...] += jnp.dot(pts_ref[...], vec, preferred_element_type=jnp.float32)
+            return carry
+
+        return add
 
     acc_ref[...] = jnp.zeros_like(acc_ref)
-    lax.fori_loop(0, parts, add_chunk, 0)
+    lax.fori_loop(0, half, add_chunk(first_ref, 0), 0)
+    lax.fori_loop(0, half, add_chunk(second_ref, half), 0)
     own_x = acc_ref[NOFF * step :, :].astype(jnp.bfloat16).astype(jnp.float32)
     weighted = (own_x * bare_ref[...]).astype(jnp.bfloat16)
     for i in range(NOFF):
@@ -272,7 +293,7 @@
     perm_ref[...] = jnp.where(moved == target, 1.0, 0.0).astype(jnp.bfloat16)
 
 
-def waves_of(full, interp_vectors, bare):
+def waves_of(part, first, second, interp_vectors, bare):
     ng = interp_vectors.shape[1]
     total = NOFF * 3 * PAIRS + PAIRS
     flops = 2 * total * interp_vectors.shape[0] * ng
@@ -285,10 +306,10 @@
             jax.ShapeDtypeStruct((NOFF * NV, columns), jnp.float32),
             jax.ShapeDtypeStruct((columns, columns), jnp.bfloat16),
         ),
-        in_specs=[VMEM] * 3,
+        in_specs=[SMEM] + [VMEM] * 4,
         out_specs=(VMEM,) * 4,
         scratch_shapes=[
-            pltpu.VMEM((total, full.shape[2]), jnp.bfloat16),
+            pltpu.VMEM((total, first.shape[2]), jnp.bfloat16),
             pltpu.VMEM((total, ng), jnp.float32),
         ],
         cost_estimate=pl.CostEstimate(
@@ -296,7 +317,7 @@
         ),
         compiler_params=pltpu.CompilerParams(vmem_limit_bytes=16 << 20),
         name="pair_waves",
-    )(full, interp_vectors, bare)
+    )(part, first, second, interp_vectors, bare)
 
 
 def final_kernel(rows_ref, cond_ref, vale_ref, exch_ref, perm_ref, out_ref, all_ref, parts_ref):
@@ -355,6 +376,7 @@
     parts = lax.axis_size("ga")
     blocks = size // NEAR
     place = lax.axis_index("ka").astype(jnp.int32).reshape(1)
+    part = lax.axis_index("ga").astype(jnp.int32).reshape(1)
     near = near_groups(size)
     far = far_groups(size)
     message = message_of(slab_kpoints, orbitals[0])
@@ -362,14 +384,18 @@
     coords, edge = edges_of(place, block, blocks)
     grid = swap(coords, "ka", far)
     edge = lax.ppermute(edge, "ka", edge_route(size))
-    window = window_of(place, block, edge, parts)
-    full = swap(window, "ga")
+    window = window_of(place, block, edge)[None]
+    swaps = [[(g, g ^ mask) for g in range(parts)] for mask in GATHER_STEPS]
+    two = jnp.concatenate([window, lax.ppermute(window, "ga", swaps[0])])
+    four = jnp.concatenate([two, lax.ppermute(two, "ga", swaps[1])])
+    other = lax.ppermute(four, "ga", swaps[2])
     picked = pick_rows(place, grid.reshape(size, 2 * LANES), screening)
     arrived = swap(picked.reshape(NEAR, blocks * NOFF, -1), "ka", near)
     summed = near_sum(arrived, blocks)
-    summed, full = lax.optimization_barrier((summed, full))
     rows = swap(summed, "ka", far)
-    cond, vale, exch, perm = waves_of(full, interp_vectors, bare_coulomb[None])
+    cond, vale, exch, perm = waves_of(
+        part, four, other, interp_vectors, bare_coulomb[None]
+    )
     partial = final_terms(rows, cond, vale, exch, perm)
     terms = swap(partial, "ga")
     return result_of(terms)[None, :, None, :]

time: 104 us -> 110 us (1.058)
  starting transfers between devices: 22.6 us -> 26.8 us
  waiting for transfers between devices: 27.2 us -> 28.8 us
    ppermute x0 -> x3, waiting for transfers between devices: none -> 17.5 us  [the longest x1 6.44 us: per_device(): four = jnp.concatenate([two, lax.ppermute(two, 'ga', swaps[1])])]
    all_to_all x4 -> x3, waiting for transfers between devices: 23 us -> 7.18 us  [swap(): lax.all_to_all(tiles, axis, 0, 0, tiled=True, axis_index_groups=groups)]
    ppermute x0 -> x3, starting transfers between devices: none -> 9.06 us  [the longest x1 4.03 us: per_device(): two = jnp.concatenate([window, lax.ppermute(window, 'ga', swaps[0])])]
    all_to_all x4 -> x3, starting transfers between devices: 17.6 us -> 12.6 us  [swap(): lax.all_to_all(tiles, axis, 0, 0, tiled=True, axis_index_groups=groups)]
  transfers between devices with their start and end apart: 5 -> 7, of which waited for: 5 -> 5; matrix products, arithmetic and copies ran while one was open for 0% -> 0% of each run, Pallas kernels for 10% -> 8%
where the time goes in v3:
time: 110 us
  blocking collectives  37.1 us (34%)
  waiting for transfers between devices  28.8 us (26%)
  starting transfers between devices  26.8 us (24%)
  Pallas kernels  11.6 us (11%)
  local copies, waits for them, and re-layouts  4.43 us (4%)
    all_to_all x2, blocking collectives, swap(): lax.all_to_all(tiles, axis, 0, 0, tiled=True, axis_index_groups=groups)  37.1 us
    all_to_all x3, starting transfers between devices, swap(): lax.all_to_all(tiles, axis, 0, 0, tiled=True, axis_index_groups=groups)  12.6 us
    pallas_call x1, Pallas kernels, waves_of(): pl.pallas_call(waves_kernel, out_shape=(jax.ShapeDtypeStruct((NOFF * PAIR...  8.2 us
    all_to_all x3, waiting for transfers between devices, swap(): lax.all_to_all(tiles, axis, 0, 0, tiled=True, axis_index_groups=groups)  7.18 us
    ppermute x1, waiting for transfers between devices, per_device(): four = jnp.concatenate([two, lax.ppermute(two, 'ga', swaps[1])])  6.44 us
    ppermute x1, waiting for transfers between devices, per_device(): other = lax.ppermute(four, 'ga', swaps[2])  6.29 us
    ppermute x1, starting transfers between devices, per_device(): edge = lax.ppermute(edge, 'ka', edge_route(size))  5.05 us
    ppermute x1, waiting for transfers between devices, per_device(): two = jnp.concatenate([window, lax.ppermute(window, 'ga', swaps[0])])  4.76 us
  transfers between devices with their start and end apart: 7, of which 5 were waited for; matrix products, arithmetic and copies ran while one was open for 0% of the time, Pallas kernels for 8%

profile of v3, /device:TPU:2, one launch (start us, length us, event | category | flops | bytes accessed | tf_op | source)
XLA Modules:
  0.0 109.6 jit_solution(3454433380126888300)
XLA Ops:
  0.0 0.0 copy-start.3
  0.7 0.0 copy-start.1
  0.7 0.7 copy-done.1
  1.4 0.7 message.1
  2.1 5.8 %all-to-all-start = ((bf16[8,24,512]{2,1,0:T(8,128)(2,1)}), bf16[8,24,512]{2,1,0:T(8,128)(2,1)S(1)}, u32[]{:S(2)}, u32[]{:S(2)}) async-start(bf16[8,24,512]{2,1,0:T(8,128)(2,1)} %message.1), calls=%async_computation | async-start | bytes 393216 | tf_op jit(solution)/shard_map/all_to_all | solution.py:30
  7.9 7.2 %all-to-all-done.block_ref = bf16[8,24,512]{2,1,0:T(8,128)(2,1)S(1)} async-done(((bf16[8,24,512]{2,1,0:T(8,128)(2,1)}), bf16[8,24,512]{2,1,0:T(8,128)(2,1)S(1)}, u32[]{:S(2)}, u32[]{:S(2)}) %all-to-all-start) | async-done | bytes 196640 | tf_op jit(solution)/shard_map/all_to_all | solution.py:30
  15.1 26.9 %all_to_all.25 = bf16[8,8,256]{2,1,0:T(8,128)(2,1)S(1)} all-to-all(bf16[8,8,256]{2,1,0:T(8,128)(2,1)S(1)} %get-tuple-element.11), channel_id=1, replica_groups={{0,64,128,192,256,320,384,448},{8,72,136,200,264,328,392,456},{16,80,14..., dimensions={0} | all-to-all | bytes 65536 | tf_op jit(solution)/shard_map/all_to_all | solution.py:30
  42.0 0.0 copy-start
  42.0 0.9 copy-done
  42.9 1.3 %pick_rows.1 = bf16[448,512]{1,0:T(8,128)(2,1)} custom-call(s32[1]{0:T(128)} %bitcast.place_ref, bf16[64,256]{1,0:T(8,128)(2,1)S(1)} %bitcast.11, bf16[144,512]{1,0:T(8,128)(2,1)S(1)} %copy-done), custom_call_target="tpu_custom_call" | custom-call | tf_op jit(solution)/shard_map/pick_rows/pallas_call | solution.py:199
  44.2 3.5 %all-to-all-start.2 = ((bf16[8,56,512]{2,1,0:T(8,128)(2,1)}), bf16[8,56,512]{2,1,0:T(8,128)(2,1)S(1)}, u32[]{:S(2)}, u32[]{:S(2)}) async-start(bf16[8,56,512]{2,1,0:T(8,128)(2,1)} %bitcast.3), calls=%async_computation.2 | async-start | bytes 917504 | tf_op jit(solution)/shard_map/all_to_all | solution.py:30
  47.7 5.0 %collective-permute-start = (bf16[48,512]{1,0:T(8,128)(2,1)S(1)}, bf16[48,512]{1,0:T(8,128)(2,1)S(1)}, u32[]{:S(2)}, u32[]{:S(2)}) collective-permute-start(bf16[48,512]{1,0:T(8,128)(2,1)S(1)} %get-tuple-element.12), channel_id=1, source_target_pairs={{0,504},{8,496},{16,488},{40,80},{48,72},{56,64},{64,56},{72,48},{... | collective-permute-start | bytes 147464 | tf_op jit(solution)/shard_map/ppermute | solution.py:386
  52.7 4.2 %collective-permute-done.edge_ref = bf16[48,512]{1,0:T(8,128)(2,1)S(1)} collective-permute-done((bf16[48,512]{1,0:T(8,128)(2,1)S(1)}, bf16[48,512]{1,0:T(8,128)(2,1)S(1)}, u32[]{:S(2)}, u32[]{:S(2)}) %collective-permute-start) | collective-permute-done | bytes 49184 | tf_op jit(solution)/shard_map/ppermute | solution.py:386
  56.9 4.0 %collective-permute-start.1 = (bf16[1,112,512]{2,1,0:T(8,128)(2,1)S(1)}, bf16[1,112,512]{2,1,0:T(8,128)(2,1)S(1)}, u32[]{:S(2)}, u32[]{:S(2)}) collective-permute-start(bf16[1,112,512]{2,1,0:T(8,128)(2,1)S(1)} %bitcast.8), channel_id=1, source_target_pairs={{0,2},{1,3},{2,0},{3,1},{4,6},{5,7},{6,4},{7,5},{8,10},{9,11},{10,... | collective-permute-start | bytes 344072 | tf_op jit(solution)/shard_map/ppermute | solution.py:389
  61.0 4.8 %collective-permute-done.1 = bf16[1,112,512]{2,1,0:T(8,128)(2,1)S(1)} collective-permute-done((bf16[1,112,512]{2,1,0:T(8,128)(2,1)S(1)}, bf16[1,112,512]{2,1,0:T(8,128)(2,1)S(1)}, u32[]{:S(2)}, u32[]{:S(2)}) %collective-permute-start.1) | collective-permute-done | bytes 114720 | tf_op jit(solution)/shard_map/ppermute | solution.py:389
  65.8 2.4 %collective-permute-start.2 = (bf16[2,112,512]{2,1,0:T(8,128)(2,1)S(1)}, bf16[2,112,512]{2,1,0:T(8,128)(2,1)S(1)}, u32[]{:S(2)}, u32[]{:S(2)}) collective-permute-start(bf16[2,112,512]{2,1,0:T(8,128)(2,1)S(1)} %pad_maximum_fusion.1), channel_id=1, source_target_pairs={{0,1},{1,0},{2,3},{3,2},{4,5},{5,4},{6,7},{7,6},{8,9},{9,8},{10,11... | collective-permute-start | bytes 688136 | tf_op jit(solution)/shard_map/ppermute | solution.py:390
  68.2 6.4 %collective-permute-done.2 = bf16[2,112,512]{2,1,0:T(8,128)(2,1)S(1)} collective-permute-done((bf16[2,112,512]{2,1,0:T(8,128)(2,1)S(1)}, bf16[2,112,512]{2,1,0:T(8,128)(2,1)S(1)}, u32[]{:S(2)}, u32[]{:S(2)}) %collective-permute-start.2) | collective-permute-done | bytes 229408 | tf_op jit(solution)/shard_map/ppermute | solution.py:390
  74.7 2.6 %collective-permute-start.3 = (bf16[4,112,512]{2,1,0:T(8,128)(2,1)S(1)}, bf16[4,112,512]{2,1,0:T(8,128)(2,1)S(1)}, u32[]{:S(2)}, u32[]{:S(2)}) collective-permute-start(bf16[4,112,512]{2,1,0:T(8,128)(2,1)S(1)} %pad_maximum_fusion.first_ref), channel_id=1, source_target_pairs={{0,4},{1,5},{2,6},{3,7},{4,0},{5,1},{6,2},{7,3},{8,12},{9,13},{10,... | collective-permute-start | bytes 1376264 | tf_op jit(solution)/shard_map/ppermute | solution.py:391
  77.3 0.0 all-to-all-done.2.rows_ref
  77.3 0.7 near_sum.1
  78.0 3.3 %all-to-all-start.3 = ((bf16[8,7,512]{2,1,0:T(8,128)(2,1)}), bf16[8,7,512]{2,1,0:T(8,128)(2,1)S(1)}, u32[]{:S(2)}, u32[]{:S(2)}) async-start(bf16[8,7,512]{2,1,0:T(8,128)(2,1)} %near_sum.1), calls=%async_computation.3 | async-start | bytes 131072 | tf_op jit(solution)/shard_map/all_to_all | solution.py:30
  81.4 6.3 %collective-permute-done.3.second_ref = bf16[4,112,512]{2,1,0:T(8,128)(2,1)S(1)} collective-permute-done((bf16[4,112,512]{2,1,0:T(8,128)(2,1)S(1)}, bf16[4,112,512]{2,1,0:T(8,128)(2,1)S(1)}, u32[]{:S(2)}, u32[]{:S(2)}) %collective-permute-start.3) | collective-permute-done | bytes 458784 | tf_op jit(solution)/shard_map/ppermute | solution.py:391
  87.7 0.0 copy-done.3
  87.7 0.0 copy-start.2
  87.7 2.2 %copy-done.2 = bf16[4096,512]{1,0:T(8,128)(2,1)S(1)} copy-done((bf16[4096,512]{1,0:T(8,128)(2,1)S(1)}, bf16[4096,512]{1,0:T(8,128)(2,1)}, u32[]{:S(2)}) %copy-start.2) | copy-done | bytes 4194328
  89.8 8.2 %pair_waves.1 = (bf16[448,512]{1,0:T(8,128)(2,1)S(1)}, bf16[448,512]{1,0:T(8,128)(2,1)S(1)}, f32[56,512]{1,0:T(8,128)S(1)}, bf16[512,512]{1,0:T(8,128)(2,1)S(1)}) custom-call(s32[1]{0:T(128)} %bitcast.4.part_ref, bf16[4,112,512]{2,1,0:T(8,128)(2,1)S(1)} %pad_maximum_fusion.first_ref, bf16[4,112,512]{2,1,0:T(8,128)(2,1)S(1)} %collective-permute-done.3.second_ref, ...), custom_call_target="tpu_custom_call" | custom-call | flops 5905580032 | bytes 6291456 | tf_op jit(solution)/shard_map/pair_waves/pallas_call | solution.py:301
  98.1 0.0 all-to-all-done.3.rows_ref
  98.1 0.7 final_terms.1
  98.8 10.2 %all_to_all.26.terms_ref = f32[8,7,512]{2,1,0:T(8,128)S(1)} all-to-all(f32[8,7,512]{2,1,0:T(8,128)S(1)} %final_terms.1), channel_id=1, replica_groups=mesh['ka'=64,'ga'=8] {'ga'}, dimensions={0} | all-to-all | bytes 229376 | tf_op jit(solution)/shard_map/all_to_all | solution.py:30
  109.0 0.6 copy.6
  (5 shorter events, 0.1 us)
Async XLA Ops:
  0.0 87.7 %copy-start.3 = (f32[512]{0:T(512)S(1)}, f32[512]{0:T(512)}, u32[]{:S(2)}) copy-start(f32[512]{0:T(512)} %param.8) | copy-start | bytes 6148
  0.7 0.7 copy-start.1
  2.1 13.0 %all-to-all-start = ((bf16[8,24,512]{2,1,0:T(8,128)(2,1)}), bf16[8,24,512]{2,1,0:T(8,128)(2,1)S(1)}, u32[]{:S(2)}, u32[]{:S(2)}) async-start(bf16[8,24,512]{2,1,0:T(8,128)(2,1)} %message.1), calls=%async_computation | async-start | bytes 393216 | tf_op jit(solution)/shard_map/all_to_all | solution.py:30
  42.0 0.9 copy-start
  44.2 33.1 %all-to-all-start.2 = ((bf16[8,56,512]{2,1,0:T(8,128)(2,1)}), bf16[8,56,512]{2,1,0:T(8,128)(2,1)S(1)}, u32[]{:S(2)}, u32[]{:S(2)}) async-start(bf16[8,56,512]{2,1,0:T(8,128)(2,1)} %bitcast.3), calls=%async_computation.2 | async-start | bytes 917504 | tf_op jit(solution)/shard_map/all_to_all | solution.py:30
  47.7 9.2 %collective-permute-start = (bf16[48,512]{1,0:T(8,128)(2,1)S(1)}, bf16[48,512]{1,0:T(8,128)(2,1)S(1)}, u32[]{:S(2)}, u32[]{:S(2)}) collective-permute-start(bf16[48,512]{1,0:T(8,128)(2,1)S(1)} %get-tuple-element.12), channel_id=1, source_target_pairs={{0,504},{8,496},{16,488},{40,80},{48,72},{56,64},{64,56},{72,48},{... | collective-permute-start | bytes 147464 | tf_op jit(solution)/shard_map/ppermute | solution.py:386
  56.9 8.8 %collective-permute-start.1 = (bf16[1,112,512]{2,1,0:T(8,128)(2,1)S(1)}, bf16[1,112,512]{2,1,0:T(8,128)(2,1)S(1)}, u32[]{:S(2)}, u32[]{:S(2)}) collective-permute-start(bf16[1,112,512]{2,1,0:T(8,128)(2,1)S(1)} %bitcast.8), channel_id=1, source_target_pairs={{0,2},{1,3},{2,0},{3,1},{4,6},{5,7},{6,4},{7,5},{8,10},{9,11},{10,... | collective-permute-start | bytes 344072 | tf_op jit(solution)/shard_map/ppermute | solution.py:389
  65.8 8.9 %collective-permute-start.2 = (bf16[2,112,512]{2,1,0:T(8,128)(2,1)S(1)}, bf16[2,112,512]{2,1,0:T(8,128)(2,1)S(1)}, u32[]{:S(2)}, u32[]{:S(2)}) collective-permute-start(bf16[2,112,512]{2,1,0:T(8,128)(2,1)S(1)} %pad_maximum_fusion.1), channel_id=1, source_target_pairs={{0,1},{1,0},{2,3},{3,2},{4,5},{5,4},{6,7},{7,6},{8,9},{9,8},{10,11... | collective-permute-start | bytes 688136 | tf_op jit(solution)/shard_map/ppermute | solution.py:390
  74.7 13.0 %collective-permute-start.3 = (bf16[4,112,512]{2,1,0:T(8,128)(2,1)S(1)}, bf16[4,112,512]{2,1,0:T(8,128)(2,1)S(1)}, u32[]{:S(2)}, u32[]{:S(2)}) collective-permute-start(bf16[4,112,512]{2,1,0:T(8,128)(2,1)S(1)} %pad_maximum_fusion.first_ref), channel_id=1, source_target_pairs={{0,4},{1,5},{2,6},{3,7},{4,0},{5,1},{6,2},{7,3},{8,12},{9,13},{10,... | collective-permute-start | bytes 1376264 | tf_op jit(solution)/shard_map/ppermute | solution.py:391
  78.0 20.1 %all-to-all-start.3 = ((bf16[8,7,512]{2,1,0:T(8,128)(2,1)}), bf16[8,7,512]{2,1,0:T(8,128)(2,1)S(1)}, u32[]{:S(2)}, u32[]{:S(2)}) async-start(bf16[8,7,512]{2,1,0:T(8,128)(2,1)} %near_sum.1), calls=%async_computation.3 | async-start | bytes 131072 | tf_op jit(solution)/shard_map/all_to_all | solution.py:30
  87.7 2.2 %copy-start.2 = (bf16[4096,512]{1,0:T(8,128)(2,1)S(1)}, bf16[4096,512]{1,0:T(8,128)(2,1)}, u32[]{:S(2)}) copy-start(bf16[4096,512]{1,0:T(8,128)(2,1)} %vec_ref.1) | copy-start | bytes 12582916

commit v4 on v3

--- a/solution.py
+++ b/solution.py
@@ -34,24 +34,29 @@
 SMEM = pl.BlockSpec(memory_space=pltpu.SMEM)
 
 
-def message_kernel(point_ref, own_ref, out_ref):
+def message_kernel(point_ref, own_hbm, out_ref, own_ref, own_sem):
+    own_copy = pltpu.make_async_copy(own_hbm, own_ref, own_sem)
+    own_copy.start()
     chunk = own_ref.shape[1]
     row = point_ref[0] // NKX
     col = point_ref[0] - row * NKX
     lane = lax.broadcasted_iota(jnp.int32, (NEAR, chunk), 1)
     coords = jnp.where(lane < LANES, row, col).astype(jnp.float32).astype(jnp.bfloat16)
     for j in range(out_ref.shape[0]):
+        out_ref[j, BANDS:, :] = coords
+    own_copy.wait()
+    for j in range(out_ref.shape[0]):
         out_ref[j, :BANDS, :] = own_ref[...]
-        out_ref[j, BANDS:, :] = coords
 
 
 def message_of(points, own):
     return pl.pallas_call(
         message_kernel,
         out_shape=jax.ShapeDtypeStruct((NEAR, BANDS + NEAR, own.shape[1]), own.dtype),
-        in_specs=[SMEM, VMEM],
+        in_specs=[SMEM, pl.BlockSpec(memory_space=pl.ANY)],
         out_specs=VMEM,
-        compiler_params=pltpu.CompilerParams(vmem_limit_bytes=2 << 20),
+        scratch_shapes=[pltpu.VMEM(own.shape, own.dtype), pltpu.SemaphoreType.DMA],
+        compiler_params=pltpu.CompilerParams(vmem_limit_bytes=67043328),
         name="message",
     )(points, own)
 
@@ -92,7 +97,8 @@
     return route
 
 
-def window_kernel(place_ref, block_ref, edge_ref, out_ref):
+def window_kernel(place_ref, block_ref, edge_ref, table_ref, out_ref, held_ref):
+    held_ref[...] = table_ref[...]
     inner = lax.rem(place_ref[0], NEAR)
 
     def put(n, value):
@@ -113,15 +119,18 @@
             put(n, edge_ref[rows, :])
 
 
-def window_of(place, block, edge):
+def window_of(place, block, edge, table):
     return pl.pallas_call(
         window_kernel,
-        out_shape=jax.ShapeDtypeStruct((NOFF * BANDS, block.shape[2]), block.dtype),
-        in_specs=[SMEM, VMEM, VMEM],
-        out_specs=VMEM,
+        out_shape=(
+            jax.ShapeDtypeStruct((NOFF * BANDS, block.shape[2]), block.dtype),
+            jax.ShapeDtypeStruct(table.shape, table.dtype),
+        ),
+        in_specs=[SMEM, VMEM, VMEM, VMEM],
+        out_specs=(VMEM, VMEM),
         compiler_params=pltpu.CompilerParams(vmem_limit_bytes=4 << 20),
         name="window",
-    )(place, block, edge)
+    )(place, block, edge, table)
 
 
 def near_sum_kernel(rows_ref, out_ref):
@@ -147,13 +156,13 @@
     total = terms_ref[0]
     for g in range(1, terms_ref.shape[0]):
         total = total + terms_ref[g]
-    out_ref[...] = total * NG ** (-0.5)
+    out_ref[0, :, 0, :] = total * NG ** (-0.5)
 
 
 def result_of(terms):
     return pl.pallas_call(
         result_kernel,
-        out_shape=jax.ShapeDtypeStruct(terms.shape[1:], terms.dtype),
+        out_shape=jax.ShapeDtypeStruct((1, NOFF, 1, terms.shape[2]), terms.dtype),
         in_specs=[VMEM],
         out_specs=VMEM,
         compiler_params=pltpu.CompilerParams(vmem_limit_bytes=2 << 20),
@@ -232,44 +241,65 @@
     part_ref,
     first_ref,
     second_ref,
-    vec_ref,
+    vec_hbm,
     bare_ref,
     cond_ref,
     vale_ref,
     exch_ref,
     perm_ref,
-    pts_ref,
+    all_ref,
+    even_ref,
+    odd_ref,
     acc_ref,
+    vec_ref,
+    vec_sem,
 ):
     half = first_ref.shape[0]
     chunk = first_ref.shape[2]
     step = 3 * PAIRS
 
-    def put(start, pieces):
-        for h, piece in enumerate(pieces):
-            pts_ref[start + 2 * NV * h : start + 2 * NV * (h + 1), :] = piece
-
-    def add_chunk(source_ref, offset):
-        def add(s, carry):
-            own = source_ref[s, RSTEPS * BANDS : (RSTEPS + 1) * BANDS, :].astype(jnp.float32)
-            own_v, own_c = own[:NV], own[NV:]
-            for n in range(NOFF):
-                there = source_ref[s, n * BANDS : (n + 1) * BANDS, :].astype(jnp.float32)
-                there_v, there_c = there[:NV], there[NV:]
-                put(n * step, outer_rows(own_c, there_c))
-                put(n * step + PAIRS, outer_rows(there_v, own_v))
-                put(n * step + 2 * PAIRS, outer_rows(there_v, there_c))
-            put(NOFF * step, outer_rows(own_c, own_v))
-            at = jnp.bitwise_xor(part_ref[0], gather_mask(s + offset))
-            vec = vec_ref[pl.ds(pl.multiple_of(at * chunk, chunk), chunk), :]
-            acc_ref[...] += jnp.dot(pts_ref[...], vec, preferred_element_type=jnp.float32)
-            return carry
-
-        return add
-
+    def vec_copy(s):
+        at = jnp.bitwise_xor(part_ref[0], gather_mask(s)) * chunk
+        source = vec_hbm.at[pl.ds(pl.multiple_of(at, chunk), chunk), :]
+        return pltpu.make_async_copy(source, vec_ref.at[s], vec_sem.at[s])
+
+    for s in range(2 * half):
+        vec_copy(s).start()
+    all_ref[:half] = first_ref[...]
+    all_ref[half:] = second_ref[...]
+
+    def build(s, pts_ref):
+        def put(start, pieces):
+            for h, piece in enumerate(pieces):
+                pts_ref[start + 2 * NV * h : start + 2 * NV * (h + 1), :] = piece
+
+        own = all_ref[s, RSTEPS * BANDS : (RSTEPS + 1) * BANDS, :].astype(jnp.float32)
+        own_v, own_c = own[:NV], own[NV:]
+        for n in range(NOFF):
+            there = all_ref[s, n * BANDS : (n + 1) * BANDS, :].astype(jnp.float32)
+            there_v, there_c = there[:NV], there[NV:]
+            put(n * step, outer_rows(own_c, there_c))
+            put(n * step + PAIRS, outer_rows(there_v, own_v))
+            put(n * step + 2 * PAIRS, outer_rows(there_v, there_c))
+        put(NOFF * step, outer_rows(own_c, own_v))
+
+    def multiply(s, pts_ref):
+        acc_ref[...] += jnp.dot(pts_ref[...], vec_ref[s], preferred_element_type=jnp.float32)
+
+    build(0, even_ref)
     acc_ref[...] = jnp.zeros_like(acc_ref)
-    lax.fori_loop(0, half, add_chunk(first_ref, 0), 0)
-    lax.fori_loop(0, half, add_chunk(second_ref, half), 0)
+
+    def two_chunks(i, carry):
+        s = 2 * i
+        vec_copy(s).wait()
+        build(s + 1, odd_ref)
+        multiply(s, even_ref)
+        vec_copy(s + 1).wait()
+        build(jnp.minimum(s + 2, 2 * half - 1), even_ref)
+        multiply(s + 1, odd_ref)
+        return carry
+
+    lax.fori_loop(0, half, two_chunks, 0)
     own_x = acc_ref[NOFF * step :, :].astype(jnp.bfloat16).astype(jnp.float32)
     weighted = (own_x * bare_ref[...]).astype(jnp.bfloat16)
     for i in range(NOFF):
@@ -306,16 +336,20 @@
             jax.ShapeDtypeStruct((NOFF * NV, columns), jnp.float32),
             jax.ShapeDtypeStruct((columns, columns), jnp.bfloat16),
         ),
-        in_specs=[SMEM] + [VMEM] * 4,
+        in_specs=[SMEM, VMEM, VMEM, pl.BlockSpec(memory_space=pl.ANY), VMEM],
         out_specs=(VMEM,) * 4,
         scratch_shapes=[
+            pltpu.VMEM((2 * first.shape[0], *first.shape[1:]), jnp.bfloat16),
+            pltpu.VMEM((total, first.shape[2]), jnp.bfloat16),
             pltpu.VMEM((total, first.shape[2]), jnp.bfloat16),
             pltpu.VMEM((total, ng), jnp.float32),
+            pltpu.VMEM((2 * first.shape[0], first.shape[2], ng), jnp.bfloat16),
+            pltpu.SemaphoreType.DMA((2 * first.shape[0],)),
         ],
         cost_estimate=pl.CostEstimate(
             flops=flops, bytes_accessed=6 * 1024 * 1024, transcendentals=0
         ),
-        compiler_params=pltpu.CompilerParams(vmem_limit_bytes=16 << 20),
+        compiler_params=pltpu.CompilerParams(vmem_limit_bytes=50 << 20),
         name="pair_waves",
     )(part, first, second, interp_vectors, bare)
 
@@ -384,12 +418,13 @@
     coords, edge = edges_of(place, block, blocks)
     grid = swap(coords, "ka", far)
     edge = lax.ppermute(edge, "ka", edge_route(size))
-    window = window_of(place, block, edge)[None]
+    window, table = window_of(place, block, edge, screening)
+    window = window[None]
     swaps = [[(g, g ^ mask) for g in range(parts)] for mask in GATHER_STEPS]
     two = jnp.concatenate([window, lax.ppermute(window, "ga", swaps[0])])
     four = jnp.concatenate([two, lax.ppermute(two, "ga", swaps[1])])
     other = lax.ppermute(four, "ga", swaps[2])
-    picked = pick_rows(place, grid.reshape(size, 2 * LANES), screening)
+    picked = pick_rows(place, grid.reshape(size, 2 * LANES), table)
     arrived = swap(picked.reshape(NEAR, blocks * NOFF, -1), "ka", near)
     summed = near_sum(arrived, blocks)
     rows = swap(summed, "ka", far)
@@ -398,7 +433,7 @@
     )
     partial = final_terms(rows, cond, vale, exch, perm)
     terms = swap(partial, "ga")
-    return result_of(terms)[None, :, None, :]
+    return result_of(terms)
 
 
 def solution(mesh):

time: 110 us -> 105 us (0.955)
  the two profiles are of different devices: /device:TPU:2 before, /device:TPU:16 now
where the time goes in v4:
time: 105 us; the launch traced here: 104 us
  starting transfers between devices  53.1 us (51%)
  waiting for transfers between devices  23 us (22%)
  Pallas kernels  15.5 us (15%)
  blocking collectives  10.9 us (10%)
    all_to_all x4, starting transfers between devices, swap(): lax.all_to_all(tiles, axis, 0, 0, tiled=True, axis_index_groups=groups)  35.3 us
    all_to_all x4, waiting for transfers between devices, swap(): lax.all_to_all(tiles, axis, 0, 0, tiled=True, axis_index_groups=groups)  11.4 us
    all_to_all x1, blocking collectives, swap(): lax.all_to_all(tiles, axis, 0, 0, tiled=True, axis_index_groups=groups)  10.9 us
    pallas_call x1, Pallas kernels, waves_of(): pl.pallas_call(waves_kernel, out_shape=(jax.ShapeDtypeStruct((NOFF * PAIR...  10.1 us
    ppermute x1, starting transfers between devices, per_device(): edge = lax.ppermute(edge, 'ka', edge_route(size))  6.33 us
    ppermute x1, waiting for transfers between devices, per_device(): four = jnp.concatenate([two, lax.ppermute(two, 'ga', swaps[1])])  5.26 us
    ppermute x1, starting transfers between devices, per_device(): two = jnp.concatenate([window, lax.ppermute(window, 'ga', swaps[0])])  4.92 us
    ppermute x1, waiting for transfers between devices, per_device(): two = jnp.concatenate([window, lax.ppermute(window, 'ga', swaps[0])])  3.63 us
  transfers between devices with their start and end apart: 8, of which 6 were waited for; matrix products, arithmetic and copies ran while one was open for 0% of the time, Pallas kernels for 10%

profile of v4, /device:TPU:16, one launch (start us, length us, event | category | flops | bytes accessed | tf_op | source)
XLA Modules:
  0.0 104.2 jit_solution(15181019203746448394)
XLA Ops:
  0.7 1.4 %message.1 = bf16[8,24,512]{2,1,0:T(8,128)(2,1)} custom-call(s32[1]{0:T(128)S(6)} %copy.6.point_ref, bf16[16,512]{1,0:T(8,128)(2,1)} %bitcast.12), custom_call_target="tpu_custom_call" | custom-call | tf_op jit(solution)/shard_map/message/pallas_call | solution.py:53
  2.1 0.0 copy-start.1
  2.1 9.0 %all-to-all-start = ((bf16[8,24,512]{2,1,0:T(8,128)(2,1)}), bf16[8,24,512]{2,1,0:T(8,128)(2,1)S(1)}, u32[]{:S(2)}, u32[]{:S(2)}) async-start(bf16[8,24,512]{2,1,0:T(8,128)(2,1)} %message.1), calls=%async_computation | async-start | bytes 393216 | tf_op jit(solution)/shard_map/all_to_all | solution.py:30
  11.1 4.8 %all-to-all-done.block_ref = bf16[8,24,512]{2,1,0:T(8,128)(2,1)S(1)} async-done(((bf16[8,24,512]{2,1,0:T(8,128)(2,1)}), bf16[8,24,512]{2,1,0:T(8,128)(2,1)S(1)}, u32[]{:S(2)}, u32[]{:S(2)}) %all-to-all-start) | async-done | bytes 196640 | tf_op jit(solution)/shard_map/all_to_all | solution.py:30
  15.8 0.6 edges.1
  16.5 11.3 %all-to-all-start.1 = ((bf16[8,8,256]{2,1,0:T(8,128)(2,1)}), bf16[8,8,256]{2,1,0:T(8,128)(2,1)S(1)}, u32[]{:S(2)}, u32[]{:S(2)}) async-start(bf16[8,8,256]{2,1,0:T(8,128)(2,1)} %get-tuple-element.13), calls=%async_computation.1 | async-start | bytes 65536 | tf_op jit(solution)/shard_map/all_to_all | solution.py:30
  27.8 6.3 %collective-permute-start = (bf16[48,512]{1,0:T(8,128)(2,1)S(1)}, bf16[48,512]{1,0:T(8,128)(2,1)S(1)}, u32[]{:S(2)}, u32[]{:S(2)}) collective-permute-start(bf16[48,512]{1,0:T(8,128)(2,1)S(1)} %get-tuple-element.14), channel_id=1, source_target_pairs={{0,504},{8,496},{16,488},{40,80},{48,72},{56,64},{64,56},{72,48},{... | collective-permute-start | bytes 147464 | tf_op jit(solution)/shard_map/ppermute | solution.py:420
  34.1 2.7 %collective-permute-done.edge_ref = bf16[48,512]{1,0:T(8,128)(2,1)S(1)} collective-permute-done((bf16[48,512]{1,0:T(8,128)(2,1)S(1)}, bf16[48,512]{1,0:T(8,128)(2,1)S(1)}, u32[]{:S(2)}, u32[]{:S(2)}) %collective-permute-start) | collective-permute-done | bytes 49184 | tf_op jit(solution)/shard_map/ppermute | solution.py:420
  36.8 0.0 copy-start
  36.8 0.9 copy-done
  37.7 0.1 window.1
  37.8 2.9 %all-to-all-done.1 = bf16[8,8,256]{2,1,0:T(8,128)(2,1)S(1)} async-done(((bf16[8,8,256]{2,1,0:T(8,128)(2,1)}), bf16[8,8,256]{2,1,0:T(8,128)(2,1)S(1)}, u32[]{:S(2)}, u32[]{:S(2)}) %all-to-all-start.1) | async-done | bytes 32800 | tf_op jit(solution)/shard_map/all_to_all | solution.py:30
  40.7 1.3 %pick_rows.1 = bf16[448,512]{1,0:T(8,128)(2,1)} custom-call(s32[1]{0:T(128)} %bitcast.place_ref, bf16[64,256]{1,0:T(8,128)(2,1)S(1)} %bitcast.10, bf16[144,512]{1,0:T(8,128)(2,1)S(1)} %get-tuple-element.15.table_ref), custom_call_target="tpu_custom_call" | custom-call | tf_op jit(solution)/shard_map/pick_rows/pallas_call | solution.py:208
  42.0 5.8 %all-to-all-start.2 = ((bf16[8,56,512]{2,1,0:T(8,128)(2,1)}), bf16[8,56,512]{2,1,0:T(8,128)(2,1)S(1)}, u32[]{:S(2)}, u32[]{:S(2)}) async-start(bf16[8,56,512]{2,1,0:T(8,128)(2,1)} %bitcast.3), calls=%async_computation.2 | async-start | bytes 917504 | tf_op jit(solution)/shard_map/all_to_all | solution.py:30
  47.8 4.9 %collective-permute-start.1 = (bf16[1,112,512]{2,1,0:T(8,128)(2,1)S(1)}, bf16[1,112,512]{2,1,0:T(8,128)(2,1)S(1)}, u32[]{:S(2)}, u32[]{:S(2)}) collective-permute-start(bf16[1,112,512]{2,1,0:T(8,128)(2,1)S(1)} %bitcast.7), channel_id=1, source_target_pairs={{0,2},{1,3},{2,0},{3,1},{4,6},{5,7},{6,4},{7,5},{8,10},{9,11},{10,... | collective-permute-start | bytes 344072 | tf_op jit(solution)/shard_map/ppermute | solution.py:424
  52.7 3.6 %collective-permute-done.1 = bf16[1,112,512]{2,1,0:T(8,128)(2,1)S(1)} collective-permute-done((bf16[1,112,512]{2,1,0:T(8,128)(2,1)S(1)}, bf16[1,112,512]{2,1,0:T(8,128)(2,1)S(1)}, u32[]{:S(2)}, u32[]{:S(2)}) %collective-permute-start.1) | collective-permute-done | bytes 114720 | tf_op jit(solution)/shard_map/ppermute | solution.py:424
  56.4 3.4 %collective-permute-start.2 = (bf16[2,112,512]{2,1,0:T(8,128)(2,1)S(1)}, bf16[2,112,512]{2,1,0:T(8,128)(2,1)S(1)}, u32[]{:S(2)}, u32[]{:S(2)}) collective-permute-start(bf16[2,112,512]{2,1,0:T(8,128)(2,1)S(1)} %pad_maximum_fusion.1), channel_id=1, source_target_pairs={{0,1},{1,0},{2,3},{3,2},{4,5},{5,4},{6,7},{7,6},{8,9},{9,8},{10,11... | collective-permute-start | bytes 688136 | tf_op jit(solution)/shard_map/ppermute | solution.py:425
  59.8 5.3 %collective-permute-done.2 = bf16[2,112,512]{2,1,0:T(8,128)(2,1)S(1)} collective-permute-done((bf16[2,112,512]{2,1,0:T(8,128)(2,1)S(1)}, bf16[2,112,512]{2,1,0:T(8,128)(2,1)S(1)}, u32[]{:S(2)}, u32[]{:S(2)}) %collective-permute-start.2) | collective-permute-done | bytes 229408 | tf_op jit(solution)/shard_map/ppermute | solution.py:425
  65.1 3.2 %collective-permute-start.3 = (bf16[4,112,512]{2,1,0:T(8,128)(2,1)S(1)}, bf16[4,112,512]{2,1,0:T(8,128)(2,1)S(1)}, u32[]{:S(2)}, u32[]{:S(2)}) collective-permute-start(bf16[4,112,512]{2,1,0:T(8,128)(2,1)S(1)} %pad_maximum_fusion.first_ref), channel_id=1, source_target_pairs={{0,4},{1,5},{2,6},{3,7},{4,0},{5,1},{6,2},{7,3},{8,12},{9,13},{10,... | collective-permute-start | bytes 1376264 | tf_op jit(solution)/shard_map/ppermute | solution.py:426
  68.3 0.0 all-to-all-done.2.rows_ref
  68.3 0.7 near_sum.1
  69.0 9.1 %all-to-all-start.3 = ((bf16[8,7,512]{2,1,0:T(8,128)(2,1)}), bf16[8,7,512]{2,1,0:T(8,128)(2,1)S(1)}, u32[]{:S(2)}, u32[]{:S(2)}) async-start(bf16[8,7,512]{2,1,0:T(8,128)(2,1)} %near_sum.1), calls=%async_computation.3 | async-start | bytes 131072 | tf_op jit(solution)/shard_map/all_to_all | solution.py:30
  78.1 0.0 collective-permute-done.3.second_ref
  78.2 0.0 copy-done.1
  78.2 10.1 %pair_waves.1 = (bf16[448,512]{1,0:T(8,128)(2,1)S(1)}, bf16[448,512]{1,0:T(8,128)(2,1)S(1)}, f32[56,512]{1,0:T(8,128)S(1)}, bf16[512,512]{1,0:T(8,128)(2,1)S(1)}) custom-call(s32[1]{0:T(128)} %bitcast.4.part_ref, bf16[4,112,512]{2,1,0:T(8,128)(2,1)S(1)} %pad_maximum_fusion.first_ref, bf16[4,112,512]{2,1,0:T(8,128)(2,1)S(1)} %collective-permute-done.3.second_ref, ...), custom_call_target="tpu_custom_call" | custom-call | flops 5905580032 | bytes 6291456 | tf_op jit(solution)/shard_map/pair_waves/pallas_call | solution.py:331
  88.3 3.7 %all-to-all-done.3.rows_ref = bf16[8,7,512]{2,1,0:T(8,128)(2,1)S(1)} async-done(((bf16[8,7,512]{2,1,0:T(8,128)(2,1)}), bf16[8,7,512]{2,1,0:T(8,128)(2,1)S(1)}, u32[]{:S(2)}, u32[]{:S(2)}) %all-to-all-start.3) | async-done | bytes 57376 | tf_op jit(solution)/shard_map/all_to_all | solution.py:30
  92.0 0.7 final_terms.1
  92.7 10.9 %all_to_all.25.terms_ref = f32[8,7,512]{2,1,0:T(8,128)S(1)} all-to-all(f32[8,7,512]{2,1,0:T(8,128)S(1)} %final_terms.1), channel_id=1, replica_groups=mesh['ka'=64,'ga'=8] {'ga'}, dimensions={0} | all-to-all | bytes 229376 | tf_op jit(solution)/shard_map/all_to_all | solution.py:30
  103.6 0.6 result.1
  (2 shorter events, 0.1 us)
Async XLA Ops:
  2.1 76.1 %copy-start.1 = (f32[512]{0:T(512)S(1)}, f32[512]{0:T(512)}, u32[]{:S(2)}) copy-start(f32[512]{0:T(512)} %param.8) | copy-start | bytes 6148
  2.1 13.8 %all-to-all-start = ((bf16[8,24,512]{2,1,0:T(8,128)(2,1)}), bf16[8,24,512]{2,1,0:T(8,128)(2,1)S(1)}, u32[]{:S(2)}, u32[]{:S(2)}) async-start(bf16[8,24,512]{2,1,0:T(8,128)(2,1)} %message.1), calls=%async_computation | async-start | bytes 393216 | tf_op jit(solution)/shard_map/all_to_all | solution.py:30
  16.5 24.3 %all-to-all-start.1 = ((bf16[8,8,256]{2,1,0:T(8,128)(2,1)}), bf16[8,8,256]{2,1,0:T(8,128)(2,1)S(1)}, u32[]{:S(2)}, u32[]{:S(2)}) async-start(bf16[8,8,256]{2,1,0:T(8,128)(2,1)} %get-tuple-element.13), calls=%async_computation.1 | async-start | bytes 65536 | tf_op jit(solution)/shard_map/all_to_all | solution.py:30
  27.8 9.0 %collective-permute-start = (bf16[48,512]{1,0:T(8,128)(2,1)S(1)}, bf16[48,512]{1,0:T(8,128)(2,1)S(1)}, u32[]{:S(2)}, u32[]{:S(2)}) collective-permute-start(bf16[48,512]{1,0:T(8,128)(2,1)S(1)} %get-tuple-element.14), channel_id=1, source_target_pairs={{0,504},{8,496},{16,488},{40,80},{48,72},{56,64},{64,56},{72,48},{... | collective-permute-start | bytes 147464 | tf_op jit(solution)/shard_map/ppermute | solution.py:420
  36.8 0.9 copy-start
  42.0 26.3 %all-to-all-start.2 = ((bf16[8,56,512]{2,1,0:T(8,128)(2,1)}), bf16[8,56,512]{2,1,0:T(8,128)(2,1)S(1)}, u32[]{:S(2)}, u32[]{:S(2)}) async-start(bf16[8,56,512]{2,1,0:T(8,128)(2,1)} %bitcast.3), calls=%async_computation.2 | async-start | bytes 917504 | tf_op jit(solution)/shard_map/all_to_all | solution.py:30
  47.8 8.6 %collective-permute-start.1 = (bf16[1,112,512]{2,1,0:T(8,128)(2,1)S(1)}, bf16[1,112,512]{2,1,0:T(8,128)(2,1)S(1)}, u32[]{:S(2)}, u32[]{:S(2)}) collective-permute-start(bf16[1,112,512]{2,1,0:T(8,128)(2,1)S(1)} %bitcast.7), channel_id=1, source_target_pairs={{0,2},{1,3},{2,0},{3,1},{4,6},{5,7},{6,4},{7,5},{8,10},{9,11},{10,... | collective-permute-start | bytes 344072 | tf_op jit(solution)/shard_map/ppermute | solution.py:424
  56.4 8.7 %collective-permute-start.2 = (bf16[2,112,512]{2,1,0:T(8,128)(2,1)S(1)}, bf16[2,112,512]{2,1,0:T(8,128)(2,1)S(1)}, u32[]{:S(2)}, u32[]{:S(2)}) collective-permute-start(bf16[2,112,512]{2,1,0:T(8,128)(2,1)S(1)} %pad_maximum_fusion.1), channel_id=1, source_target_pairs={{0,1},{1,0},{2,3},{3,2},{4,5},{5,4},{6,7},{7,6},{8,9},{9,8},{10,11... | collective-permute-start | bytes 688136 | tf_op jit(solution)/shard_map/ppermute | solution.py:425
  65.1 13.0 %collective-permute-start.3 = (bf16[4,112,512]{2,1,0:T(8,128)(2,1)S(1)}, bf16[4,112,512]{2,1,0:T(8,128)(2,1)S(1)}, u32[]{:S(2)}, u32[]{:S(2)}) collective-permute-start(bf16[4,112,512]{2,1,0:T(8,128)(2,1)S(1)} %pad_maximum_fusion.first_ref), channel_id=1, source_target_pairs={{0,4},{1,5},{2,6},{3,7},{4,0},{5,1},{6,2},{7,3},{8,12},{9,13},{10,... | collective-permute-start | bytes 1376264 | tf_op jit(solution)/shard_map/ppermute | solution.py:426
  69.0 23.0 %all-to-all-start.3 = ((bf16[8,7,512]{2,1,0:T(8,128)(2,1)}), bf16[8,7,512]{2,1,0:T(8,128)(2,1)S(1)}, u32[]{:S(2)}, u32[]{:S(2)}) async-start(bf16[8,7,512]{2,1,0:T(8,128)(2,1)} %near_sum.1), calls=%async_computation.3 | async-start | bytes 131072 | tf_op jit(solution)/shard_map/all_to_all | solution.py:30

commit v5 on v3

--- a/solution.py
+++ b/solution.py
@@ -22,8 +22,8 @@
     return [[start + j for j in range(NEAR)] for start in range(0, size, NEAR)]
 
 
-def far_groups(size):
-    return [[j + start for start in range(0, size, NEAR)] for j in range(NEAR)]
+def far_groups(size, step):
+    return [[j + start for start in range(0, size, step)] for j in range(step)]
 
 
 def swap(tiles, axis, groups=None):
@@ -34,24 +34,29 @@
 SMEM = pl.BlockSpec(memory_space=pltpu.SMEM)
 
 
-def message_kernel(point_ref, own_ref, out_ref):
+def message_kernel(point_ref, own_hbm, out_ref, own_ref, own_sem):
+    own_copy = pltpu.make_async_copy(own_hbm, own_ref, own_sem)
+    own_copy.start()
     chunk = own_ref.shape[1]
     row = point_ref[0] // NKX
     col = point_ref[0] - row * NKX
     lane = lax.broadcasted_iota(jnp.int32, (NEAR, chunk), 1)
     coords = jnp.where(lane < LANES, row, col).astype(jnp.float32).astype(jnp.bfloat16)
     for j in range(out_ref.shape[0]):
+        out_ref[j, BANDS:, :] = coords
+    own_copy.wait()
+    for j in range(out_ref.shape[0]):
         out_ref[j, :BANDS, :] = own_ref[...]
-        out_ref[j, BANDS:, :] = coords
 
 
 def message_of(points, own):
     return pl.pallas_call(
         message_kernel,
         out_shape=jax.ShapeDtypeStruct((NEAR, BANDS + NEAR, own.shape[1]), own.dtype),
-        in_specs=[SMEM, VMEM],
-        out_specs=VMEM,
-        compiler_params=pltpu.CompilerParams(vmem_limit_bytes=2 << 20),
+        in_specs=[SMEM, pl.BlockSpec(memory_space=pl.ANY)],
+        out_specs=VMEM,
+        scratch_shapes=[pltpu.VMEM(own.shape, own.dtype), pltpu.SemaphoreType.DMA],
+        compiler_params=pltpu.CompilerParams(vmem_limit_bytes=67043328),
         name="message",
     )(points, own)
 
@@ -124,36 +129,17 @@
     )(place, block, edge)
 
 
-def near_sum_kernel(rows_ref, out_ref):
-    total = rows_ref[0].astype(jnp.float32)
-    for b in range(1, rows_ref.shape[0]):
-        total = total + rows_ref[b].astype(jnp.float32)
-    for b in range(out_ref.shape[0]):
-        out_ref[b] = total[b * NOFF : (b + 1) * NOFF].astype(out_ref.dtype)
-
-
-def near_sum(rows, blocks):
-    return pl.pallas_call(
-        near_sum_kernel,
-        out_shape=jax.ShapeDtypeStruct((blocks, NOFF, rows.shape[2]), rows.dtype),
-        in_specs=[VMEM],
-        out_specs=VMEM,
-        compiler_params=pltpu.CompilerParams(vmem_limit_bytes=4 << 20),
-        name="near_sum",
-    )(rows)
-
-
 def result_kernel(terms_ref, out_ref):
     total = terms_ref[0]
     for g in range(1, terms_ref.shape[0]):
         total = total + terms_ref[g]
-    out_ref[...] = total * NG ** (-0.5)
+    out_ref[0, :, 0, :] = total * NG ** (-0.5)
 
 
 def result_of(terms):
     return pl.pallas_call(
         result_kernel,
-        out_shape=jax.ShapeDtypeStruct(terms.shape[1:], terms.dtype),
+        out_shape=jax.ShapeDtypeStruct((1, NOFF, 1, terms.shape[2]), terms.dtype),
         in_specs=[VMEM],
         out_specs=VMEM,
         compiler_params=pltpu.CompilerParams(vmem_limit_bytes=2 << 20),
@@ -161,49 +147,67 @@
     )(terms)
 
 
-def pick_kernel(place_ref, grid_ref, table_ref, out_ref, local_ref, hot_ref):
+def table_mask(s):
+    first, second = TABLE_STEPS
+    return (s & 1) * first + ((s >> 1) & 1) * second
+
+
+def pick_kernel(place_ref, grid_ref, table_ref, out_ref, column_ref, hot_ref):
     size = grid_ref.shape[0]
-    blocks = size // NEAR
-    table_rows = table_ref.shape[0]
+    pieces, table_rows, _ = table_ref.shape
+    askers = size // pieces
     row = grid_ref[:, :LANES].astype(jnp.float32)
     col = grid_ref[:, LANES:].astype(jnp.float32)
-    base = (place_ref[0] * table_rows).astype(jnp.float32)
     for i in range(NOFF):
         d = i - RSTEPS
         row_step = row - jnp.roll(row, d, axis=0) if d else jnp.zeros_like(row)
         col_step = col - jnp.roll(col, d, axis=0) if d else jnp.zeros_like(col)
         row_step = jnp.where(row_step < 0, row_step + NKX, row_step)
         col_step = jnp.where(col_step < 0, col_step + NKX, col_step)
-        local_ref[i * size : (i + 1) * size, :] = row_step * NKX + col_step - base
-    lane = lax.broadcasted_iota(jnp.int32, (blocks, LANES), 1).astype(jnp.float32)
-    for j in range(NEAR):
-        for i in range(NOFF):
-            local = local_ref[pl.ds(i * size + j, blocks, stride=NEAR), :]
-            rows = pl.ds(j * blocks * NOFF + i, blocks, stride=NOFF)
-            for part in range(hot_ref.shape[0]):
-                hot_ref[part, rows, :] = jnp.where(local == lane + part * LANES, 1.0, 0.0)
+        momentum = row_step * NKX + col_step
+        column = jnp.full_like(momentum, -1.0)
+        for s in range(pieces):
+            base = (jnp.bitwise_xor(place_ref[0], table_mask(s)) * table_rows).astype(jnp.float32)
+            local = momentum - base
+            inside = jnp.logical_and(local >= 0, local < table_rows)
+            column = jnp.where(inside, local + s * table_rows, column)
+        column_ref[i * size : (i + 1) * size, :] = column
+    lane = lax.broadcasted_iota(jnp.int32, (askers, LANES), 1).astype(jnp.float32)
+    inner = lax.rem(place_ref[0], pieces)
+    for i in range(NOFF):
+        column = column_ref[pl.ds(i * size + inner, askers, stride=pieces), :]
+        for part in range(hot_ref.shape[0]):
+            hot_ref[part, pl.ds(i, askers, stride=NOFF), :] = jnp.where(
+                column == lane + part * LANES, 1.0, 0.0
+            )
+    table = table_ref[...].reshape(pieces * table_rows, -1)
     total = None
     for part in range(hot_ref.shape[0]):
-        count = min(LANES, table_rows - part * LANES)
+        count = min(LANES, table.shape[0] - part * LANES)
         term = jnp.dot(
             hot_ref[part, :, :count].astype(jnp.bfloat16),
-            table_ref[part * LANES : part * LANES + count, :],
+            table[part * LANES : part * LANES + count, :],
             preferred_element_type=jnp.float32,
         )
         total = term if total is None else total + term
-    out_ref[...] = total.astype(jnp.bfloat16)
+    for a in range(askers):
+        out_ref[a] = total[a * NOFF : (a + 1) * NOFF].astype(jnp.bfloat16)
 
 
 def pick_rows(place, grid, table):
     size = grid.shape[0]
+    pieces, table_rows, width = table.shape
+    askers = size // pieces
     return pl.pallas_call(
         pick_kernel,
-        out_shape=jax.ShapeDtypeStruct((size * NOFF, table.shape[1]), jnp.bfloat16),
+        out_shape=jax.ShapeDtypeStruct((askers, NOFF, width), jnp.bfloat16),
         in_specs=[SMEM, VMEM, VMEM],
         out_specs=VMEM,
         scratch_shapes=[
             pltpu.VMEM((NOFF * size, LANES), jnp.float32),
-            pltpu.VMEM((pl.cdiv(table.shape[0], LANES), size * NOFF, LANES), jnp.float32),
+            pltpu.VMEM(
+                (pl.cdiv(pieces * table_rows, LANES), askers * NOFF, LANES), jnp.float32
+            ),
         ],
         compiler_params=pltpu.CompilerParams(vmem_limit_bytes=6 << 20),
         name="pick_rows",
@@ -220,7 +224,10 @@
     return rows
 
 
-GATHER_STEPS = (2, 1, 4)
+GATHER_STEPS = (4, 2, 1)
+TABLE_STEPS = (1, 2)
+FIRST_LIMIT = 50
+SECOND_LIMIT = 47
 
 
 def gather_mask(s):
@@ -228,48 +235,65 @@
     return (s & 1) * first + ((s >> 1) & 1) * second + ((s >> 2) & 1) * third
 
 
+def pair_products(
+    part_ref, source_ref, vec_hbm, pts_ref, vec_ref, vec_sem, first
+):
+    count, _, chunk = source_ref.shape
+    step = 3 * PAIRS
+
+    def vec_copy(s):
+        at = jnp.bitwise_xor(part_ref[0], gather_mask(first + s)) * chunk
+        source = vec_hbm.at[pl.ds(pl.multiple_of(at, chunk), chunk), :]
+        return pltpu.make_async_copy(
+            source, vec_ref.at[s * chunk : (s + 1) * chunk, :], vec_sem.at[s]
+        )
+
+    for s in range(count):
+        vec_copy(s).start()
+    for s in range(count):
+
+        def put(start, pieces):
+            for h, piece in enumerate(pieces):
+                rows = slice(start + 2 * NV * h, start + 2 * NV * (h + 1))
+                pts_ref[rows, s * chunk : (s + 1) * chunk] = piece
+
+        own = source_ref[s, RSTEPS * BANDS : (RSTEPS + 1) * BANDS, :].astype(jnp.float32)
+        own_v, own_c = own[:NV], own[NV:]
+        for n in range(NOFF):
+            there = source_ref[s, n * BANDS : (n + 1) * BANDS, :].astype(jnp.float32)
+            there_v, there_c = there[:NV], there[NV:]
+            put(n * step, outer_rows(own_c, there_c))
+            put(n * step + PAIRS, outer_rows(there_v, own_v))
+            put(n * step + 2 * PAIRS, outer_rows(there_v, there_c))
+        put(NOFF * step, outer_rows(own_c, own_v))
+    for s in range(count):
+        vec_copy(s).wait()
+    return jnp.dot(pts_ref[...], vec_ref[...], preferred_element_type=jnp.float32)
+
+
+def first_waves_kernel(part_ref, source_ref, vec_hbm, acc_ref, pts_ref, vec_ref, vec_sem):
+    acc_ref[...] = pair_products(part_ref, source_ref, vec_hbm, pts_ref, vec_ref, vec_sem, 0)
+
+
 def waves_kernel(
     part_ref,
-    first_ref,
-    second_ref,
-    vec_ref,
+    source_ref,
+    vec_hbm,
     bare_ref,
+    begun_ref,
     cond_ref,
     vale_ref,
     exch_ref,
     perm_ref,
     pts_ref,
+    vec_ref,
+    vec_sem,
     acc_ref,
 ):
-    half = first_ref.shape[0]
-    chunk = first_ref.shape[2]
     step = 3 * PAIRS
-
-    def put(start, pieces):
-        for h, piece in enumerate(pieces):
-            pts_ref[start + 2 * NV * h : start + 2 * NV * (h + 1), :] = piece
-
-    def add_chunk(source_ref, offset):
-        def add(s, carry):
-            own = source_ref[s, RSTEPS * BANDS : (RSTEPS + 1) * BANDS, :].astype(jnp.float32)
-            own_v, own_c = own[:NV], own[NV:]
-            for n in range(NOFF):
-                there = source_ref[s, n * BANDS : (n + 1) * BANDS, :].astype(jnp.float32)
-                there_v, there_c = there[:NV], there[NV:]
-                put(n * step, outer_rows(own_c, there_c))
-                put(n * step + PAIRS, outer_rows(there_v, own_v))
-                put(n * step + 2 * PAIRS, outer_rows(there_v, there_c))
-            put(NOFF * step, outer_rows(own_c, own_v))
-            at = jnp.bitwise_xor(part_ref[0], gather_mask(s + offset))
-            vec = vec_ref[pl.ds(pl.multiple_of(at * chunk, chunk), chunk), :]
-            acc_ref[...] += jnp.dot(pts_ref[...], vec, preferred_element_type=jnp.float32)
-            return carry
-
-        return add
-
-    acc_ref[...] = jnp.zeros_like(acc_ref)
-    lax.fori_loop(0, half, add_chunk(first_ref, 0), 0)
-    lax.fori_loop(0, half, add_chunk(second_ref, half), 0)
+    acc_ref[...] = begun_ref[...] + pair_products(
+        part_ref, source_ref, vec_hbm, pts_ref, vec_ref, vec_sem, source_ref.shape[0]
+    )
     own_x = acc_ref[NOFF * step :, :].astype(jnp.bfloat16).astype(jnp.float32)
     weighted = (own_x * bare_ref[...]).astype(jnp.bfloat16)
     for i in range(NOFF):
@@ -293,10 +317,39 @@
     perm_ref[...] = jnp.where(moved == target, 1.0, 0.0).astype(jnp.bfloat16)
 
 
-def waves_of(part, first, second, interp_vectors, bare):
+def waves_scratch(source, ng):
+    count, _, chunk = source.shape
+    total = NOFF * 3 * PAIRS + PAIRS
+    return [
+        pltpu.VMEM((total, count * chunk), jnp.bfloat16),
+        pltpu.VMEM((count * chunk, ng), jnp.bfloat16),
+        pltpu.SemaphoreType.DMA((count,)),
+    ]
+
+
+def waves_cost(source, ng):
+    total = NOFF * 3 * PAIRS + PAIRS
+    flops = 2 * total * source.shape[0] * source.shape[2] * ng
+    return pl.CostEstimate(flops=flops, bytes_accessed=6 * 1024 * 1024, transcendentals=0)
+
+
+def first_waves_of(part, source, interp_vectors):
     ng = interp_vectors.shape[1]
     total = NOFF * 3 * PAIRS + PAIRS
-    flops = 2 * total * interp_vectors.shape[0] * ng
+    return pl.pallas_call(
+        first_waves_kernel,
+        out_shape=jax.ShapeDtypeStruct((total, ng), jnp.float32),
+        in_specs=[SMEM, VMEM, pl.BlockSpec(memory_space=pl.ANY)],
+        out_specs=VMEM,
+        scratch_shapes=waves_scratch(source, ng),
+        compiler_params=pltpu.CompilerParams(vmem_limit_bytes=FIRST_LIMIT << 20),
+        cost_estimate=waves_cost(source, ng),
+        name="first_waves",
+    )(part, source, interp_vectors)
+
+
+def waves_of(part, source, interp_vectors, bare, begun):
+    ng = interp_vectors.shape[1]
     columns = NC * NV * NC
     return pl.pallas_call(
         waves_kernel,
@@ -306,18 +359,13 @@
             jax.ShapeDtypeStruct((NOFF * NV, columns), jnp.float32),
             jax.ShapeDtypeStruct((columns, columns), jnp.bfloat16),
         ),
-        in_specs=[SMEM] + [VMEM] * 4,
+        in_specs=[SMEM, VMEM, pl.BlockSpec(memory_space=pl.ANY), VMEM, VMEM],
         out_specs=(VMEM,) * 4,
-        scratch_shapes=[
-            pltpu.VMEM((total, first.shape[2]), jnp.bfloat16),
-            pltpu.VMEM((total, ng), jnp.float32),
-        ],
-        cost_estimate=pl.CostEstimate(
-            flops=flops, bytes_accessed=6 * 1024 * 1024, transcendentals=0
-        ),
-        compiler_params=pltpu.CompilerParams(vmem_limit_bytes=16 << 20),
+        scratch_shapes=waves_scratch(source, ng) + [pltpu.VMEM(begun.shape, begun.dtype)],
+        compiler_params=pltpu.CompilerParams(vmem_limit_bytes=SECOND_LIMIT << 20),
+        cost_estimate=waves_cost(source, ng),
         name="pair_waves",
-    )(part, first, second, interp_vectors, bare)
+    )(part, source, interp_vectors, bare, begun)
 
 
 def final_kernel(rows_ref, cond_ref, vale_ref, exch_ref, perm_ref, out_ref, all_ref, parts_ref):
@@ -378,27 +426,29 @@
     place = lax.axis_index("ka").astype(jnp.int32).reshape(1)
     part = lax.axis_index("ga").astype(jnp.int32).reshape(1)
     near = near_groups(size)
-    far = far_groups(size)
+    turns = [[(k, k ^ mask) for k in range(size)] for mask in TABLE_STEPS]
+    swaps = [[(g, g ^ mask) for g in range(parts)] for mask in GATHER_STEPS]
     message = message_of(slab_kpoints, orbitals[0])
     block = swap(message, "ka", near)
+    table = screening[None]
+    table = jnp.concatenate([table, lax.ppermute(table, "ka", turns[0])])
+    table = jnp.concatenate([table, lax.ppermute(table, "ka", turns[1])])
     coords, edge = edges_of(place, block, blocks)
-    grid = swap(coords, "ka", far)
+    grid = swap(coords, "ka", far_groups(size, NEAR))
     edge = lax.ppermute(edge, "ka", edge_route(size))
     window = window_of(place, block, edge)[None]
-    swaps = [[(g, g ^ mask) for g in range(parts)] for mask in GATHER_STEPS]
     two = jnp.concatenate([window, lax.ppermute(window, "ga", swaps[0])])
     four = jnp.concatenate([two, lax.ppermute(two, "ga", swaps[1])])
     other = lax.ppermute(four, "ga", swaps[2])
-    picked = pick_rows(place, grid.reshape(size, 2 * LANES), screening)
-    arrived = swap(picked.reshape(NEAR, blocks * NOFF, -1), "ka", near)
-    summed = near_sum(arrived, blocks)
-    rows = swap(summed, "ka", far)
+    picked = pick_rows(place, grid.reshape(size, 2 * LANES), table)
+    rows = swap(picked, "ka", far_groups(size, table.shape[0]))
+    begun = first_waves_of(part, four, interp_vectors)
     cond, vale, exch, perm = waves_of(
-        part, four, other, interp_vectors, bare_coulomb[None]
+        part, other, interp_vectors, bare_coulomb[None], begun
     )
     partial = final_terms(rows, cond, vale, exch, perm)
     terms = swap(partial, "ga")
-    return result_of(terms)[None, :, None, :]
+    return result_of(terms)
 
 
 def solution(mesh):

time: 110 us -> 102 us (0.927)
  the two profiles are of different devices: /device:TPU:2 before, /device:TPU:32 now
where the time goes in v5:
time: 102 us; the launch traced here: 101 us
  starting transfers between devices  51.4 us (50%)
  waiting for transfers between devices  22.1 us (22%)
  Pallas kernels  14.7 us (14%)
  blocking collectives  10.3 us (10%)
  other arithmetic  1.98 us (2%)
    all_to_all x3, starting transfers between devices, swap(): lax.all_to_all(tiles, axis, 0, 0, tiled=True, axis_index_groups=groups)  29.1 us
    all_to_all x3, waiting for transfers between devices, swap(): lax.all_to_all(tiles, axis, 0, 0, tiled=True, axis_index_groups=groups)  20.9 us
    all_to_all x1, blocking collectives, swap(): lax.all_to_all(tiles, axis, 0, 0, tiled=True, axis_index_groups=groups)  10.3 us
    ppermute x1, starting transfers between devices, per_device(): table = jnp.concatenate([table, lax.ppermute(table, 'ka', turns[0])])  8.78 us
    ppermute x1, starting transfers between devices, per_device(): table = jnp.concatenate([table, lax.ppermute(table, 'ka', turns[1])])  6.55 us
    pallas_call x1, Pallas kernels, waves_of(): pl.pallas_call(waves_kernel, out_shape=(jax.ShapeDtypeStruct((NOFF * PAIR...  5.28 us
    pallas_call x1, Pallas kernels, first_waves_of(): pl.pallas_call(first_waves_kernel, out_shape=jax.ShapeDtypeStruct((total,...  4.71 us
    ppermute x1, starting transfers between devices, per_device(): four = jnp.concatenate([two, lax.ppermute(two, 'ga', swaps[1])])  2.43 us
  transfers between devices with their start and end apart: 9, of which 4 were waited for; matrix products, arithmetic and copies ran while one was open for 2% of the time, Pallas kernels for 11%

profile of v5, /device:TPU:32, one launch (start us, length us, event | category | flops | bytes accessed | tf_op | source)
XLA Modules:
  0.0 101.3 jit_solution(10468329376540260537)
XLA Ops:
  0.7 1.4 %message.1 = bf16[8,24,512]{2,1,0:T(8,128)(2,1)} custom-call(s32[1]{0:T(128)S(6)} %copy.6.point_ref, bf16[16,512]{1,0:T(8,128)(2,1)} %bitcast.15), custom_call_target="tpu_custom_call" | custom-call | tf_op jit(solution)/shard_map/message/pallas_call | solution.py:53
  2.1 8.8 %all-to-all-start = ((bf16[8,24,512]{2,1,0:T(8,128)(2,1)}), bf16[8,24,512]{2,1,0:T(8,128)(2,1)S(1)}, u32[]{:S(2)}, u32[]{:S(2)}) async-start(bf16[8,24,512]{2,1,0:T(8,128)(2,1)} %message.1), calls=%async_computation | async-start | bytes 393216 | tf_op jit(solution)/shard_map/all_to_all | solution.py:30
  10.9 6.3 %all-to-all-done.block_ref = bf16[8,24,512]{2,1,0:T(8,128)(2,1)S(1)} async-done(((bf16[8,24,512]{2,1,0:T(8,128)(2,1)}), bf16[8,24,512]{2,1,0:T(8,128)(2,1)S(1)}, u32[]{:S(2)}, u32[]{:S(2)}) %all-to-all-start) | async-done | bytes 196640 | tf_op jit(solution)/shard_map/all_to_all | solution.py:30
  17.1 0.6 edges.1
  17.7 0.7 collective-permute-start.2
  18.4 0.0 collective-permute-done.2.edge_ref
  18.4 0.1 window.1
  18.5 1.9 %collective-permute-start.3 = (bf16[1,112,512]{2,1,0:T(8,128)(2,1)S(1)}, bf16[1,112,512]{2,1,0:T(8,128)(2,1)S(1)}, u32[]{:S(2)}, u32[]{:S(2)}) collective-permute-start(bf16[1,112,512]{2,1,0:T(8,128)(2,1)S(1)} %bitcast.7), channel_id=1, source_target_pairs={{0,4},{1,5},{2,6},{3,7},{4,0},{5,1},{6,2},{7,3},{8,12},{9,13},{10,... | collective-permute-start | bytes 344072 | tf_op jit(solution)/shard_map/ppermute | solution.py:440
  20.4 8.8 %collective-permute-start = (bf16[1,144,512]{2,1,0:T(8,128)(2,1)}, bf16[1,144,512]{2,1,0:T(8,128)(2,1)S(1)}, u32[]{:S(2)}, u32[]{:S(2)}) collective-permute-start(bf16[1,144,512]{2,1,0:T(8,128)(2,1)} %bitcast.12), channel_id=1, source_target_pairs={{0,8},{8,0},{16,24},{24,16},{32,40},{40,32},{48,56},{56,48},{64,72... | collective-permute-start | bytes 442376 | tf_op jit(solution)/shard_map/ppermute | solution.py:434
  29.2 0.0 collective-permute-done.3
  29.3 2.4 %collective-permute-start.4 = (bf16[2,112,512]{2,1,0:T(8,128)(2,1)S(1)}, bf16[2,112,512]{2,1,0:T(8,128)(2,1)S(1)}, u32[]{:S(2)}, u32[]{:S(2)}) collective-permute-start(bf16[2,112,512]{2,1,0:T(8,128)(2,1)S(1)} %pad_maximum_fusion.3), channel_id=1, source_target_pairs={{0,2},{1,3},{2,0},{3,1},{4,6},{5,7},{6,4},{7,5},{8,10},{9,11},{10,... | collective-permute-start | bytes 688136 | tf_op jit(solution)/shard_map/ppermute | solution.py:441
  31.7 0.0 collective-permute-done
  31.7 0.9 pad_maximum_fusion.2
  32.7 6.6 %collective-permute-start.1 = (bf16[2,144,512]{2,1,0:T(8,128)(2,1)S(1)}, bf16[2,144,512]{2,1,0:T(8,128)(2,1)S(1)}, u32[]{:S(2)}, u32[]{:S(2)}) collective-permute-start(bf16[2,144,512]{2,1,0:T(8,128)(2,1)S(1)} %pad_maximum_fusion.2), channel_id=1, source_target_pairs={{0,16},{8,24},{16,0},{24,8},{32,48},{40,56},{48,32},{56,40},{64,80... | collective-permute-start | bytes 884744 | tf_op jit(solution)/shard_map/ppermute | solution.py:435
  39.2 1.2 %collective-permute-done.4 = bf16[2,112,512]{2,1,0:T(8,128)(2,1)S(1)} collective-permute-done((bf16[2,112,512]{2,1,0:T(8,128)(2,1)S(1)}, bf16[2,112,512]{2,1,0:T(8,128)(2,1)S(1)}, u32[]{:S(2)}, u32[]{:S(2)}) %collective-permute-start.4) | collective-permute-done | bytes 229408 | tf_op jit(solution)/shard_map/ppermute | solution.py:441
  40.5 1.9 %collective-permute-start.5 = (bf16[4,112,512]{2,1,0:T(8,128)(2,1)S(1)}, bf16[4,112,512]{2,1,0:T(8,128)(2,1)S(1)}, u32[]{:S(2)}, u32[]{:S(2)}) collective-permute-start(bf16[4,112,512]{2,1,0:T(8,128)(2,1)S(1)} %pad_maximum_fusion.1.source_ref), channel_id=1, source_target_pairs={{0,1},{1,0},{2,3},{3,2},{4,5},{5,4},{6,7},{7,6},{8,9},{9,8},{10,11... | collective-permute-start | bytes 1376264 | tf_op jit(solution)/shard_map/ppermute | solution.py:442
  42.4 13.9 %all-to-all-start.1 = ((bf16[8,8,256]{2,1,0:T(8,128)(2,1)}), bf16[8,8,256]{2,1,0:T(8,128)(2,1)S(1)}, u32[]{:S(2)}, u32[]{:S(2)}) async-start(bf16[8,8,256]{2,1,0:T(8,128)(2,1)} %get-tuple-element.11), calls=%async_computation.1 | async-start | bytes 65536 | tf_op jit(solution)/shard_map/all_to_all | solution.py:30
  56.3 0.0 collective-permute-done.1
  56.3 1.0 pad_maximum_fusion.table_ref
  57.3 11.9 %all-to-all-done.1 = bf16[8,8,256]{2,1,0:T(8,128)(2,1)S(1)} async-done(((bf16[8,8,256]{2,1,0:T(8,128)(2,1)}), bf16[8,8,256]{2,1,0:T(8,128)(2,1)S(1)}, u32[]{:S(2)}, u32[]{:S(2)}) %all-to-all-start.1) | async-done | bytes 32800 | tf_op jit(solution)/shard_map/all_to_all | solution.py:30
  69.2 1.2 %pick_rows.1 = bf16[16,7,512]{2,1,0:T(8,128)(2,1)} custom-call(s32[1]{0:T(128)} %bitcast.place_ref, bf16[64,256]{1,0:T(8,128)(2,1)S(1)} %bitcast.10, bf16[4,144,512]{2,1,0:T(8,128)(2,1)S(1)} %pad_maximum_fusion.table_ref), custom_call_target="tpu_custom_call" | custom-call | tf_op jit(solution)/shard_map/pick_rows/pallas_call | solution.py:201
  70.4 6.5 %all-to-all-start.2 = ((bf16[16,7,512]{2,1,0:T(8,128)(2,1)}), bf16[16,7,512]{2,1,0:T(8,128)(2,1)S(1)}, u32[]{:S(2)}, u32[]{:S(2)}) async-start(bf16[16,7,512]{2,1,0:T(8,128)(2,1)} %pick_rows.1), calls=%async_computation.2 | async-start | bytes 262144 | tf_op jit(solution)/shard_map/all_to_all | solution.py:30
  76.9 0.0 copy-start
  76.9 4.7 %first_waves.1.begun_ref = f32[1408,512]{1,0:T(8,128)S(1)} custom-call(s32[1]{0:T(128)} %bitcast.4.part_ref, bf16[4,112,512]{2,1,0:T(8,128)(2,1)S(1)} %pad_maximum_fusion.1.source_ref, bf16[4096,512]{1,0:T(8,128)(2,1)} %vec_hbm.3), custom_call_target="tpu_custom_call" | custom-call | flops 2952790016 | bytes 6291456 | tf_op jit(solution)/shard_map/first_waves/pallas_call | solution.py:339
  81.6 0.0 collective-permute-done.5.source_ref
  81.6 0.0 copy-done
  81.6 5.3 %pair_waves.1 = (bf16[448,512]{1,0:T(8,128)(2,1)S(1)}, bf16[448,512]{1,0:T(8,128)(2,1)S(1)}, f32[56,512]{1,0:T(8,128)S(1)}, bf16[512,512]{1,0:T(8,128)(2,1)S(1)}) custom-call(s32[1]{0:T(128)} %bitcast.4.part_ref, bf16[4,112,512]{2,1,0:T(8,128)(2,1)S(1)} %collective-permute-done.5.source_ref, bf16[4096,512]{1,0:T(8,128)(2,1)} %vec_hbm.3, ...), custom_call_target="tpu_custom_call" | custom-call | flops 2952790016 | bytes 6291456 | tf_op jit(solution)/shard_map/pair_waves/pallas_call | solution.py:354
  86.9 2.7 %all-to-all-done.2.rows_ref = bf16[16,7,512]{2,1,0:T(8,128)(2,1)S(1)} async-done(((bf16[16,7,512]{2,1,0:T(8,128)(2,1)}), bf16[16,7,512]{2,1,0:T(8,128)(2,1)S(1)}, u32[]{:S(2)}, u32[]{:S(2)}) %all-to-all-start.2) | async-done | bytes 114720 | tf_op jit(solution)/shard_map/all_to_all | solution.py:30
  89.6 0.7 final_terms.1
  90.3 10.3 %all_to_all.20.terms_ref = f32[8,7,512]{2,1,0:T(8,128)S(1)} all-to-all(f32[8,7,512]{2,1,0:T(8,128)S(1)} %final_terms.1), channel_id=1, replica_groups=mesh['ka'=64,'ga'=8] {'ga'}, dimensions={0} | all-to-all | bytes 229376 | tf_op jit(solution)/shard_map/all_to_all | solution.py:30
  100.7 0.6 result.1
  (2 shorter events, 0.1 us)
Async XLA Ops:
  2.1 15.0 %all-to-all-start = ((bf16[8,24,512]{2,1,0:T(8,128)(2,1)}), bf16[8,24,512]{2,1,0:T(8,128)(2,1)S(1)}, u32[]{:S(2)}, u32[]{:S(2)}) async-start(bf16[8,24,512]{2,1,0:T(8,128)(2,1)} %message.1), calls=%async_computation | async-start | bytes 393216 | tf_op jit(solution)/shard_map/all_to_all | solution.py:30
  17.7 0.7 collective-permute-start.2
  18.5 10.7 %collective-permute-start.3 = (bf16[1,112,512]{2,1,0:T(8,128)(2,1)S(1)}, bf16[1,112,512]{2,1,0:T(8,128)(2,1)S(1)}, u32[]{:S(2)}, u32[]{:S(2)}) collective-permute-start(bf16[1,112,512]{2,1,0:T(8,128)(2,1)S(1)} %bitcast.7), channel_id=1, source_target_pairs={{0,4},{1,5},{2,6},{3,7},{4,0},{5,1},{6,2},{7,3},{8,12},{9,13},{10,... | collective-permute-start | bytes 344072 | tf_op jit(solution)/shard_map/ppermute | solution.py:440
  20.4 11.3 %collective-permute-start = (bf16[1,144,512]{2,1,0:T(8,128)(2,1)}, bf16[1,144,512]{2,1,0:T(8,128)(2,1)S(1)}, u32[]{:S(2)}, u32[]{:S(2)}) collective-permute-start(bf16[1,144,512]{2,1,0:T(8,128)(2,1)} %bitcast.12), channel_id=1, source_target_pairs={{0,8},{8,0},{16,24},{24,16},{32,40},{40,32},{48,56},{56,48},{64,72... | collective-permute-start | bytes 442376 | tf_op jit(solution)/shard_map/ppermute | solution.py:434
  29.3 11.2 %collective-permute-start.4 = (bf16[2,112,512]{2,1,0:T(8,128)(2,1)S(1)}, bf16[2,112,512]{2,1,0:T(8,128)(2,1)S(1)}, u32[]{:S(2)}, u32[]{:S(2)}) collective-permute-start(bf16[2,112,512]{2,1,0:T(8,128)(2,1)S(1)} %pad_maximum_fusion.3), channel_id=1, source_target_pairs={{0,2},{1,3},{2,0},{3,1},{4,6},{5,7},{6,4},{7,5},{8,10},{9,11},{10,... | collective-permute-start | bytes 688136 | tf_op jit(solution)/shard_map/ppermute | solution.py:441
  32.7 23.6 %collective-permute-start.1 = (bf16[2,144,512]{2,1,0:T(8,128)(2,1)S(1)}, bf16[2,144,512]{2,1,0:T(8,128)(2,1)S(1)}, u32[]{:S(2)}, u32[]{:S(2)}) collective-permute-start(bf16[2,144,512]{2,1,0:T(8,128)(2,1)S(1)} %pad_maximum_fusion.2), channel_id=1, source_target_pairs={{0,16},{8,24},{16,0},{24,8},{32,48},{40,56},{48,32},{56,40},{64,80... | collective-permute-start | bytes 884744 | tf_op jit(solution)/shard_map/ppermute | solution.py:435
  40.5 41.1 %collective-permute-start.5 = (bf16[4,112,512]{2,1,0:T(8,128)(2,1)S(1)}, bf16[4,112,512]{2,1,0:T(8,128)(2,1)S(1)}, u32[]{:S(2)}, u32[]{:S(2)}) collective-permute-start(bf16[4,112,512]{2,1,0:T(8,128)(2,1)S(1)} %pad_maximum_fusion.1.source_ref), channel_id=1, source_target_pairs={{0,1},{1,0},{2,3},{3,2},{4,5},{5,4},{6,7},{7,6},{8,9},{9,8},{10,11... | collective-permute-start | bytes 1376264 | tf_op jit(solution)/shard_map/ppermute | solution.py:442
  42.4 26.8 %all-to-all-start.1 = ((bf16[8,8,256]{2,1,0:T(8,128)(2,1)}), bf16[8,8,256]{2,1,0:T(8,128)(2,1)S(1)}, u32[]{:S(2)}, u32[]{:S(2)}) async-start(bf16[8,8,256]{2,1,0:T(8,128)(2,1)} %get-tuple-element.11), calls=%async_computation.1 | async-start | bytes 65536 | tf_op jit(solution)/shard_map/all_to_all | solution.py:30
  70.4 19.2 %all-to-all-start.2 = ((bf16[16,7,512]{2,1,0:T(8,128)(2,1)}), bf16[16,7,512]{2,1,0:T(8,128)(2,1)S(1)}, u32[]{:S(2)}, u32[]{:S(2)}) async-start(bf16[16,7,512]{2,1,0:T(8,128)(2,1)} %pick_rows.1), calls=%async_computation.2 | async-start | bytes 262144 | tf_op jit(solution)/shard_map/all_to_all | solution.py:30
  76.9 4.7 %copy-start = (f32[512]{0:T(512)S(1)}, f32[512]{0:T(512)}, u32[]{:S(2)}) copy-start(f32[512]{0:T(512)} %param.8) | copy-start | bytes 6148

commit v6 on v5

--- a/solution.py
+++ b/solution.py
@@ -152,10 +152,12 @@
     return (s & 1) * first + ((s >> 1) & 1) * second
 
 
-def pick_kernel(place_ref, grid_ref, table_ref, out_ref, column_ref, hot_ref):
+def pick_kernel(place_ref, grid_ref, table_ref, other_ref, out_ref, column_ref, hot_ref):
     size = grid_ref.shape[0]
-    pieces, table_rows, _ = table_ref.shape
+    half, table_rows, width = table_ref.shape
+    pieces = 2 * half
     askers = size // pieces
+    held = hot_ref.shape[0] // 2 * LANES
     row = grid_ref[:, :LANES].astype(jnp.float32)
     col = grid_ref[:, LANES:].astype(jnp.float32)
     for i in range(NOFF):
@@ -170,7 +172,8 @@
             base = (jnp.bitwise_xor(place_ref[0], table_mask(s)) * table_rows).astype(jnp.float32)
             local = momentum - base
             inside = jnp.logical_and(local >= 0, local < table_rows)
-            column = jnp.where(inside, local + s * table_rows, column)
+            start = s // half * held + s % half * table_rows
+            column = jnp.where(inside, local + start, column)
         column_ref[i * size : (i + 1) * size, :] = column
     lane = lax.broadcasted_iota(jnp.int32, (askers, LANES), 1).astype(jnp.float32)
     inner = lax.rem(place_ref[0], pieces)
@@ -180,13 +183,15 @@
             hot_ref[part, pl.ds(i, askers, stride=NOFF), :] = jnp.where(
                 column == lane + part * LANES, 1.0, 0.0
             )
-    table = table_ref[...].reshape(pieces * table_rows, -1)
     total = None
     for part in range(hot_ref.shape[0]):
-        count = min(LANES, table.shape[0] - part * LANES)
+        ref = table_ref if part * LANES < held else other_ref
+        table = ref[...].reshape(half * table_rows, width)
+        start = part * LANES % held
+        count = min(LANES, half * table_rows - start)
         term = jnp.dot(
             hot_ref[part, :, :count].astype(jnp.bfloat16),
-            table[part * LANES : part * LANES + count, :],
+            table[start : start + count, :],
             preferred_element_type=jnp.float32,
         )
         total = term if total is None else total + term
@@ -194,24 +199,25 @@
         out_ref[a] = total[a * NOFF : (a + 1) * NOFF].astype(jnp.bfloat16)
 
 
-def pick_rows(place, grid, table):
+def pick_rows(place, grid, table, other):
     size = grid.shape[0]
-    pieces, table_rows, width = table.shape
+    half, table_rows, width = table.shape
+    pieces = 2 * half
     askers = size // pieces
     return pl.pallas_call(
         pick_kernel,
         out_shape=jax.ShapeDtypeStruct((askers, NOFF, width), jnp.bfloat16),
-        in_specs=[SMEM, VMEM, VMEM],
+        in_specs=[SMEM, VMEM, VMEM, VMEM],
         out_specs=VMEM,
         scratch_shapes=[
             pltpu.VMEM((NOFF * size, LANES), jnp.float32),
             pltpu.VMEM(
-                (pl.cdiv(pieces * table_rows, LANES), askers * NOFF, LANES), jnp.float32
+                (2 * pl.cdiv(half * table_rows, LANES), askers * NOFF, LANES), jnp.float32
             ),
         ],
         compiler_params=pltpu.CompilerParams(vmem_limit_bytes=6 << 20),
         name="pick_rows",
-    )(place, grid, table)
+    )(place, grid, table, other)
 
 
 def outer_rows(singles, many):
@@ -224,39 +230,46 @@
     return rows
 
 
-GATHER_STEPS = (4, 2, 1)
 TABLE_STEPS = (1, 2)
 FIRST_LIMIT = 50
 SECOND_LIMIT = 47
-
-
-def gather_mask(s):
-    first, second, third = GATHER_STEPS
-    return (s & 1) * first + ((s >> 1) & 1) * second + ((s >> 2) & 1) * third
-
-
-def pair_products(
-    part_ref, source_ref, vec_hbm, pts_ref, vec_ref, vec_sem, first
-):
-    count, _, chunk = source_ref.shape
+RING = 4
+OWN, FACING, NEXT, LAST = 0, 2, 1, 3
+FIRST_PIECES = (OWN, FACING)
+SECOND_PIECES = (NEXT, LAST)
+
+
+def ring_route(parts, shift):
+    return [
+        (g // RING * RING + (g + shift) % RING, g) for g in range(parts)
+    ]
+
+
+def pair_products(part_ref, source_refs, vec_hbm, pts_ref, vec_ref, vec_sem, pieces):
+    pair, _, chunk = source_refs[0].shape
     step = 3 * PAIRS
 
-    def vec_copy(s):
-        at = jnp.bitwise_xor(part_ref[0], gather_mask(first + s)) * chunk
+    def vec_copy(p, s):
+        place = lax.rem(part_ref[0] + pieces[p], RING)
+        line = jnp.bitwise_xor(part_ref[0] // RING, s)
+        at = (line * RING + place) * chunk
         source = vec_hbm.at[pl.ds(pl.multiple_of(at, chunk), chunk), :]
+        k = p * pair + s
         return pltpu.make_async_copy(
-            source, vec_ref.at[s * chunk : (s + 1) * chunk, :], vec_sem.at[s]
-        )
-
-    for s in range(count):
-        vec_copy(s).start()
-    for s in range(count):
-
-        def put(start, pieces):
-            for h, piece in enumerate(pieces):
-                rows = slice(start + 2 * NV * h, start + 2 * NV * (h + 1))
-                pts_ref[rows, s * chunk : (s + 1) * chunk] = piece
-
+            source, vec_ref.at[k * chunk : (k + 1) * chunk, :], vec_sem.at[k]
+        )
+
+    every = [(p, s) for p in range(len(source_refs)) for s in range(pair)]
+    for p, s in every:
+        vec_copy(p, s).start()
+    for p, s in every:
+        lanes = slice((p * pair + s) * chunk, (p * pair + s + 1) * chunk)
+
+        def put(start, values):
+            for h, value in enumerate(values):
+                pts_ref[start + 2 * NV * h : start + 2 * NV * (h + 1), lanes] = value
+
+        source_ref = source_refs[p]
         own = source_ref[s, RSTEPS * BANDS : (RSTEPS + 1) * BANDS, :].astype(jnp.float32)
         own_v, own_c = own[:NV], own[NV:]
         for n in range(NOFF):
@@ -266,18 +279,23 @@
             put(n * step + PAIRS, outer_rows(there_v, own_v))
             put(n * step + 2 * PAIRS, outer_rows(there_v, there_c))
         put(NOFF * step, outer_rows(own_c, own_v))
-    for s in range(count):
-        vec_copy(s).wait()
+    for p, s in every:
+        vec_copy(p, s).wait()
     return jnp.dot(pts_ref[...], vec_ref[...], preferred_element_type=jnp.float32)
 
 
-def first_waves_kernel(part_ref, source_ref, vec_hbm, acc_ref, pts_ref, vec_ref, vec_sem):
-    acc_ref[...] = pair_products(part_ref, source_ref, vec_hbm, pts_ref, vec_ref, vec_sem, 0)
+def first_waves_kernel(
+    part_ref, one_ref, two_ref, vec_hbm, acc_ref, pts_ref, vec_ref, vec_sem
+):
+    acc_ref[...] = pair_products(
+        part_ref, (one_ref, two_ref), vec_hbm, pts_ref, vec_ref, vec_sem, FIRST_PIECES
+    )
 
 
 def waves_kernel(
     part_ref,
-    source_ref,
+    one_ref,
+    two_ref,
     vec_hbm,
     bare_ref,
     begun_ref,
@@ -292,7 +310,7 @@
 ):
     step = 3 * PAIRS
     acc_ref[...] = begun_ref[...] + pair_products(
-        part_ref, source_ref, vec_hbm, pts_ref, vec_ref, vec_sem, source_ref.shape[0]
+        part_ref, (one_ref, two_ref), vec_hbm, pts_ref, vec_ref, vec_sem, SECOND_PIECES
     )
     own_x = acc_ref[NOFF * step :, :].astype(jnp.bfloat16).astype(jnp.float32)
     weighted = (own_x * bare_ref[...]).astype(jnp.bfloat16)
@@ -318,7 +336,7 @@
 
 
 def waves_scratch(source, ng):
-    count, _, chunk = source.shape
+    count, chunk = 2 * source.shape[0], source.shape[2]
     total = NOFF * 3 * PAIRS + PAIRS
     return [
         pltpu.VMEM((total, count * chunk), jnp.bfloat16),
@@ -329,26 +347,26 @@
 
 def waves_cost(source, ng):
     total = NOFF * 3 * PAIRS + PAIRS
-    flops = 2 * total * source.shape[0] * source.shape[2] * ng
+    flops = 4 * total * source.shape[0] * source.shape[2] * ng
     return pl.CostEstimate(flops=flops, bytes_accessed=6 * 1024 * 1024, transcendentals=0)
 
 
-def first_waves_of(part, source, interp_vectors):
+def first_waves_of(part, source, other, interp_vectors):
     ng = interp_vectors.shape[1]
     total = NOFF * 3 * PAIRS + PAIRS
     return pl.pallas_call(
         first_waves_kernel,
         out_shape=jax.ShapeDtypeStruct((total, ng), jnp.float32),
-        in_specs=[SMEM, VMEM, pl.BlockSpec(memory_space=pl.ANY)],
+        in_specs=[SMEM, VMEM, VMEM, pl.BlockSpec(memory_space=pl.ANY)],
         out_specs=VMEM,
         scratch_shapes=waves_scratch(source, ng),
         compiler_params=pltpu.CompilerParams(vmem_limit_bytes=FIRST_LIMIT << 20),
         cost_estimate=waves_cost(source, ng),
         name="first_waves",
-    )(part, source, interp_vectors)
-
-
-def waves_of(part, source, interp_vectors, bare, begun):
+    )(part, source, other, interp_vectors)
+
+
+def waves_of(part, source, other, interp_vectors, bare, begun):
     ng = interp_vectors.shape[1]
     columns = NC * NV * NC
     return pl.pallas_call(
@@ -359,13 +377,13 @@
             jax.ShapeDtypeStruct((NOFF * NV, columns), jnp.float32),
             jax.ShapeDtypeStruct((columns, columns), jnp.bfloat16),
         ),
-        in_specs=[SMEM, VMEM, pl.BlockSpec(memory_space=pl.ANY), VMEM, VMEM],
+        in_specs=[SMEM, VMEM, VMEM, pl.BlockSpec(memory_space=pl.ANY), VMEM, VMEM],
         out_specs=(VMEM,) * 4,
         scratch_shapes=waves_scratch(source, ng) + [pltpu.VMEM(begun.shape, begun.dtype)],
         compiler_params=pltpu.CompilerParams(vmem_limit_bytes=SECOND_LIMIT << 20),
         cost_estimate=waves_cost(source, ng),
         name="pair_waves",
-    )(part, source, interp_vectors, bare, begun)
+    )(part, source, other, interp_vectors, bare, begun)
 
 
 def final_kernel(rows_ref, cond_ref, vale_ref, exch_ref, perm_ref, out_ref, all_ref, parts_ref):
@@ -427,24 +445,25 @@
     part = lax.axis_index("ga").astype(jnp.int32).reshape(1)
     near = near_groups(size)
     turns = [[(k, k ^ mask) for k in range(size)] for mask in TABLE_STEPS]
-    swaps = [[(g, g ^ mask) for g in range(parts)] for mask in GATHER_STEPS]
+    across = [(g, g ^ RING) for g in range(parts)]
     message = message_of(slab_kpoints, orbitals[0])
     block = swap(message, "ka", near)
     table = screening[None]
     table = jnp.concatenate([table, lax.ppermute(table, "ka", turns[0])])
-    table = jnp.concatenate([table, lax.ppermute(table, "ka", turns[1])])
+    other_table = lax.ppermute(table, "ka", turns[1])
     coords, edge = edges_of(place, block, blocks)
     grid = swap(coords, "ka", far_groups(size, NEAR))
     edge = lax.ppermute(edge, "ka", edge_route(size))
     window = window_of(place, block, edge)[None]
-    two = jnp.concatenate([window, lax.ppermute(window, "ga", swaps[0])])
-    four = jnp.concatenate([two, lax.ppermute(two, "ga", swaps[1])])
-    other = lax.ppermute(four, "ga", swaps[2])
-    picked = pick_rows(place, grid.reshape(size, 2 * LANES), table)
-    rows = swap(picked, "ka", far_groups(size, table.shape[0]))
-    begun = first_waves_of(part, four, interp_vectors)
+    two = jnp.concatenate([window, lax.ppermute(window, "ga", across)])
+    facing = lax.ppermute(two, "ga", ring_route(parts, FACING))
+    following = lax.ppermute(two, "ga", ring_route(parts, NEXT))
+    previous = lax.ppermute(two, "ga", ring_route(parts, LAST))
+    picked = pick_rows(place, grid.reshape(size, 2 * LANES), table, other_table)
+    rows = swap(picked, "ka", far_groups(size, 2 * table.shape[0]))
+    begun = first_waves_of(part, two, facing, interp_vectors)
     cond, vale, exch, perm = waves_of(
-        part, other, interp_vectors, bare_coulomb[None], begun
+        part, following, previous, interp_vectors, bare_coulomb[None], begun
     )
     partial = final_terms(rows, cond, vale, exch, perm)
     terms = swap(partial, "ga")

time: 102 us -> 97.2 us (0.953)
  waiting for transfers between devices: 22.1 us -> 19 us
  blocking collectives: 10.3 us -> 8.98 us
    ppermute x4 -> x5, starting transfers between devices: 12.8 us -> 20.9 us  [the longest x1 10.2 us: per_device(): other_table = lax.ppermute(table, 'ka', turns[1])]
    ppermute x1, starting transfers between devices: 8.78 us -> 2.02 us  [per_device(): table = jnp.concatenate([table, lax.ppermute(table, 'ka', turns[0])])]
    all_to_all x3, waiting for transfers between devices: 20.9 us -> 17.4 us  [swap(): lax.all_to_all(tiles, axis, 0, 0, tiled=True, axis_index_groups=groups)]
    all_to_all x1, blocking collectives: 10.3 us -> 8.98 us  [swap(): lax.all_to_all(tiles, axis, 0, 0, tiled=True, axis_index_groups=groups)]
  transfers between devices with their start and end apart: 9 -> 10, of which waited for: 4 -> 3; matrix products, arithmetic and copies ran while one was open for 2% -> 1% of each run, Pallas kernels for 11% -> 12%
where the time goes in v6:
time: 97.2 us; the launch traced here: 96.5 us
  starting transfers between devices  52 us (53%)
  waiting for transfers between devices  19 us (20%)
  Pallas kernels  14.7 us (15%)
  blocking collectives  8.98 us (9%)
    all_to_all x3, starting transfers between devices, swap(): lax.all_to_all(tiles, axis, 0, 0, tiled=True, axis_index_groups=groups)  28.5 us
    all_to_all x3, waiting for transfers between devices, swap(): lax.all_to_all(tiles, axis, 0, 0, tiled=True, axis_index_groups=groups)  17.4 us
    ppermute x1, starting transfers between devices, per_device(): other_table = lax.ppermute(table, 'ka', turns[1])  10.2 us
    all_to_all x1, blocking collectives, swap(): lax.all_to_all(tiles, axis, 0, 0, tiled=True, axis_index_groups=groups)  8.98 us
    pallas_call x1, Pallas kernels, waves_of(): pl.pallas_call(waves_kernel, out_shape=(jax.ShapeDtypeStruct((NOFF * PAIR...  5.29 us
    pallas_call x1, Pallas kernels, first_waves_of(): pl.pallas_call(first_waves_kernel, out_shape=jax.ShapeDtypeStruct((total,...  4.72 us
    ppermute x1, starting transfers between devices, per_device(): following = lax.ppermute(two, 'ga', ring_route(parts, NEXT))  3.04 us
    ppermute x1, starting transfers between devices, per_device(): facing = lax.ppermute(two, 'ga', ring_route(parts, FACING))  2.96 us
  transfers between devices with their start and end apart: 10, of which 3 were waited for; matrix products, arithmetic and copies ran while one was open for 1% of the time, Pallas kernels for 12%

profile of v6, /device:TPU:32, one launch (start us, length us, event | category | flops | bytes accessed | tf_op | source)
XLA Modules:
  0.0 96.5 jit_solution(3295360592294455074)
XLA Ops:
  0.7 1.4 %message.1 = bf16[8,24,512]{2,1,0:T(8,128)(2,1)} custom-call(s32[1]{0:T(128)S(6)} %copy.6.point_ref, bf16[16,512]{1,0:T(8,128)(2,1)} %bitcast.13), custom_call_target="tpu_custom_call" | custom-call | tf_op jit(solution)/shard_map/message/pallas_call | solution.py:53
  2.1 8.8 %all-to-all-start = ((bf16[8,24,512]{2,1,0:T(8,128)(2,1)}), bf16[8,24,512]{2,1,0:T(8,128)(2,1)S(1)}, u32[]{:S(2)}, u32[]{:S(2)}) async-start(bf16[8,24,512]{2,1,0:T(8,128)(2,1)} %message.1), calls=%async_computation | async-start | bytes 393216 | tf_op jit(solution)/shard_map/all_to_all | solution.py:30
  10.9 2.0 %collective-permute-start = (bf16[1,144,512]{2,1,0:T(8,128)(2,1)}, bf16[1,144,512]{2,1,0:T(8,128)(2,1)S(1)}, u32[]{:S(2)}, u32[]{:S(2)}) collective-permute-start(bf16[1,144,512]{2,1,0:T(8,128)(2,1)} %bitcast.11), channel_id=1, source_target_pairs={{0,8},{8,0},{16,24},{24,16},{32,40},{40,32},{48,56},{56,48},{64,72... | collective-permute-start | bytes 442376 | tf_op jit(solution)/shard_map/ppermute | solution.py:452
  12.9 4.2 %all-to-all-done.block_ref = bf16[8,24,512]{2,1,0:T(8,128)(2,1)S(1)} async-done(((bf16[8,24,512]{2,1,0:T(8,128)(2,1)}), bf16[8,24,512]{2,1,0:T(8,128)(2,1)S(1)}, u32[]{:S(2)}, u32[]{:S(2)}) %all-to-all-start) | async-done | bytes 196640 | tf_op jit(solution)/shard_map/all_to_all | solution.py:30
  17.1 0.6 edges.1
  17.7 0.7 collective-permute-start.2
  18.4 0.0 collective-permute-done.2.edge_ref
  18.4 0.1 window.1
  18.5 1.9 %collective-permute-start.3 = (bf16[1,112,512]{2,1,0:T(8,128)(2,1)S(1)}, bf16[1,112,512]{2,1,0:T(8,128)(2,1)S(1)}, u32[]{:S(2)}, u32[]{:S(2)}) collective-permute-start(bf16[1,112,512]{2,1,0:T(8,128)(2,1)S(1)} %bitcast.7), channel_id=1, source_target_pairs={{0,4},{1,5},{2,6},{3,7},{4,0},{5,1},{6,2},{7,3},{8,12},{9,13},{10,... | collective-permute-start | bytes 344072 | tf_op jit(solution)/shard_map/ppermute | solution.py:458
  20.4 0.0 collective-permute-done
  20.4 0.9 pad_maximum_fusion.table_ref
  21.4 10.2 %collective-permute-start.1 = (bf16[2,144,512]{2,1,0:T(8,128)(2,1)S(1)}, bf16[2,144,512]{2,1,0:T(8,128)(2,1)S(1)}, u32[]{:S(2)}, u32[]{:S(2)}) collective-permute-start(bf16[2,144,512]{2,1,0:T(8,128)(2,1)S(1)} %pad_maximum_fusion.table_ref), channel_id=1, source_target_pairs={{0,16},{8,24},{16,0},{24,8},{32,48},{40,56},{48,32},{56,40},{64,80... | collective-permute-start | bytes 884744 | tf_op jit(solution)/shard_map/ppermute | solution.py:453
  31.5 0.0 collective-permute-done.3
  31.6 3.0 %collective-permute-start.6 = (bf16[2,112,512]{2,1,0:T(8,128)(2,1)S(1)}, bf16[2,112,512]{2,1,0:T(8,128)(2,1)S(1)}, u32[]{:S(2)}, u32[]{:S(2)}) collective-permute-start(bf16[2,112,512]{2,1,0:T(8,128)(2,1)S(1)} %pad_maximum_fusion.1.one_ref), channel_id=1, source_target_pairs={{2,0},{3,1},{0,2},{1,3},{6,4},{7,5},{4,6},{5,7},{10,8},{11,9},{8,1... | collective-permute-start | bytes 688136 | tf_op jit(solution)/shard_map/ppermute | solution.py:459
  34.5 14.9 %all-to-all-start.1 = ((bf16[8,8,256]{2,1,0:T(8,128)(2,1)}), bf16[8,8,256]{2,1,0:T(8,128)(2,1)S(1)}, u32[]{:S(2)}, u32[]{:S(2)}) async-start(bf16[8,8,256]{2,1,0:T(8,128)(2,1)} %get-tuple-element.11), calls=%async_computation.1 | async-start | bytes 65536 | tf_op jit(solution)/shard_map/all_to_all | solution.py:30
  49.4 0.0 collective-permute-done.1.other_ref
  49.5 13.2 %all-to-all-done.1 = bf16[8,8,256]{2,1,0:T(8,128)(2,1)S(1)} async-done(((bf16[8,8,256]{2,1,0:T(8,128)(2,1)}), bf16[8,8,256]{2,1,0:T(8,128)(2,1)S(1)}, u32[]{:S(2)}, u32[]{:S(2)}) %all-to-all-start.1) | async-done | bytes 32800 | tf_op jit(solution)/shard_map/all_to_all | solution.py:30
  62.6 1.3 %pick_rows.1 = bf16[16,7,512]{2,1,0:T(8,128)(2,1)} custom-call(s32[1]{0:T(128)} %bitcast.place_ref, bf16[64,256]{1,0:T(8,128)(2,1)S(1)} %bitcast.9, bf16[2,144,512]{2,1,0:T(8,128)(2,1)S(1)} %pad_maximum_fusion.table_ref, bf16[2,144,512]{2,1,0:T(8,128)(2,1)S(1)} %collective-permute-done.1.other_ref), custom_call_target="tpu_custom_call" | custom-call | tf_op jit(solution)/shard_map/pick_rows/pallas_call | solution.py:207
  63.9 4.8 %all-to-all-start.2 = ((bf16[16,7,512]{2,1,0:T(8,128)(2,1)}), bf16[16,7,512]{2,1,0:T(8,128)(2,1)S(1)}, u32[]{:S(2)}, u32[]{:S(2)}) async-start(bf16[16,7,512]{2,1,0:T(8,128)(2,1)} %pick_rows.1), calls=%async_computation.2 | async-start | bytes 262144 | tf_op jit(solution)/shard_map/all_to_all | solution.py:30
  68.7 3.0 %collective-permute-start.4 = (bf16[2,112,512]{2,1,0:T(8,128)(2,1)S(1)}, bf16[2,112,512]{2,1,0:T(8,128)(2,1)S(1)}, u32[]{:S(2)}, u32[]{:S(2)}) collective-permute-start(bf16[2,112,512]{2,1,0:T(8,128)(2,1)S(1)} %pad_maximum_fusion.1.one_ref), channel_id=1, source_target_pairs={{1,0},{2,1},{3,2},{0,3},{5,4},{6,5},{7,6},{4,7},{9,8},{10,9},{11,1... | collective-permute-start | bytes 688136 | tf_op jit(solution)/shard_map/ppermute | solution.py:460
  71.7 2.8 %collective-permute-start.5 = (bf16[2,112,512]{2,1,0:T(8,128)(2,1)S(1)}, bf16[2,112,512]{2,1,0:T(8,128)(2,1)S(1)}, u32[]{:S(2)}, u32[]{:S(2)}) collective-permute-start(bf16[2,112,512]{2,1,0:T(8,128)(2,1)S(1)} %pad_maximum_fusion.1.one_ref), channel_id=1, source_target_pairs={{3,0},{0,1},{1,2},{2,3},{7,4},{4,5},{5,6},{6,7},{11,8},{8,9},{9,10... | collective-permute-start | bytes 688136 | tf_op jit(solution)/shard_map/ppermute | solution.py:461
  74.5 0.0 collective-permute-done.6.two_ref
  74.5 0.0 copy-start
  74.5 4.7 %first_waves.1.begun_ref = f32[1408,512]{1,0:T(8,128)S(1)} custom-call(s32[1]{0:T(128)} %bitcast.4.part_ref, bf16[2,112,512]{2,1,0:T(8,128)(2,1)S(1)} %pad_maximum_fusion.1.one_ref, bf16[2,112,512]{2,1,0:T(8,128)(2,1)S(1)} %collective-permute-done.6.two_ref, bf16[4096,512]{1,0:T(8,128)(2,1)} %vec_hbm.3), custom_call_target="tpu_custom_call" | custom-call | flops 2952790016 | bytes 6291456 | tf_op jit(solution)/shard_map/first_waves/pallas_call | solution.py:357
  79.3 0.0 collective-permute-done.4.one_ref
  79.3 1.6 %collective-permute-done.5.two_ref = bf16[2,112,512]{2,1,0:T(8,128)(2,1)S(1)} collective-permute-done((bf16[2,112,512]{2,1,0:T(8,128)(2,1)S(1)}, bf16[2,112,512]{2,1,0:T(8,128)(2,1)S(1)}, u32[]{:S(2)}, u32[]{:S(2)}) %collective-permute-start.5) | collective-permute-done | bytes 229408 | tf_op jit(solution)/shard_map/ppermute | solution.py:461
  80.8 0.0 copy-done
  80.8 5.3 %pair_waves.1 = (bf16[448,512]{1,0:T(8,128)(2,1)S(1)}, bf16[448,512]{1,0:T(8,128)(2,1)S(1)}, f32[56,512]{1,0:T(8,128)S(1)}, bf16[512,512]{1,0:T(8,128)(2,1)S(1)}) custom-call(s32[1]{0:T(128)} %bitcast.4.part_ref, bf16[2,112,512]{2,1,0:T(8,128)(2,1)S(1)} %collective-permute-done.4.one_ref, bf16[2,112,512]{2,1,0:T(8,128)(2,1)S(1)} %collective-permute-done.5.two_ref, ...), custom_call_target="tpu_custom_call" | custom-call | flops 2952790016 | bytes 6291456 | tf_op jit(solution)/shard_map/pair_waves/pallas_call | solution.py:372
  86.2 0.0 all-to-all-done.2.rows_ref
  86.2 0.7 final_terms.1
  86.9 9.0 %all_to_all.20.terms_ref = f32[8,7,512]{2,1,0:T(8,128)S(1)} all-to-all(f32[8,7,512]{2,1,0:T(8,128)S(1)} %final_terms.1), channel_id=1, replica_groups=mesh['ka'=64,'ga'=8] {'ga'}, dimensions={0} | all-to-all | bytes 229376 | tf_op jit(solution)/shard_map/all_to_all | solution.py:30
  95.9 0.6 result.1
  (1 shorter events, 0.0 us)
Async XLA Ops:
  2.1 15.0 %all-to-all-start = ((bf16[8,24,512]{2,1,0:T(8,128)(2,1)}), bf16[8,24,512]{2,1,0:T(8,128)(2,1)S(1)}, u32[]{:S(2)}, u32[]{:S(2)}) async-start(bf16[8,24,512]{2,1,0:T(8,128)(2,1)} %message.1), calls=%async_computation | async-start | bytes 393216 | tf_op jit(solution)/shard_map/all_to_all | solution.py:30
  10.9 9.6 %collective-permute-start = (bf16[1,144,512]{2,1,0:T(8,128)(2,1)}, bf16[1,144,512]{2,1,0:T(8,128)(2,1)S(1)}, u32[]{:S(2)}, u32[]{:S(2)}) collective-permute-start(bf16[1,144,512]{2,1,0:T(8,128)(2,1)} %bitcast.11), channel_id=1, source_target_pairs={{0,8},{8,0},{16,24},{24,16},{32,40},{40,32},{48,56},{56,48},{64,72... | collective-permute-start | bytes 442376 | tf_op jit(solution)/shard_map/ppermute | solution.py:452
  17.7 0.7 collective-permute-start.2
  18.5 13.0 %collective-permute-start.3 = (bf16[1,112,512]{2,1,0:T(8,128)(2,1)S(1)}, bf16[1,112,512]{2,1,0:T(8,128)(2,1)S(1)}, u32[]{:S(2)}, u32[]{:S(2)}) collective-permute-start(bf16[1,112,512]{2,1,0:T(8,128)(2,1)S(1)} %bitcast.7), channel_id=1, source_target_pairs={{0,4},{1,5},{2,6},{3,7},{4,0},{5,1},{6,2},{7,3},{8,12},{9,13},{10,... | collective-permute-start | bytes 344072 | tf_op jit(solution)/shard_map/ppermute | solution.py:458
  21.4 28.1 %collective-permute-start.1 = (bf16[2,144,512]{2,1,0:T(8,128)(2,1)S(1)}, bf16[2,144,512]{2,1,0:T(8,128)(2,1)S(1)}, u32[]{:S(2)}, u32[]{:S(2)}) collective-permute-start(bf16[2,144,512]{2,1,0:T(8,128)(2,1)S(1)} %pad_maximum_fusion.table_ref), channel_id=1, source_target_pairs={{0,16},{8,24},{16,0},{24,8},{32,48},{40,56},{48,32},{56,40},{64,80... | collective-permute-start | bytes 884744 | tf_op jit(solution)/shard_map/ppermute | solution.py:453
  31.6 43.0 %collective-permute-start.6 = (bf16[2,112,512]{2,1,0:T(8,128)(2,1)S(1)}, bf16[2,112,512]{2,1,0:T(8,128)(2,1)S(1)}, u32[]{:S(2)}, u32[]{:S(2)}) collective-permute-start(bf16[2,112,512]{2,1,0:T(8,128)(2,1)S(1)} %pad_maximum_fusion.1.one_ref), channel_id=1, source_target_pairs={{2,0},{3,1},{0,2},{1,3},{6,4},{7,5},{4,6},{5,7},{10,8},{11,9},{8,1... | collective-permute-start | bytes 688136 | tf_op jit(solution)/shard_map/ppermute | solution.py:459
  34.5 28.1 %all-to-all-start.1 = ((bf16[8,8,256]{2,1,0:T(8,128)(2,1)}), bf16[8,8,256]{2,1,0:T(8,128)(2,1)S(1)}, u32[]{:S(2)}, u32[]{:S(2)}) async-start(bf16[8,8,256]{2,1,0:T(8,128)(2,1)} %get-tuple-element.11), calls=%async_computation.1 | async-start | bytes 65536 | tf_op jit(solution)/shard_map/all_to_all | solution.py:30
  63.9 22.3 %all-to-all-start.2 = ((bf16[16,7,512]{2,1,0:T(8,128)(2,1)}), bf16[16,7,512]{2,1,0:T(8,128)(2,1)S(1)}, u32[]{:S(2)}, u32[]{:S(2)}) async-start(bf16[16,7,512]{2,1,0:T(8,128)(2,1)} %pick_rows.1), calls=%async_computation.2 | async-start | bytes 262144 | tf_op jit(solution)/shard_map/all_to_all | solution.py:30
  68.7 10.6 %collective-permute-start.4 = (bf16[2,112,512]{2,1,0:T(8,128)(2,1)S(1)}, bf16[2,112,512]{2,1,0:T(8,128)(2,1)S(1)}, u32[]{:S(2)}, u32[]{:S(2)}) collective-permute-start(bf16[2,112,512]{2,1,0:T(8,128)(2,1)S(1)} %pad_maximum_fusion.1.one_ref), channel_id=1, source_target_pairs={{1,0},{2,1},{3,2},{0,3},{5,4},{6,5},{7,6},{4,7},{9,8},{10,9},{11,1... | collective-permute-start | bytes 688136 | tf_op jit(solution)/shard_map/ppermute | solution.py:460
  71.7 9.1 %collective-permute-start.5 = (bf16[2,112,512]{2,1,0:T(8,128)(2,1)S(1)}, bf16[2,112,512]{2,1,0:T(8,128)(2,1)S(1)}, u32[]{:S(2)}, u32[]{:S(2)}) collective-permute-start(bf16[2,112,512]{2,1,0:T(8,128)(2,1)S(1)} %pad_maximum_fusion.1.one_ref), channel_id=1, source_target_pairs={{3,0},{0,1},{1,2},{2,3},{7,4},{4,5},{5,6},{6,7},{11,8},{8,9},{9,10... | collective-permute-start | bytes 688136 | tf_op jit(solution)/shard_map/ppermute | solution.py:461
  74.5 6.3 %copy-start = (f32[512]{0:T(512)S(1)}, f32[512]{0:T(512)}, u32[]{:S(2)}) copy-start(f32[512]{0:T(512)} %param.8) | copy-start | bytes 6148

commit v7 on v6

--- a/solution.py
+++ b/solution.py
@@ -231,8 +231,8 @@
 
 
 TABLE_STEPS = (1, 2)
-FIRST_LIMIT = 50
-SECOND_LIMIT = 47
+FIRST_LIMIT = 48
+SECOND_LIMIT = 20
 RING = 4
 OWN, FACING, NEXT, LAST = 0, 2, 1, 3
 FIRST_PIECES = (OWN, FACING)
@@ -245,23 +245,22 @@
     ]
 
 
-def pair_products(part_ref, source_refs, vec_hbm, pts_ref, vec_ref, vec_sem, pieces):
+def vec_copies(part_ref, vec_hbm, vec_ref, vec_sem, pieces):
+    chunk = vec_ref.shape[1]
+    copies = []
+    for k in range(vec_ref.shape[0]):
+        place = lax.rem(part_ref[0] + pieces[k // 2], RING)
+        line = jnp.bitwise_xor(part_ref[0] // RING, k % 2)
+        at = (line * RING + place) * chunk
+        source = vec_hbm.at[pl.ds(pl.multiple_of(at, chunk), chunk), :]
+        copies.append(pltpu.make_async_copy(source, vec_ref.at[k], vec_sem.at[k]))
+    return copies
+
+
+def pair_products(source_refs, pts_ref, vec_ref, copies=()):
     pair, _, chunk = source_refs[0].shape
     step = 3 * PAIRS
-
-    def vec_copy(p, s):
-        place = lax.rem(part_ref[0] + pieces[p], RING)
-        line = jnp.bitwise_xor(part_ref[0] // RING, s)
-        at = (line * RING + place) * chunk
-        source = vec_hbm.at[pl.ds(pl.multiple_of(at, chunk), chunk), :]
-        k = p * pair + s
-        return pltpu.make_async_copy(
-            source, vec_ref.at[k * chunk : (k + 1) * chunk, :], vec_sem.at[k]
-        )
-
     every = [(p, s) for p in range(len(source_refs)) for s in range(pair)]
-    for p, s in every:
-        vec_copy(p, s).start()
     for p, s in every:
         lanes = slice((p * pair + s) * chunk, (p * pair + s + 1) * chunk)
 
@@ -278,25 +277,28 @@
             put(n * step, outer_rows(own_c, there_c))
             put(n * step + PAIRS, outer_rows(there_v, own_v))
             put(n * step + 2 * PAIRS, outer_rows(there_v, there_c))
-        put(NOFF * step, outer_rows(own_c, own_v))
-    for p, s in every:
-        vec_copy(p, s).wait()
-    return jnp.dot(pts_ref[...], vec_ref[...], preferred_element_type=jnp.float32)
+    for copy in copies:
+        copy.wait()
+    vec = vec_ref[...].reshape(len(every) * chunk, -1)
+    return jnp.dot(pts_ref[...], vec, preferred_element_type=jnp.float32)
 
 
 def first_waves_kernel(
-    part_ref, one_ref, two_ref, vec_hbm, acc_ref, pts_ref, vec_ref, vec_sem
+    part_ref, one_ref, two_ref, vec_hbm, acc_ref, next_ref, pts_ref, vec_ref, vec_sem, next_sem
 ):
-    acc_ref[...] = pair_products(
-        part_ref, (one_ref, two_ref), vec_hbm, pts_ref, vec_ref, vec_sem, FIRST_PIECES
-    )
+    copies = vec_copies(part_ref, vec_hbm, vec_ref, vec_sem, FIRST_PIECES)
+    later = vec_copies(part_ref, vec_hbm, next_ref, next_sem, SECOND_PIECES)
+    for copy in copies + later:
+        copy.start()
+    acc_ref[...] = pair_products((one_ref, two_ref), pts_ref, vec_ref, copies)
+    for copy in later:
+        copy.wait()
 
 
 def waves_kernel(
-    part_ref,
     one_ref,
     two_ref,
-    vec_hbm,
+    vec_ref,
     bare_ref,
     begun_ref,
     cond_ref,
@@ -304,15 +306,18 @@
     exch_ref,
     perm_ref,
     pts_ref,
-    vec_ref,
-    vec_sem,
     acc_ref,
 ):
     step = 3 * PAIRS
-    acc_ref[...] = begun_ref[...] + pair_products(
-        part_ref, (one_ref, two_ref), vec_hbm, pts_ref, vec_ref, vec_sem, SECOND_PIECES
+    acc_ref[...] = begun_ref[...] + pair_products((one_ref, two_ref), pts_ref, vec_ref)
+    own_start = RSTEPS * step + 2 * PAIRS
+    own_x = acc_ref[own_start : own_start + PAIRS, :].astype(jnp.bfloat16)
+    here = lax.broadcasted_iota(jnp.int32, (PAIRS, PAIRS), 0)
+    there = lax.broadcasted_iota(jnp.int32, (PAIRS, PAIRS), 1)
+    turned = (here & 7) * NC + (here >> 3) == there
+    own_x = jnp.dot(
+        jnp.where(turned, 1.0, 0.0).astype(jnp.bfloat16), own_x, preferred_element_type=jnp.float32
     )
-    own_x = acc_ref[NOFF * step :, :].astype(jnp.bfloat16).astype(jnp.float32)
     weighted = (own_x * bare_ref[...]).astype(jnp.bfloat16)
     for i in range(NOFF):
         start = (NOFF - 1 - i) * step
@@ -335,39 +340,43 @@
     perm_ref[...] = jnp.where(moved == target, 1.0, 0.0).astype(jnp.bfloat16)
 
 
-def waves_scratch(source, ng):
-    count, chunk = 2 * source.shape[0], source.shape[2]
-    total = NOFF * 3 * PAIRS + PAIRS
-    return [
-        pltpu.VMEM((total, count * chunk), jnp.bfloat16),
-        pltpu.VMEM((count * chunk, ng), jnp.bfloat16),
-        pltpu.SemaphoreType.DMA((count,)),
-    ]
+def waves_scratch(source):
+    total = NOFF * 3 * PAIRS
+    return [pltpu.VMEM((total, 2 * source.shape[0] * source.shape[2]), jnp.bfloat16)]
 
 
 def waves_cost(source, ng):
-    total = NOFF * 3 * PAIRS + PAIRS
+    total = NOFF * 3 * PAIRS
     flops = 4 * total * source.shape[0] * source.shape[2] * ng
     return pl.CostEstimate(flops=flops, bytes_accessed=6 * 1024 * 1024, transcendentals=0)
 
 
 def first_waves_of(part, source, other, interp_vectors):
     ng = interp_vectors.shape[1]
-    total = NOFF * 3 * PAIRS + PAIRS
+    total = NOFF * 3 * PAIRS
+    count, chunk = 2 * source.shape[0], source.shape[2]
     return pl.pallas_call(
         first_waves_kernel,
-        out_shape=jax.ShapeDtypeStruct((total, ng), jnp.float32),
+        out_shape=(
+            jax.ShapeDtypeStruct((total, ng), jnp.float32),
+            jax.ShapeDtypeStruct((count, chunk, ng), interp_vectors.dtype),
+        ),
         in_specs=[SMEM, VMEM, VMEM, pl.BlockSpec(memory_space=pl.ANY)],
-        out_specs=VMEM,
-        scratch_shapes=waves_scratch(source, ng),
+        out_specs=(VMEM, VMEM),
+        scratch_shapes=waves_scratch(source)
+        + [
+            pltpu.VMEM((count, chunk, ng), interp_vectors.dtype),
+            pltpu.SemaphoreType.DMA((count,)),
+            pltpu.SemaphoreType.DMA((count,)),
+        ],
         compiler_params=pltpu.CompilerParams(vmem_limit_bytes=FIRST_LIMIT << 20),
         cost_estimate=waves_cost(source, ng),
         name="first_waves",
     )(part, source, other, interp_vectors)
 
 
-def waves_of(part, source, other, interp_vectors, bare, begun):
-    ng = interp_vectors.shape[1]
+def waves_of(source, other, vectors, bare, begun):
+    ng = vectors.shape[2]
     columns = NC * NV * NC
     return pl.pallas_call(
         waves_kernel,
@@ -377,13 +386,13 @@
             jax.ShapeDtypeStruct((NOFF * NV, columns), jnp.float32),
             jax.ShapeDtypeStruct((columns, columns), jnp.bfloat16),
         ),
-        in_specs=[SMEM, VMEM, VMEM, pl.BlockSpec(memory_space=pl.ANY), VMEM, VMEM],
+        in_specs=[VMEM] * 5,
         out_specs=(VMEM,) * 4,
-        scratch_shapes=waves_scratch(source, ng) + [pltpu.VMEM(begun.shape, begun.dtype)],
+        scratch_shapes=waves_scratch(source) + [pltpu.VMEM(begun.shape, begun.dtype)],
         compiler_params=pltpu.CompilerParams(vmem_limit_bytes=SECOND_LIMIT << 20),
         cost_estimate=waves_cost(source, ng),
         name="pair_waves",
-    )(part, source, other, interp_vectors, bare, begun)
+    )(source, other, vectors, bare, begun)
 
 
 def final_kernel(rows_ref, cond_ref, vale_ref, exch_ref, perm_ref, out_ref, all_ref, parts_ref):
@@ -461,9 +470,9 @@
     previous = lax.ppermute(two, "ga", ring_route(parts, LAST))
     picked = pick_rows(place, grid.reshape(size, 2 * LANES), table, other_table)
     rows = swap(picked, "ka", far_groups(size, 2 * table.shape[0]))
-    begun = first_waves_of(part, two, facing, interp_vectors)
+    begun, vectors = first_waves_of(part, two, facing, interp_vectors)
     cond, vale, exch, perm = waves_of(
-        part, following, previous, interp_vectors, bare_coulomb[None], begun
+        following, previous, vectors, bare_coulomb[None], begun
     )
     partial = final_terms(rows, cond, vale, exch, perm)
     terms = swap(partial, "ga")

time: 97.2 us -> 95.7 us (0.985)
  the two profiles are of different devices: /device:TPU:32 before, /device:TPU:16 now
where the time goes in v7:
time: 95.7 us; the launch traced here: 95.1 us
  starting transfers between devices  50.9 us (53%)
  waiting for transfers between devices  18.8 us (20%)
  Pallas kernels  13.4 us (14%)
  blocking collectives  10.2 us (11%)
  other arithmetic  0.96 us (1%)
    all_to_all x3, starting transfers between devices, swap(): lax.all_to_all(tiles, axis, 0, 0, tiled=True, axis_index_groups=groups)  23.6 us
    all_to_all x3, waiting for transfers between devices, swap(): lax.all_to_all(tiles, axis, 0, 0, tiled=True, axis_index_groups=groups)  15.7 us
    all_to_all x1, blocking collectives, swap(): lax.all_to_all(tiles, axis, 0, 0, tiled=True, axis_index_groups=groups)  10.2 us
    ppermute x1, starting transfers between devices, per_device(): edge = lax.ppermute(edge, 'ka', edge_route(size))  8.94 us
    pallas_call x1, Pallas kernels, first_waves_of(): pl.pallas_call(first_waves_kernel, out_shape=(jax.ShapeDtypeStruct((total...  5.1 us
    ppermute x1, starting transfers between devices, per_device(): facing = lax.ppermute(two, 'ga', ring_route(parts, FACING))  4.93 us
    pallas_call x1, Pallas kernels, waves_of(): pl.pallas_call(waves_kernel, out_shape=(jax.ShapeDtypeStruct((NOFF * PAIR...  3.65 us
    ppermute x1, starting transfers between devices, per_device(): two = jnp.concatenate([window, lax.ppermute(window, 'ga', across)])  3.19 us
  transfers between devices with their start and end apart: 10, of which 5 were waited for; matrix products, arithmetic and copies ran while one was open for 1% of the time, Pallas kernels for 11%

profile of v7, /device:TPU:16, one launch (start us, length us, event | category | flops | bytes accessed | tf_op | source)
XLA Modules:
  0.0 95.1 jit_solution(15464385760386586910)
XLA Ops:
  0.7 1.4 %message.1 = bf16[8,24,512]{2,1,0:T(8,128)(2,1)} custom-call(s32[1]{0:T(128)S(6)} %copy.6.point_ref, bf16[16,512]{1,0:T(8,128)(2,1)} %bitcast.13), custom_call_target="tpu_custom_call" | custom-call | tf_op jit(solution)/shard_map/message/pallas_call | solution.py:53
  2.1 9.0 %all-to-all-start = ((bf16[8,24,512]{2,1,0:T(8,128)(2,1)}), bf16[8,24,512]{2,1,0:T(8,128)(2,1)S(1)}, u32[]{:S(2)}, u32[]{:S(2)}) async-start(bf16[8,24,512]{2,1,0:T(8,128)(2,1)} %message.1), calls=%async_computation | async-start | bytes 393216 | tf_op jit(solution)/shard_map/all_to_all | solution.py:30
  11.1 2.0 %collective-permute-start = (bf16[1,144,512]{2,1,0:T(8,128)(2,1)}, bf16[1,144,512]{2,1,0:T(8,128)(2,1)S(1)}, u32[]{:S(2)}, u32[]{:S(2)}) collective-permute-start(bf16[1,144,512]{2,1,0:T(8,128)(2,1)} %bitcast.11), channel_id=1, source_target_pairs={{0,8},{8,0},{16,24},{24,16},{32,40},{40,32},{48,56},{56,48},{64,72... | collective-permute-start | bytes 442376 | tf_op jit(solution)/shard_map/ppermute | solution.py:461
  13.1 2.7 %all-to-all-done.block_ref = bf16[8,24,512]{2,1,0:T(8,128)(2,1)S(1)} async-done(((bf16[8,24,512]{2,1,0:T(8,128)(2,1)}), bf16[8,24,512]{2,1,0:T(8,128)(2,1)S(1)}, u32[]{:S(2)}, u32[]{:S(2)}) %all-to-all-start) | async-done | bytes 196640 | tf_op jit(solution)/shard_map/all_to_all | solution.py:30
  15.8 0.6 edges.1
  16.5 8.9 %collective-permute-start.2 = (bf16[48,512]{1,0:T(8,128)(2,1)S(1)}, bf16[48,512]{1,0:T(8,128)(2,1)S(1)}, u32[]{:S(2)}, u32[]{:S(2)}) collective-permute-start(bf16[48,512]{1,0:T(8,128)(2,1)S(1)} %get-tuple-element.14), channel_id=1, source_target_pairs={{0,504},{8,496},{16,488},{40,80},{48,72},{56,64},{64,56},{72,48},{... | collective-permute-start | bytes 147464 | tf_op jit(solution)/shard_map/ppermute | solution.py:465
  25.4 1.8 %collective-permute-done.2.edge_ref = bf16[48,512]{1,0:T(8,128)(2,1)S(1)} collective-permute-done((bf16[48,512]{1,0:T(8,128)(2,1)S(1)}, bf16[48,512]{1,0:T(8,128)(2,1)S(1)}, u32[]{:S(2)}, u32[]{:S(2)}) %collective-permute-start.2) | collective-permute-done | bytes 49184 | tf_op jit(solution)/shard_map/ppermute | solution.py:465
  27.2 3.2 %collective-permute-start.3 = (bf16[1,112,512]{2,1,0:T(8,128)(2,1)S(1)}, bf16[1,112,512]{2,1,0:T(8,128)(2,1)S(1)}, u32[]{:S(2)}, u32[]{:S(2)}) collective-permute-start(bf16[1,112,512]{2,1,0:T(8,128)(2,1)S(1)} %bitcast.7), channel_id=1, source_target_pairs={{0,4},{1,5},{2,6},{3,7},{4,0},{5,1},{6,2},{7,3},{8,12},{9,13},{10,... | collective-permute-start | bytes 344072 | tf_op jit(solution)/shard_map/ppermute | solution.py:467
  30.4 0.0 collective-permute-done
  30.4 0.9 pad_maximum_fusion.table_ref
  31.4 2.3 %collective-permute-start.1 = (bf16[2,144,512]{2,1,0:T(8,128)(2,1)S(1)}, bf16[2,144,512]{2,1,0:T(8,128)(2,1)S(1)}, u32[]{:S(2)}, u32[]{:S(2)}) collective-permute-start(bf16[2,144,512]{2,1,0:T(8,128)(2,1)S(1)} %pad_maximum_fusion.table_ref), channel_id=1, source_target_pairs={{0,16},{8,24},{16,0},{24,8},{32,48},{40,56},{48,32},{56,40},{64,80... | collective-permute-start | bytes 884744 | tf_op jit(solution)/shard_map/ppermute | solution.py:462
  33.7 0.2 collective-permute-done.3
  33.9 4.9 %collective-permute-start.6 = (bf16[2,112,512]{2,1,0:T(8,128)(2,1)S(1)}, bf16[2,112,512]{2,1,0:T(8,128)(2,1)S(1)}, u32[]{:S(2)}, u32[]{:S(2)}) collective-permute-start(bf16[2,112,512]{2,1,0:T(8,128)(2,1)S(1)} %pad_maximum_fusion.1.one_ref), channel_id=1, source_target_pairs={{2,0},{3,1},{0,2},{1,3},{6,4},{7,5},{4,6},{5,7},{10,8},{11,9},{8,1... | collective-permute-start | bytes 688136 | tf_op jit(solution)/shard_map/ppermute | solution.py:468
  38.9 11.1 %all-to-all-start.1 = ((bf16[8,8,256]{2,1,0:T(8,128)(2,1)}), bf16[8,8,256]{2,1,0:T(8,128)(2,1)S(1)}, u32[]{:S(2)}, u32[]{:S(2)}) async-start(bf16[8,8,256]{2,1,0:T(8,128)(2,1)} %get-tuple-element.13), calls=%async_computation.1 | async-start | bytes 65536 | tf_op jit(solution)/shard_map/all_to_all | solution.py:30
  50.0 0.0 collective-permute-done.1.other_ref
  50.0 12.9 %all-to-all-done.1 = bf16[8,8,256]{2,1,0:T(8,128)(2,1)S(1)} async-done(((bf16[8,8,256]{2,1,0:T(8,128)(2,1)}), bf16[8,8,256]{2,1,0:T(8,128)(2,1)S(1)}, u32[]{:S(2)}, u32[]{:S(2)}) %all-to-all-start.1) | async-done | bytes 32800 | tf_op jit(solution)/shard_map/all_to_all | solution.py:30
  62.9 1.3 %pick_rows.1 = bf16[16,7,512]{2,1,0:T(8,128)(2,1)} custom-call(s32[1]{0:T(128)} %bitcast.place_ref, bf16[64,256]{1,0:T(8,128)(2,1)S(1)} %bitcast.9, bf16[2,144,512]{2,1,0:T(8,128)(2,1)S(1)} %pad_maximum_fusion.table_ref, bf16[2,144,512]{2,1,0:T(8,128)(2,1)S(1)} %collective-permute-done.1.other_ref), custom_call_target="tpu_custom_call" | custom-call | tf_op jit(solution)/shard_map/pick_rows/pallas_call | solution.py:207
  64.2 3.5 %all-to-all-start.2 = ((bf16[16,7,512]{2,1,0:T(8,128)(2,1)}), bf16[16,7,512]{2,1,0:T(8,128)(2,1)S(1)}, u32[]{:S(2)}, u32[]{:S(2)}) async-start(bf16[16,7,512]{2,1,0:T(8,128)(2,1)} %pick_rows.1), calls=%async_computation.2 | async-start | bytes 262144 | tf_op jit(solution)/shard_map/all_to_all | solution.py:30
  67.7 3.1 %collective-permute-start.4 = (bf16[2,112,512]{2,1,0:T(8,128)(2,1)S(1)}, bf16[2,112,512]{2,1,0:T(8,128)(2,1)S(1)}, u32[]{:S(2)}, u32[]{:S(2)}) collective-permute-start(bf16[2,112,512]{2,1,0:T(8,128)(2,1)S(1)} %pad_maximum_fusion.1.one_ref), channel_id=1, source_target_pairs={{1,0},{2,1},{3,2},{0,3},{5,4},{6,5},{7,6},{4,7},{9,8},{10,9},{11,1... | collective-permute-start | bytes 688136 | tf_op jit(solution)/shard_map/ppermute | solution.py:469
  70.7 2.8 %collective-permute-start.5 = (bf16[2,112,512]{2,1,0:T(8,128)(2,1)S(1)}, bf16[2,112,512]{2,1,0:T(8,128)(2,1)S(1)}, u32[]{:S(2)}, u32[]{:S(2)}) collective-permute-start(bf16[2,112,512]{2,1,0:T(8,128)(2,1)S(1)} %pad_maximum_fusion.1.one_ref), channel_id=1, source_target_pairs={{3,0},{0,1},{1,2},{2,3},{7,4},{4,5},{5,6},{6,7},{11,8},{8,9},{9,10... | collective-permute-start | bytes 688136 | tf_op jit(solution)/shard_map/ppermute | solution.py:470
  73.5 0.0 collective-permute-done.6.two_ref
  73.5 0.0 copy-start
  73.6 5.1 %first_waves.1 = (f32[1344,512]{1,0:T(8,128)S(1)}, bf16[4,512,512]{2,1,0:T(8,128)(2,1)S(1)}) custom-call(s32[1]{0:T(128)} %bitcast.5.part_ref, bf16[2,112,512]{2,1,0:T(8,128)(2,1)S(1)} %pad_maximum_fusion.1.one_ref, bf16[2,112,512]{2,1,0:T(8,128)(2,1)S(1)} %collective-permute-done.6.two_ref, bf16[4096,512]{1,0:T(8,128)(2,1)} %vec_hbm.1), custom_call_target="tpu_custom_call" | custom-call | flops 2818572288 | bytes 6291456 | tf_op jit(solution)/shard_map/first_waves/pallas_call | solution.py:358
  78.7 0.0 collective-permute-done.4.one_ref
  78.7 1.2 %collective-permute-done.5.two_ref = bf16[2,112,512]{2,1,0:T(8,128)(2,1)S(1)} collective-permute-done((bf16[2,112,512]{2,1,0:T(8,128)(2,1)S(1)}, bf16[2,112,512]{2,1,0:T(8,128)(2,1)S(1)}, u32[]{:S(2)}, u32[]{:S(2)}) %collective-permute-start.5) | collective-permute-done | bytes 229408 | tf_op jit(solution)/shard_map/ppermute | solution.py:470
  79.9 0.0 copy-done
  79.9 3.7 %pair_waves.1 = (bf16[448,512]{1,0:T(8,128)(2,1)S(1)}, bf16[448,512]{1,0:T(8,128)(2,1)S(1)}, f32[56,512]{1,0:T(8,128)S(1)}, bf16[512,512]{1,0:T(8,128)(2,1)S(1)}) custom-call(bf16[2,112,512]{2,1,0:T(8,128)(2,1)S(1)} %collective-permute-done.4.one_ref, bf16[2,112,512]{2,1,0:T(8,128)(2,1)S(1)} %collective-permute-done.5.two_ref, ...), custom_call_target="tpu_custom_call" | custom-call | flops 2818572288 | bytes 6291456 | tf_op jit(solution)/shard_map/pair_waves/pallas_call | solution.py:381
  83.5 0.0 all-to-all-done.2.rows_ref
  83.5 0.7 final_terms.1
  84.3 10.2 %all_to_all.20.terms_ref = f32[8,7,512]{2,1,0:T(8,128)S(1)} all-to-all(f32[8,7,512]{2,1,0:T(8,128)S(1)} %final_terms.1), channel_id=1, replica_groups=mesh['ka'=64,'ga'=8] {'ga'}, dimensions={0} | all-to-all | bytes 229376 | tf_op jit(solution)/shard_map/all_to_all | solution.py:30
  94.5 0.6 result.1
  (2 shorter events, 0.1 us)
Async XLA Ops:
  2.1 13.8 %all-to-all-start = ((bf16[8,24,512]{2,1,0:T(8,128)(2,1)}), bf16[8,24,512]{2,1,0:T(8,128)(2,1)S(1)}, u32[]{:S(2)}, u32[]{:S(2)}) async-start(bf16[8,24,512]{2,1,0:T(8,128)(2,1)} %message.1), calls=%async_computation | async-start | bytes 393216 | tf_op jit(solution)/shard_map/all_to_all | solution.py:30
  11.1 19.3 %collective-permute-start = (bf16[1,144,512]{2,1,0:T(8,128)(2,1)}, bf16[1,144,512]{2,1,0:T(8,128)(2,1)S(1)}, u32[]{:S(2)}, u32[]{:S(2)}) collective-permute-start(bf16[1,144,512]{2,1,0:T(8,128)(2,1)} %bitcast.11), channel_id=1, source_target_pairs={{0,8},{8,0},{16,24},{24,16},{32,40},{40,32},{48,56},{56,48},{64,72... | collective-permute-start | bytes 442376 | tf_op jit(solution)/shard_map/ppermute | solution.py:461
  16.5 10.7 %collective-permute-start.2 = (bf16[48,512]{1,0:T(8,128)(2,1)S(1)}, bf16[48,512]{1,0:T(8,128)(2,1)S(1)}, u32[]{:S(2)}, u32[]{:S(2)}) collective-permute-start(bf16[48,512]{1,0:T(8,128)(2,1)S(1)} %get-tuple-element.14), channel_id=1, source_target_pairs={{0,504},{8,496},{16,488},{40,80},{48,72},{56,64},{64,56},{72,48},{... | collective-permute-start | bytes 147464 | tf_op jit(solution)/shard_map/ppermute | solution.py:465
  27.2 6.7 %collective-permute-start.3 = (bf16[1,112,512]{2,1,0:T(8,128)(2,1)S(1)}, bf16[1,112,512]{2,1,0:T(8,128)(2,1)S(1)}, u32[]{:S(2)}, u32[]{:S(2)}) collective-permute-start(bf16[1,112,512]{2,1,0:T(8,128)(2,1)S(1)} %bitcast.7), channel_id=1, source_target_pairs={{0,4},{1,5},{2,6},{3,7},{4,0},{5,1},{6,2},{7,3},{8,12},{9,13},{10,... | collective-permute-start | bytes 344072 | tf_op jit(solution)/shard_map/ppermute | solution.py:467
  31.4 18.6 %collective-permute-start.1 = (bf16[2,144,512]{2,1,0:T(8,128)(2,1)S(1)}, bf16[2,144,512]{2,1,0:T(8,128)(2,1)S(1)}, u32[]{:S(2)}, u32[]{:S(2)}) collective-permute-start(bf16[2,144,512]{2,1,0:T(8,128)(2,1)S(1)} %pad_maximum_fusion.table_ref), channel_id=1, source_target_pairs={{0,16},{8,24},{16,0},{24,8},{32,48},{40,56},{48,32},{56,40},{64,80... | collective-permute-start | bytes 884744 | tf_op jit(solution)/shard_map/ppermute | solution.py:462
  33.9 39.6 %collective-permute-start.6 = (bf16[2,112,512]{2,1,0:T(8,128)(2,1)S(1)}, bf16[2,112,512]{2,1,0:T(8,128)(2,1)S(1)}, u32[]{:S(2)}, u32[]{:S(2)}) collective-permute-start(bf16[2,112,512]{2,1,0:T(8,128)(2,1)S(1)} %pad_maximum_fusion.1.one_ref), channel_id=1, source_target_pairs={{2,0},{3,1},{0,2},{1,3},{6,4},{7,5},{4,6},{5,7},{10,8},{11,9},{8,1... | collective-permute-start | bytes 688136 | tf_op jit(solution)/shard_map/ppermute | solution.py:468
  38.9 24.0 %all-to-all-start.1 = ((bf16[8,8,256]{2,1,0:T(8,128)(2,1)}), bf16[8,8,256]{2,1,0:T(8,128)(2,1)S(1)}, u32[]{:S(2)}, u32[]{:S(2)}) async-start(bf16[8,8,256]{2,1,0:T(8,128)(2,1)} %get-tuple-element.13), calls=%async_computation.1 | async-start | bytes 65536 | tf_op jit(solution)/shard_map/all_to_all | solution.py:30
  64.2 19.4 %all-to-all-start.2 = ((bf16[16,7,512]{2,1,0:T(8,128)(2,1)}), bf16[16,7,512]{2,1,0:T(8,128)(2,1)S(1)}, u32[]{:S(2)}, u32[]{:S(2)}) async-start(bf16[16,7,512]{2,1,0:T(8,128)(2,1)} %pick_rows.1), calls=%async_computation.2 | async-start | bytes 262144 | tf_op jit(solution)/shard_map/all_to_all | solution.py:30
  67.7 11.0 %collective-permute-start.4 = (bf16[2,112,512]{2,1,0:T(8,128)(2,1)S(1)}, bf16[2,112,512]{2,1,0:T(8,128)(2,1)S(1)}, u32[]{:S(2)}, u32[]{:S(2)}) collective-permute-start(bf16[2,112,512]{2,1,0:T(8,128)(2,1)S(1)} %pad_maximum_fusion.1.one_ref), channel_id=1, source_target_pairs={{1,0},{2,1},{3,2},{0,3},{5,4},{6,5},{7,6},{4,7},{9,8},{10,9},{11,1... | collective-permute-start | bytes 688136 | tf_op jit(solution)/shard_map/ppermute | solution.py:469
  70.7 9.1 %collective-permute-start.5 = (bf16[2,112,512]{2,1,0:T(8,128)(2,1)S(1)}, bf16[2,112,512]{2,1,0:T(8,128)(2,1)S(1)}, u32[]{:S(2)}, u32[]{:S(2)}) collective-permute-start(bf16[2,112,512]{2,1,0:T(8,128)(2,1)S(1)} %pad_maximum_fusion.1.one_ref), channel_id=1, source_target_pairs={{3,0},{0,1},{1,2},{2,3},{7,4},{4,5},{5,6},{6,7},{11,8},{8,9},{9,10... | collective-permute-start | bytes 688136 | tf_op jit(solution)/shard_map/ppermute | solution.py:470
  73.5 6.3 %copy-start = (f32[512]{0:T(512)S(1)}, f32[512]{0:T(512)}, u32[]{:S(2)}) copy-start(f32[512]{0:T(512)} %param.8) | copy-start | bytes 6148

commit v8 on v7

--- a/solution.py
+++ b/solution.py
@@ -231,7 +231,7 @@
 
 
 TABLE_STEPS = (1, 2)
-FIRST_LIMIT = 48
+FIRST_LIMIT = 46
 SECOND_LIMIT = 20
 RING = 4
 OWN, FACING, NEXT, LAST = 0, 2, 1, 3
@@ -257,7 +257,7 @@
     return copies
 
 
-def pair_products(source_refs, pts_ref, vec_ref, copies=()):
+def pair_products(source_refs, pts_ref, vec_ref, copies=(), later=()):
     pair, _, chunk = source_refs[0].shape
     step = 3 * PAIRS
     every = [(p, s) for p in range(len(source_refs)) for s in range(pair)]
@@ -279,18 +279,25 @@
             put(n * step + 2 * PAIRS, outer_rows(there_v, there_c))
     for copy in copies:
         copy.wait()
+    for copy in later:
+        copy.start()
     vec = vec_ref[...].reshape(len(every) * chunk, -1)
     return jnp.dot(pts_ref[...], vec, preferred_element_type=jnp.float32)
 
 
 def first_waves_kernel(
-    part_ref, one_ref, two_ref, vec_hbm, acc_ref, next_ref, pts_ref, vec_ref, vec_sem, next_sem
+    part_ref, one_ref, two_ref, vec_hbm, acc_ref, next_ref, perm_ref, pts_ref, vec_ref,
+    vec_sem, next_sem
 ):
     copies = vec_copies(part_ref, vec_hbm, vec_ref, vec_sem, FIRST_PIECES)
     later = vec_copies(part_ref, vec_hbm, next_ref, next_sem, SECOND_PIECES)
-    for copy in copies + later:
+    for copy in copies:
         copy.start()
-    acc_ref[...] = pair_products((one_ref, two_ref), pts_ref, vec_ref, copies)
+    acc_ref[...] = pair_products((one_ref, two_ref), pts_ref, vec_ref, copies, later)
+    source = lax.broadcasted_iota(jnp.int32, perm_ref.shape, 0)
+    target = lax.broadcasted_iota(jnp.int32, perm_ref.shape, 1)
+    moved = ((source >> 3) & 7) * (NV * NC) + (source >> 6) * NC + (source & 7)
+    perm_ref[...] = jnp.where(moved == target, 1.0, 0.0).astype(jnp.bfloat16)
     for copy in later:
         copy.wait()
 
@@ -304,7 +311,6 @@
     cond_ref,
     vale_ref,
     exch_ref,
-    perm_ref,
     pts_ref,
     acc_ref,
 ):
@@ -334,10 +340,6 @@
         exch_ref[i * NV : (i + 1) * NV, :] = jnp.concatenate(
             [term[c * NV : (c + 1) * NV] for c in range(NC)], axis=1
         )
-    source = lax.broadcasted_iota(jnp.int32, perm_ref.shape, 0)
-    target = lax.broadcasted_iota(jnp.int32, perm_ref.shape, 1)
-    moved = ((source >> 3) & 7) * (NV * NC) + (source >> 6) * NC + (source & 7)
-    perm_ref[...] = jnp.where(moved == target, 1.0, 0.0).astype(jnp.bfloat16)
 
 
 def waves_scratch(source):
@@ -355,14 +357,16 @@
     ng = interp_vectors.shape[1]
     total = NOFF * 3 * PAIRS
     count, chunk = 2 * source.shape[0], source.shape[2]
+    columns = NC * NV * NC
     return pl.pallas_call(
         first_waves_kernel,
         out_shape=(
             jax.ShapeDtypeStruct((total, ng), jnp.float32),
             jax.ShapeDtypeStruct((count, chunk, ng), interp_vectors.dtype),
+            jax.ShapeDtypeStruct((columns, columns), jnp.bfloat16),
         ),
         in_specs=[SMEM, VMEM, VMEM, pl.BlockSpec(memory_space=pl.ANY)],
-        out_specs=(VMEM, VMEM),
+        out_specs=(VMEM,) * 3,
         scratch_shapes=waves_scratch(source)
         + [
             pltpu.VMEM((count, chunk, ng), interp_vectors.dtype),
@@ -384,10 +388,9 @@
             jax.ShapeDtypeStruct((NOFF * PAIRS, ng), jnp.bfloat16),
             jax.ShapeDtypeStruct((NOFF * PAIRS, ng), jnp.bfloat16),
             jax.ShapeDtypeStruct((NOFF * NV, columns), jnp.float32),
-            jax.ShapeDtypeStruct((columns, columns), jnp.bfloat16),
         ),
         in_specs=[VMEM] * 5,
-        out_specs=(VMEM,) * 4,
+        out_specs=(VMEM,) * 3,
         scratch_shapes=waves_scratch(source) + [pltpu.VMEM(begun.shape, begun.dtype)],
         compiler_params=pltpu.CompilerParams(vmem_limit_bytes=SECOND_LIMIT << 20),
         cost_estimate=waves_cost(source, ng),
@@ -470,8 +473,8 @@
     previous = lax.ppermute(two, "ga", ring_route(parts, LAST))
     picked = pick_rows(place, grid.reshape(size, 2 * LANES), table, other_table)
     rows = swap(picked, "ka", far_groups(size, 2 * table.shape[0]))
-    begun, vectors = first_waves_of(part, two, facing, interp_vectors)
-    cond, vale, exch, perm = waves_of(
+    begun, vectors, perm = first_waves_of(part, two, facing, interp_vectors)
+    cond, vale, exch = waves_of(
         following, previous, vectors, bare_coulomb[None], begun
     )
     partial = final_terms(rows, cond, vale, exch, perm)

time: 95.7 us -> 95.2 us (level)
  no operation moved by 1% of the time
where the time goes in v8:
time: 95.2 us; the launch traced here: 94.6 us
  starting transfers between devices  50.9 us (53%)
  waiting for transfers between devices  19 us (20%)
  Pallas kernels  12.9 us (14%)
  blocking collectives  10 us (11%)
  other arithmetic  0.96 us (1%)
    all_to_all x3, starting transfers between devices, swap(): lax.all_to_all(tiles, axis, 0, 0, tiled=True, axis_index_groups=groups)  23.6 us
    all_to_all x3, waiting for transfers between devices, swap(): lax.all_to_all(tiles, axis, 0, 0, tiled=True, axis_index_groups=groups)  15.7 us
    all_to_all x1, blocking collectives, swap(): lax.all_to_all(tiles, axis, 0, 0, tiled=True, axis_index_groups=groups)  10 us
    ppermute x1, starting transfers between devices, per_device(): edge = lax.ppermute(edge, 'ka', edge_route(size))  8.94 us
    ppermute x1, starting transfers between devices, per_device(): facing = lax.ppermute(two, 'ga', ring_route(parts, FACING))  4.93 us
    pallas_call x1, Pallas kernels, first_waves_of(): pl.pallas_call(first_waves_kernel, out_shape=(jax.ShapeDtypeStruct((total...  4.89 us
    pallas_call x1, Pallas kernels, waves_of(): pl.pallas_call(waves_kernel, out_shape=(jax.ShapeDtypeStruct((NOFF * PAIR...  3.36 us
    ppermute x1, starting transfers between devices, per_device(): two = jnp.concatenate([window, lax.ppermute(window, 'ga', across)])  3.19 us
  transfers between devices with their start and end apart: 10, of which 5 were waited for; matrix products, arithmetic and copies ran while one was open for 1% of the time, Pallas kernels for 11%

profile of v8, /device:TPU:16, one launch (start us, length us, event | category | flops | bytes accessed | tf_op | source)
XLA Modules:
  0.0 94.6 jit_solution(3940200529951540969)
XLA Ops:
  0.7 1.4 %message.1 = bf16[8,24,512]{2,1,0:T(8,128)(2,1)} custom-call(s32[1]{0:T(128)S(6)} %copy.6.point_ref, bf16[16,512]{1,0:T(8,128)(2,1)} %bitcast.13), custom_call_target="tpu_custom_call" | custom-call | tf_op jit(solution)/shard_map/message/pallas_call | solution.py:53
  2.1 9.0 %all-to-all-start = ((bf16[8,24,512]{2,1,0:T(8,128)(2,1)}), bf16[8,24,512]{2,1,0:T(8,128)(2,1)S(1)}, u32[]{:S(2)}, u32[]{:S(2)}) async-start(bf16[8,24,512]{2,1,0:T(8,128)(2,1)} %message.1), calls=%async_computation | async-start | bytes 393216 | tf_op jit(solution)/shard_map/all_to_all | solution.py:30
  11.1 2.0 %collective-permute-start = (bf16[1,144,512]{2,1,0:T(8,128)(2,1)}, bf16[1,144,512]{2,1,0:T(8,128)(2,1)S(1)}, u32[]{:S(2)}, u32[]{:S(2)}) collective-permute-start(bf16[1,144,512]{2,1,0:T(8,128)(2,1)} %bitcast.11), channel_id=1, source_target_pairs={{0,8},{8,0},{16,24},{24,16},{32,40},{40,32},{48,56},{56,48},{64,72... | collective-permute-start | bytes 442376 | tf_op jit(solution)/shard_map/ppermute | solution.py:464
  13.1 2.7 %all-to-all-done.block_ref = bf16[8,24,512]{2,1,0:T(8,128)(2,1)S(1)} async-done(((bf16[8,24,512]{2,1,0:T(8,128)(2,1)}), bf16[8,24,512]{2,1,0:T(8,128)(2,1)S(1)}, u32[]{:S(2)}, u32[]{:S(2)}) %all-to-all-start) | async-done | bytes 196640 | tf_op jit(solution)/shard_map/all_to_all | solution.py:30
  15.8 0.6 edges.1
  16.5 8.9 %collective-permute-start.2 = (bf16[48,512]{1,0:T(8,128)(2,1)S(1)}, bf16[48,512]{1,0:T(8,128)(2,1)S(1)}, u32[]{:S(2)}, u32[]{:S(2)}) collective-permute-start(bf16[48,512]{1,0:T(8,128)(2,1)S(1)} %get-tuple-element.14), channel_id=1, source_target_pairs={{0,504},{8,496},{16,488},{40,80},{48,72},{56,64},{64,56},{72,48},{... | collective-permute-start | bytes 147464 | tf_op jit(solution)/shard_map/ppermute | solution.py:468
  25.4 1.8 %collective-permute-done.2.edge_ref = bf16[48,512]{1,0:T(8,128)(2,1)S(1)} collective-permute-done((bf16[48,512]{1,0:T(8,128)(2,1)S(1)}, bf16[48,512]{1,0:T(8,128)(2,1)S(1)}, u32[]{:S(2)}, u32[]{:S(2)}) %collective-permute-start.2) | collective-permute-done | bytes 49184 | tf_op jit(solution)/shard_map/ppermute | solution.py:468
  27.2 3.2 %collective-permute-start.3 = (bf16[1,112,512]{2,1,0:T(8,128)(2,1)S(1)}, bf16[1,112,512]{2,1,0:T(8,128)(2,1)S(1)}, u32[]{:S(2)}, u32[]{:S(2)}) collective-permute-start(bf16[1,112,512]{2,1,0:T(8,128)(2,1)S(1)} %bitcast.7), channel_id=1, source_target_pairs={{0,4},{1,5},{2,6},{3,7},{4,0},{5,1},{6,2},{7,3},{8,12},{9,13},{10,... | collective-permute-start | bytes 344072 | tf_op jit(solution)/shard_map/ppermute | solution.py:470
  30.4 0.0 collective-permute-done
  30.4 0.9 pad_maximum_fusion.table_ref
  31.4 2.3 %collective-permute-start.1 = (bf16[2,144,512]{2,1,0:T(8,128)(2,1)S(1)}, bf16[2,144,512]{2,1,0:T(8,128)(2,1)S(1)}, u32[]{:S(2)}, u32[]{:S(2)}) collective-permute-start(bf16[2,144,512]{2,1,0:T(8,128)(2,1)S(1)} %pad_maximum_fusion.table_ref), channel_id=1, source_target_pairs={{0,16},{8,24},{16,0},{24,8},{32,48},{40,56},{48,32},{56,40},{64,80... | collective-permute-start | bytes 884744 | tf_op jit(solution)/shard_map/ppermute | solution.py:465
  33.7 0.2 collective-permute-done.3
  33.9 4.9 %collective-permute-start.6 = (bf16[2,112,512]{2,1,0:T(8,128)(2,1)S(1)}, bf16[2,112,512]{2,1,0:T(8,128)(2,1)S(1)}, u32[]{:S(2)}, u32[]{:S(2)}) collective-permute-start(bf16[2,112,512]{2,1,0:T(8,128)(2,1)S(1)} %pad_maximum_fusion.1.one_ref), channel_id=1, source_target_pairs={{2,0},{3,1},{0,2},{1,3},{6,4},{7,5},{4,6},{5,7},{10,8},{11,9},{8,1... | collective-permute-start | bytes 688136 | tf_op jit(solution)/shard_map/ppermute | solution.py:471
  38.9 11.1 %all-to-all-start.1 = ((bf16[8,8,256]{2,1,0:T(8,128)(2,1)}), bf16[8,8,256]{2,1,0:T(8,128)(2,1)S(1)}, u32[]{:S(2)}, u32[]{:S(2)}) async-start(bf16[8,8,256]{2,1,0:T(8,128)(2,1)} %get-tuple-element.13), calls=%async_computation.1 | async-start | bytes 65536 | tf_op jit(solution)/shard_map/all_to_all | solution.py:30
  50.0 0.0 collective-permute-done.1.other_ref
  50.0 12.9 %all-to-all-done.1 = bf16[8,8,256]{2,1,0:T(8,128)(2,1)S(1)} async-done(((bf16[8,8,256]{2,1,0:T(8,128)(2,1)}), bf16[8,8,256]{2,1,0:T(8,128)(2,1)S(1)}, u32[]{:S(2)}, u32[]{:S(2)}) %all-to-all-start.1) | async-done | bytes 32800 | tf_op jit(solution)/shard_map/all_to_all | solution.py:30
  62.9 1.3 %pick_rows.1 = bf16[16,7,512]{2,1,0:T(8,128)(2,1)} custom-call(s32[1]{0:T(128)} %bitcast.place_ref, bf16[64,256]{1,0:T(8,128)(2,1)S(1)} %bitcast.9, bf16[2,144,512]{2,1,0:T(8,128)(2,1)S(1)} %pad_maximum_fusion.table_ref, bf16[2,144,512]{2,1,0:T(8,128)(2,1)S(1)} %collective-permute-done.1.other_ref), custom_call_target="tpu_custom_call" | custom-call | tf_op jit(solution)/shard_map/pick_rows/pallas_call | solution.py:207
  64.2 3.5 %all-to-all-start.2 = ((bf16[16,7,512]{2,1,0:T(8,128)(2,1)}), bf16[16,7,512]{2,1,0:T(8,128)(2,1)S(1)}, u32[]{:S(2)}, u32[]{:S(2)}) async-start(bf16[16,7,512]{2,1,0:T(8,128)(2,1)} %pick_rows.1), calls=%async_computation.2 | async-start | bytes 262144 | tf_op jit(solution)/shard_map/all_to_all | solution.py:30
  67.7 3.1 %collective-permute-start.4 = (bf16[2,112,512]{2,1,0:T(8,128)(2,1)S(1)}, bf16[2,112,512]{2,1,0:T(8,128)(2,1)S(1)}, u32[]{:S(2)}, u32[]{:S(2)}) collective-permute-start(bf16[2,112,512]{2,1,0:T(8,128)(2,1)S(1)} %pad_maximum_fusion.1.one_ref), channel_id=1, source_target_pairs={{1,0},{2,1},{3,2},{0,3},{5,4},{6,5},{7,6},{4,7},{9,8},{10,9},{11,1... | collective-permute-start | bytes 688136 | tf_op jit(solution)/shard_map/ppermute | solution.py:472
  70.7 2.8 %collective-permute-start.5 = (bf16[2,112,512]{2,1,0:T(8,128)(2,1)S(1)}, bf16[2,112,512]{2,1,0:T(8,128)(2,1)S(1)}, u32[]{:S(2)}, u32[]{:S(2)}) collective-permute-start(bf16[2,112,512]{2,1,0:T(8,128)(2,1)S(1)} %pad_maximum_fusion.1.one_ref), channel_id=1, source_target_pairs={{3,0},{0,1},{1,2},{2,3},{7,4},{4,5},{5,6},{6,7},{11,8},{8,9},{9,10... | collective-permute-start | bytes 688136 | tf_op jit(solution)/shard_map/ppermute | solution.py:473
  73.5 0.0 collective-permute-done.6.two_ref
  73.5 0.0 copy-start
  73.6 4.9 %first_waves.1 = (f32[1344,512]{1,0:T(8,128)S(1)}, bf16[4,512,512]{2,1,0:T(8,128)(2,1)S(1)}, bf16[512,512]{1,0:T(8,128)(2,1)S(1)}) custom-call(s32[1]{0:T(128)} %bitcast.5.part_ref, bf16[2,112,512]{2,1,0:T(8,128)(2,1)S(1)} %pad_maximum_fusion.1.one_ref, bf16[2,112,512]{2,1,0:T(8,128)(2,1)S(1)} %collective-permute-done.6.two_ref, bf16[4096,512]{1,0:T(8,128)(2,1)} %vec_hbm.1), custom_call_target="tpu_custom_call" | custom-call | flops 2818572288 | bytes 6291456 | tf_op jit(solution)/shard_map/first_waves/pallas_call | solution.py:361
  78.5 0.0 collective-permute-done.4.one_ref
  78.5 1.4 %collective-permute-done.5.two_ref = bf16[2,112,512]{2,1,0:T(8,128)(2,1)S(1)} collective-permute-done((bf16[2,112,512]{2,1,0:T(8,128)(2,1)S(1)}, bf16[2,112,512]{2,1,0:T(8,128)(2,1)S(1)}, u32[]{:S(2)}, u32[]{:S(2)}) %collective-permute-start.5) | collective-permute-done | bytes 229408 | tf_op jit(solution)/shard_map/ppermute | solution.py:473
  79.9 0.0 copy-done
  79.9 3.4 %pair_waves.1 = (bf16[448,512]{1,0:T(8,128)(2,1)S(1)}, bf16[448,512]{1,0:T(8,128)(2,1)S(1)}, f32[56,512]{1,0:T(8,128)S(1)}) custom-call(bf16[2,112,512]{2,1,0:T(8,128)(2,1)S(1)} %collective-permute-done.4.one_ref, bf16[2,112,512]{2,1,0:T(8,128)(2,1)S(1)} %collective-permute-done.5.two_ref, bf16[4,512,512]{2,1,0:T(8,128)(2,1)S(1)} %get-tuple-element.15.vec_ref, ...), custom_call_target="tpu_custom_call" | custom-call | flops 2818572288 | bytes 6291456 | tf_op jit(solution)/shard_map/pair_waves/pallas_call | solution.py:385
  83.2 0.0 all-to-all-done.2.rows_ref
  83.2 0.7 final_terms.1
  84.0 10.0 %all_to_all.20.terms_ref = f32[8,7,512]{2,1,0:T(8,128)S(1)} all-to-all(f32[8,7,512]{2,1,0:T(8,128)S(1)} %final_terms.1), channel_id=1, replica_groups=mesh['ka'=64,'ga'=8] {'ga'}, dimensions={0} | all-to-all | bytes 229376 | tf_op jit(solution)/shard_map/all_to_all | solution.py:30
  94.0 0.6 result.1
  (2 shorter events, 0.1 us)
Async XLA Ops:
  2.1 13.8 %all-to-all-start = ((bf16[8,24,512]{2,1,0:T(8,128)(2,1)}), bf16[8,24,512]{2,1,0:T(8,128)(2,1)S(1)}, u32[]{:S(2)}, u32[]{:S(2)}) async-start(bf16[8,24,512]{2,1,0:T(8,128)(2,1)} %message.1), calls=%async_computation | async-start | bytes 393216 | tf_op jit(solution)/shard_map/all_to_all | solution.py:30
  11.1 19.3 %collective-permute-start = (bf16[1,144,512]{2,1,0:T(8,128)(2,1)}, bf16[1,144,512]{2,1,0:T(8,128)(2,1)S(1)}, u32[]{:S(2)}, u32[]{:S(2)}) collective-permute-start(bf16[1,144,512]{2,1,0:T(8,128)(2,1)} %bitcast.11), channel_id=1, source_target_pairs={{0,8},{8,0},{16,24},{24,16},{32,40},{40,32},{48,56},{56,48},{64,72... | collective-permute-start | bytes 442376 | tf_op jit(solution)/shard_map/ppermute | solution.py:464
  16.5 10.7 %collective-permute-start.2 = (bf16[48,512]{1,0:T(8,128)(2,1)S(1)}, bf16[48,512]{1,0:T(8,128)(2,1)S(1)}, u32[]{:S(2)}, u32[]{:S(2)}) collective-permute-start(bf16[48,512]{1,0:T(8,128)(2,1)S(1)} %get-tuple-element.14), channel_id=1, source_target_pairs={{0,504},{8,496},{16,488},{40,80},{48,72},{56,64},{64,56},{72,48},{... | collective-permute-start | bytes 147464 | tf_op jit(solution)/shard_map/ppermute | solution.py:468
  27.2 6.7 %collective-permute-start.3 = (bf16[1,112,512]{2,1,0:T(8,128)(2,1)S(1)}, bf16[1,112,512]{2,1,0:T(8,128)(2,1)S(1)}, u32[]{:S(2)}, u32[]{:S(2)}) collective-permute-start(bf16[1,112,512]{2,1,0:T(8,128)(2,1)S(1)} %bitcast.7), channel_id=1, source_target_pairs={{0,4},{1,5},{2,6},{3,7},{4,0},{5,1},{6,2},{7,3},{8,12},{9,13},{10,... | collective-permute-start | bytes 344072 | tf_op jit(solution)/shard_map/ppermute | solution.py:470
  31.4 18.6 %collective-permute-start.1 = (bf16[2,144,512]{2,1,0:T(8,128)(2,1)S(1)}, bf16[2,144,512]{2,1,0:T(8,128)(2,1)S(1)}, u32[]{:S(2)}, u32[]{:S(2)}) collective-permute-start(bf16[2,144,512]{2,1,0:T(8,128)(2,1)S(1)} %pad_maximum_fusion.table_ref), channel_id=1, source_target_pairs={{0,16},{8,24},{16,0},{24,8},{32,48},{40,56},{48,32},{56,40},{64,80... | collective-permute-start | bytes 884744 | tf_op jit(solution)/shard_map/ppermute | solution.py:465
  33.9 39.6 %collective-permute-start.6 = (bf16[2,112,512]{2,1,0:T(8,128)(2,1)S(1)}, bf16[2,112,512]{2,1,0:T(8,128)(2,1)S(1)}, u32[]{:S(2)}, u32[]{:S(2)}) collective-permute-start(bf16[2,112,512]{2,1,0:T(8,128)(2,1)S(1)} %pad_maximum_fusion.1.one_ref), channel_id=1, source_target_pairs={{2,0},{3,1},{0,2},{1,3},{6,4},{7,5},{4,6},{5,7},{10,8},{11,9},{8,1... | collective-permute-start | bytes 688136 | tf_op jit(solution)/shard_map/ppermute | solution.py:471
  38.9 24.0 %all-to-all-start.1 = ((bf16[8,8,256]{2,1,0:T(8,128)(2,1)}), bf16[8,8,256]{2,1,0:T(8,128)(2,1)S(1)}, u32[]{:S(2)}, u32[]{:S(2)}) async-start(bf16[8,8,256]{2,1,0:T(8,128)(2,1)} %get-tuple-element.13), calls=%async_computation.1 | async-start | bytes 65536 | tf_op jit(solution)/shard_map/all_to_all | solution.py:30
  64.2 19.1 %all-to-all-start.2 = ((bf16[16,7,512]{2,1,0:T(8,128)(2,1)}), bf16[16,7,512]{2,1,0:T(8,128)(2,1)S(1)}, u32[]{:S(2)}, u32[]{:S(2)}) async-start(bf16[16,7,512]{2,1,0:T(8,128)(2,1)} %pick_rows.1), calls=%async_computation.2 | async-start | bytes 262144 | tf_op jit(solution)/shard_map/all_to_all | solution.py:30
  67.7 10.8 %collective-permute-start.4 = (bf16[2,112,512]{2,1,0:T(8,128)(2,1)S(1)}, bf16[2,112,512]{2,1,0:T(8,128)(2,1)S(1)}, u32[]{:S(2)}, u32[]{:S(2)}) collective-permute-start(bf16[2,112,512]{2,1,0:T(8,128)(2,1)S(1)} %pad_maximum_fusion.1.one_ref), channel_id=1, source_target_pairs={{1,0},{2,1},{3,2},{0,3},{5,4},{6,5},{7,6},{4,7},{9,8},{10,9},{11,1... | collective-permute-start | bytes 688136 | tf_op jit(solution)/shard_map/ppermute | solution.py:472
  70.7 9.1 %collective-permute-start.5 = (bf16[2,112,512]{2,1,0:T(8,128)(2,1)S(1)}, bf16[2,112,512]{2,1,0:T(8,128)(2,1)S(1)}, u32[]{:S(2)}, u32[]{:S(2)}) collective-permute-start(bf16[2,112,512]{2,1,0:T(8,128)(2,1)S(1)} %pad_maximum_fusion.1.one_ref), channel_id=1, source_target_pairs={{3,0},{0,1},{1,2},{2,3},{7,4},{4,5},{5,6},{6,7},{11,8},{8,9},{9,10... | collective-permute-start | bytes 688136 | tf_op jit(solution)/shard_map/ppermute | solution.py:473
  73.5 6.3 %copy-start = (f32[512]{0:T(512)S(1)}, f32[512]{0:T(512)}, u32[]{:S(2)}) copy-start(f32[512]{0:T(512)} %param.8) | copy-start | bytes 6148
